TPU v7x, 256 devices: a whole 4x4x8 slice. The times are simulated.
256 devices in a mesh: gx: 4 (over x), gy: 8 (over z), gz: 8 (over y, core).
Axes of the slice: x: 4, y: 4, z: 8, core: 2. Of those that a mesh axis runs over, the one named last changes fastest.
Arguments:
- patch_fields: bfloat16 [8192, 4, 32768], P(('gx', 'gy', 'gz')), may hold values from -54 to 54
- slot_snapshot: int32 [8192], P(('gx', 'gy', 'gz')), may hold values from -1 to 15, as said below
- slot_brick: int32 [8192], P(('gx', 'gy', 'gz')), may hold values from -1 to 255, as said below
- prior_basis: float32 [64, 32], replicated, may hold values from -0.75 to 0.75
Outputs:
- gram_matrix: float32 [64, 64], replicated
- mode_fields: bfloat16 [64, 128, 4096], P('gx', 'gy', 'gz')
- diffused: bfloat16 [64, 128, 4096], P('gx', 'gy', 'gz')
- reduced: float32 [32, 32], replicated
Inputs may be any that keep to these rules, and one draw needn't show every extreme that they name: `slot_snapshot`: -1 marks an empty slot; on every device the live slots come first, and some device has all 32 slots live. `slot_brick`: a brick is named by its device index in the order gx, gy, gz with gz fastest; -1 exactly where slot_snapshot is -1; every pair of a snapshot and a brick is held by exactly one slot; a patch's owner has the same gz index as its brick; no device holds more than 1 patches of one brick, a bound reached in every gz plane.
All inputs are finite; a program needn't handle non-finite values.
Results may differ from a plain program's by a relative error of at most 0.0076.
Values may be sent and summed in bfloat16 or wider, within the bound.
A program may use at most 128 MiB of HBM per device.

v0:
```python
import jax
import jax.numpy as jnp
from jax import lax
from jax.sharding import Mesh
from jax.sharding import PartitionSpec as P

SNAPS = 16
FIELDS = 4
PATCH = 32
MODES = 32
EDGE = 16
CELLS = 4096
COLS = 64
GZ = ("gz_0", "gz_1")
GX_GY_GZ = ("gx", "gy", "gz_0", "gz_1")


HIGHEST = lax.Precision.HIGHEST


def extended(value, sides, width):
    edges = {}
    for axis, dim in sides:
        devices, length = (lax.axis_size(axis), value.shape[dim])
        up = [(i, (i + 1) % devices) for i in range(devices - 1)]
        last = lax.slice_in_dim(value, length - width, length, axis=dim)
        first = lax.slice_in_dim(value, 0, width, axis=dim)
        edges[dim] = (
            lax.ppermute(last, axis, up),
            lax.ppermute(first, axis, [(b, a) for a, b in up]),
        )
    done = []
    for _, dim in sides:
        low, high = edges[dim]
        around = [(width, width) if d in done else (0, 0) for d in range(value.ndim)]
        value = jnp.concatenate([jnp.pad(low, around), value, jnp.pad(high, around)], axis=dim)
        done.append(dim)
    return value


def extended_2(value, sides, width):
    for axis, dim in sides:
        devices, length = (lax.axis_size(axis), value.shape[dim])
        up = [(i, (i + 1) % devices) for i in range(devices - 1)]
        down = [(j, i) for i, j in up]
        last = lax.slice_in_dim(value, length - width, length, axis=dim)
        first = lax.slice_in_dim(value, 0, width, axis=dim)
        before = lax.ppermute(last, axis, up)
        after = lax.ppermute(first, axis, down)
        value = jnp.concatenate([before, value, after], axis=dim)
    return value


def over_axes(value, axes):
    for axis in axes:
        value = lax.psum(value, axis)
    return value


def average_cells(fine_data):
    row_count = fine_data.shape[0]
    view = fine_data.reshape(row_count * FIELDS * EDGE, 2, EDGE, 2 * PATCH)
    pair_x = view[:, 0].astype(jnp.float32) + view[:, 1].astype(jnp.float32)
    pair_y = pair_x[:, :, :PATCH] + pair_x[:, :, PATCH:]
    pairing = (
        jnp.arange(PATCH, dtype=jnp.int32)[:, None] // 2
        == jnp.arange(EDGE, dtype=jnp.int32)[None, :]
    ).astype(jnp.float32) * 0.125
    means = jnp.dot(pair_y.reshape(-1, PATCH), pairing, precision=HIGHEST)
    return means.reshape(row_count, FIELDS, CELLS).astype(jnp.bfloat16)


def seven_point(center, around_xy, around_z, stride):
    total = around_xy[2:, 1:-1] + around_xy[:-2, 1:-1] + around_xy[1:-1, 2:] + around_xy[1:-1, :-2]
    total = total + around_z[:, :, 2 * stride :] + around_z[:, :, : -2 * stride]
    return total - 6.0 * center


def factor_basis(gram_matrix, prior_basis):
    lower_factor = jnp.linalg.cholesky(gram_matrix)
    return lax.linalg.triangular_solve(
        lower_factor, prior_basis, left_side=True, lower=True, transpose_a=True
    )


def shards(patch_fields, slot_snapshot, slot_brick, prior_basis):
    size_x = lax.axis_size("gx")
    size_y = lax.axis_size("gy")
    size_z = lax.axis_size(GZ)
    plane_size = size_x * size_y
    slot_count = slot_snapshot.shape[0]
    pair_depth = slot_count // plane_size
    total_cells = CELLS * plane_size * size_z
    is_live = slot_snapshot >= 0
    slot_ids = jnp.arange(slot_count, dtype=jnp.int32)
    target_peer = jnp.where(is_live, slot_brick // size_z, plane_size)
    earlier = (target_peer[:, None] == target_peer[None, :]) & (
        slot_ids[None, :] < slot_ids[:, None]
    )
    pair_rank = jnp.sum(earlier.astype(jnp.int32), axis=1)
    position = jnp.where(is_live, target_peer * pair_depth + pair_rank, slot_count)
    slot_hits = position[:, None] == slot_ids[None, :]
    filled = jnp.any(slot_hits, axis=0)
    source = jnp.sum(jnp.where(slot_hits, slot_ids[:, None], 0), axis=0)
    sent_snapshot = jnp.where(filled, jnp.take(slot_snapshot, source), -1)
    payload = jnp.take(average_cells(patch_fields), source, axis=0)
    received, received_snapshot = (
        lax.all_to_all(payload, ("gx", "gy"), split_axis=0, concat_axis=0, tiled=True),
        lax.all_to_all(sent_snapshot, ("gx", "gy"), split_axis=0, concat_axis=0, tiled=True),
    )
    snapshots = jnp.arange(SNAPS, dtype=jnp.int32)
    chosen = jnp.sum(
        jnp.where(received_snapshot[None, :] == snapshots[:, None], slot_ids[None, :], 0), axis=1
    )
    arrived = jnp.take(received, chosen, axis=0)
    columns = arrived.reshape(COLS, CELLS)
    partial_gram = jnp.dot(columns, columns.T, preferred_element_type=jnp.float32)
    data_wide = columns.astype(jnp.float32).T
    data_block = columns.T.reshape(EDGE, EDGE, EDGE * COLS)
    data_xy = extended(data_block, (("gx", 0), ("gy", 1)), 1).astype(jnp.float32)
    data_z = extended_2(data_block, ((GZ, 2),), COLS).astype(jnp.float32)
    data_image = seven_point(data_block.astype(jnp.float32), data_xy, data_z, COLS).reshape(
        CELLS, COLS
    )
    partial_cross = jnp.dot(data_wide.T, data_image, precision=HIGHEST)
    gram_total, cross_total = (
        over_axes(partial_gram, GX_GY_GZ),
        over_axes(partial_cross, GX_GY_GZ),
    )
    gram_matrix = gram_total / total_cells
    coeffs = factor_basis(gram_matrix, prior_basis)
    mode_basis = jnp.dot(data_wide, coeffs, precision=HIGHEST)
    mode_image = jnp.dot(data_image, coeffs, precision=HIGHEST)
    inner = jnp.dot(cross_total / total_cells, coeffs, precision=HIGHEST)
    reduced = jnp.dot(coeffs.T, inner, precision=HIGHEST)
    mode_fields = mode_basis.reshape(EDGE, EDGE, EDGE * MODES).astype(jnp.bfloat16)
    diffused = mode_image.reshape(EDGE, EDGE, EDGE * MODES).astype(jnp.bfloat16)
    return (gram_matrix, mode_fields, diffused, reduced)


def solution(mesh):
    split = Mesh(
        mesh.devices.reshape(mesh.shape["gx"], mesh.shape["gy"], 4, 2), ("gx", "gy", "gz_0", "gz_1")
    )
    in_specs = (P(GX_GY_GZ, None, None), P(GX_GY_GZ), P(GX_GY_GZ), P())
    out_specs = (P(), P("gx", "gy", GZ), P("gx", "gy", GZ), P())
    return jax.shard_map(
        shards, mesh=split, in_specs=in_specs, out_specs=out_specs, check_vma=False
    )
```

profile of v0, /device:TPU:1, one launch (start us, length us, event | category | flops | bytes accessed | tf_op | source)
XLA Modules:
  0.0 251.8 jit_solution(11054224175543935289)
XLA Ops:
  2.4 1.4 gather_fusion
  4.4 11.9 %all-to-all-start = ((s32[32,1,1]{2,1,0:T(1,128)}), s32[32,1,1]{2,1,0:T(1,128)S(1)}, u32[]{:S(2)}, u32[]{:S(2)}) async-start(s32[32,1,1]{2,1,0:T(1,128)} %copy.36), calls=%async_computation | async-start | bytes 32768 | tf_op jit(solution)/shard_map/all_to_all | solution.py:109
  16.3 27.2 %reshape.237 = bf16[2048,2,16,64]{3,2,1,0:T(8,128)(2,1)} reshape(bf16[32,4,32768]{2,1,0:T(4,128)(2,1)} %param.4) | data formatting | bytes 16777216 | tf_op jit(solution)/shard_map/reshape | solution.py:62
  43.6 6.9 %add_bitcast_fusion = f32[2048,16,64]{2,1,0:T(8,128)S(1)} fusion(bf16[2048,2,16,64]{3,2,1,0:T(8,128)(2,1)} %reshape.237), kind=kLoop, calls=%fused_computation.5 | loop fusion | flops 6291456 | bytes 16777216 | tf_op jit(solution)/shard_map/add | solution.py:63
  50.5 7.5 %slice_add_fusion = f32[2048,16,32]{2,1,0:T(8,128)} fusion(f32[2048,16,64]{2,1,0:T(8,128)S(1)} %add_bitcast_fusion), kind=kLoop, calls=%fused_computation.4 | loop fusion | flops 1048576 | bytes 12582912 | tf_op jit(solution)/shard_map/add | solution.py:64
  58.0 17.3 %convolution_convert_fusion = bf16[32768,16]{0,1:T(8,128)(2,1)S(1)} fusion(f32[32768,32]{1,0:T(8,128)} %bitcast.40, s32[32]{0:T(128)S(1)} %and_select_fusion), kind=kOutput, calls=%fused_computation.3 | convolution fusion | flops 201851904 | bytes 5243008 | tf_op jit(solution)/shard_map/dot_general | solution.py:69
  75.3 6.2 %copy.37 = bf16[32768,16]{1,0:T(8,128)(2,1)} copy(bf16[32768,16]{0,1:T(8,128)(2,1)S(1)} %convolution_convert_fusion) | data formatting | bytes 2097152 | tf_op jit(solution)/shard_map/convert_element_type | solution.py:70
  81.5 10.8 %convert_element_type.47 = bf16[32,4,4096]{2,1,0:T(4,128)(2,1)S(1)} reshape(bf16[32768,16]{1,0:T(8,128)(2,1)} %copy.37) | data formatting | bytes 2097152 | tf_op jit(solution)/shard_map/convert_element_type | solution.py:70
  92.2 1.4 gather_fusion.1
  93.7 1.6 broadcast_select_fusion
  95.3 9.4 %all-to-all-start.1 = ((bf16[32,4,4096]{2,1,0:T(4,128)(2,1)}), bf16[32,4,4096]{2,1,0:T(4,128)(2,1)S(1)}, u32[]{:S(2)}, u32[]{:S(2)}) async-start(bf16[32,4,4096]{2,1,0:T(4,128)(2,1)} %broadcast_select_fusion), calls=%async_computation.1 | async-start | bytes 2097152 | tf_op jit(solution)/shard_map/all_to_all | solution.py:108
  105.7 23.5 %all-to-all-done.1 = bf16[32,4,4096]{2,1,0:T(4,128)(2,1)S(1)} async-done(((bf16[32,4,4096]{2,1,0:T(4,128)(2,1)}), bf16[32,4,4096]{2,1,0:T(4,128)(2,1)S(1)}, u32[]{:S(2)}, u32[]{:S(2)}) %all-to-all-start.1) | async-done | bytes 1048608 | tf_op jit(solution)/shard_map/all_to_all | solution.py:108
  129.1 1.0 gather_fusion.2
  132.1 8.2 %collective-permute-start.4 = (bf16[16,16,64]{2,1,0:T(8,128)(2,1)S(1)}, bf16[16,16,64]{2,1,0:T(8,128)(2,1)S(1)}, u32[]{:S(2)}, u32[]{:S(2)}) collective-permute-start(bf16[16,16,64]{2,1,0:T(8,128)(2,1)S(1)} %get-tuple-element.37), channel_id=1, source_target_pairs={{0,1},{1,2},{2,3},{3,4},{4,5},{5,6},{6,7},{8,9},{9,10},{10,11},{11... | collective-permute-start | bytes 98312 | tf_op jit(solution)/shard_map/ppermute | solution.py:48
  140.5 1.9 collective-permute-start.5
  142.4 1.3 collective-permute-start.3
  143.7 4.0 %collective-permute-start = (bf16[16,1,1024]{2,1,0:T(2,128)(2,1)S(1)}, bf16[16,1,1024]{2,1,0:T(2,128)(2,1)S(1)}, u32[]{:S(2)}, u32[]{:S(2)}) collective-permute-start(bf16[16,1,1024]{2,1,0:T(2,128)(2,1)S(1)} %get-tuple-element.34), channel_id=1, source_target_pairs={{0,8},{8,16},{16,24},{24,32},{32,40},{40,48},{48,56},{1,9},{9,17},... | collective-permute-start | bytes 98312 | tf_op jit(solution)/shard_map/ppermute | solution.py:29
  147.8 1.3 collective-permute-start.2
  149.2 4.0 %collective-permute-start.1 = (bf16[1,16,1024]{2,1,0:T(8,128)(2,1)S(1)}, bf16[1,16,1024]{2,1,0:T(8,128)(2,1)S(1)}, u32[]{:S(2)}, u32[]{:S(2)}) collective-permute-start(bf16[1,16,1024]{2,1,0:T(8,128)(2,1)S(1)} %slice.70), channel_id=1, source_target_pairs={{0,64},{64,128},{128,192},{1,65},{65,129},{129,193},{2,66},{66,130... | collective-permute-start | bytes 98312 | tf_op jit(solution)/shard_map/ppermute | solution.py:29
  154.7 1.5 fusion.2
  156.1 1.7 reshape.240
  157.8 1.8 fusion.31
  159.6 13.5 %all-reduce.4 = (f32[64,64]{0,1:T(8,128)S(1)}, f32[64,64]{0,1:T(8,128)S(1)}) all-reduce(f32[64,64]{0,1:T(8,128)S(1)} %fusion.30, f32[64,64]{0,1:T(8,128)S(1)} %fusion.31), channel_id=1, replica_groups=mesh['gx'=4,'gy'=8,'gz_0'=4,'gz_1'=2] {'gx'}, use_global_device_ids=true, to_apply=%region_4.5 | all-reduce | flops 8192 | bytes 65536 | tf_op jit(solution)/shard_map/psum | solution.py:56
  173.1 21.7 %all-reduce.2 = (f32[64,64]{0,1:T(8,128)S(1)}, f32[64,64]{0,1:T(8,128)S(1)}) all-reduce(f32[64,64]{0,1:T(8,128)S(1)} %get-tuple-element.28, f32[64,64]{0,1:T(8,128)S(1)} %get-tuple-element.29), channel_id=1, replica_groups=mesh['gx'=4,'gy'=8,'gz_0'=4,'gz_1'=2] {'gy'}, use_global_device_ids=true, to_apply=%region_5.6 | all-reduce | flops 8192 | bytes 65536 | tf_op jit(solution)/shard_map/psum | solution.py:56
  194.8 13.0 %all-reduce.3 = (f32[64,64]{0,1:T(8,128)S(1)}, f32[64,64]{0,1:T(8,128)S(1)}) all-reduce(f32[64,64]{0,1:T(8,128)S(1)} %get-tuple-element.24, f32[64,64]{0,1:T(8,128)S(1)} %get-tuple-element.25), channel_id=1, replica_groups=mesh['gx'=4,'gy'=8,'gz_0'=4,'gz_1'=2] {'gz_0'}, use_global_device_ids=true, to_apply=%region_6.7 | all-reduce | flops 8192 | bytes 65536 | tf_op jit(solution)/shard_map/psum | solution.py:56
  207.9 21.5 %all-reduce.5 = (f32[64,64]{0,1:T(8,128)S(1)}, f32[64,64]{0,1:T(8,128)S(1)}) all-reduce(f32[64,64]{0,1:T(8,128)S(1)} %get-tuple-element.26, f32[64,64]{0,1:T(8,128)S(1)} %get-tuple-element.27), channel_id=1, replica_groups=mesh['gx'=4,'gy'=8,'gz_0'=4,'gz_1'=2] {'gz_1'}, use_global_device_ids=true, to_apply=%region_7.8 | all-reduce | flops 8192 | bytes 65536 | tf_op jit(solution)/shard_map/psum | solution.py:56
  229.6 5.8 %cholesky.16 = f32[64,64]{1,0:T(8,128)S(1)} custom-call(f32[64,64]{1,0:T(8,128)S(1)} %fusion.11), custom_call_target="Cholesky" | custom-call | tf_op jit(solution)/shard_map/jit(cholesky)/cholesky | solution.py:80
  236.7 4.9 %custom-call.6 = f32[1,64,64]{1,2,0:T(8,128)S(1)} custom-call(f32[1,64,64]{2,1,0:T(8,128)S(1)} %fusion.8), custom_call_target="InvertDiagBlocksLowerTriangular" | custom-call | tf_op jit(solution)/shard_map/triangular_solve | solution.py:81
  241.8 2.4 convolution_convert_fusion.2
  244.2 2.3 convolution_convert_fusion.1
  247.0 1.7 convert_element_type.49
  249.2 1.7 convert_element_type.54
  (57 shorter events, 10.5 us)
Async XLA Ops:
  0.6 241.0 %copy-start = (f32[64,32]{0,1:T(8,128)S(1)}, f32[64,32]{0,1:T(8,128)}, u32[]{:S(2)}) copy-start(f32[64,32]{0,1:T(8,128)} %param.7) | copy-start | bytes 24580
  4.4 90.8 %all-to-all-start = ((s32[32,1,1]{2,1,0:T(1,128)}), s32[32,1,1]{2,1,0:T(1,128)S(1)}, u32[]{:S(2)}, u32[]{:S(2)}) async-start(s32[32,1,1]{2,1,0:T(1,128)} %copy.36), calls=%async_computation | async-start | bytes 32768 | tf_op jit(solution)/shard_map/all_to_all | solution.py:109
  95.3 33.9 %all-to-all-start.1 = ((bf16[32,4,4096]{2,1,0:T(4,128)(2,1)}), bf16[32,4,4096]{2,1,0:T(4,128)(2,1)S(1)}, u32[]{:S(2)}, u32[]{:S(2)}) async-start(bf16[32,4,4096]{2,1,0:T(4,128)(2,1)} %broadcast_select_fusion), calls=%async_computation.1 | async-start | bytes 2097152 | tf_op jit(solution)/shard_map/all_to_all | solution.py:108
  131.1 1.1 copy-start.1
  132.1 17.1 %collective-permute-start.4 = (bf16[16,16,64]{2,1,0:T(8,128)(2,1)S(1)}, bf16[16,16,64]{2,1,0:T(8,128)(2,1)S(1)}, u32[]{:S(2)}, u32[]{:S(2)}) collective-permute-start(bf16[16,16,64]{2,1,0:T(8,128)(2,1)S(1)} %get-tuple-element.37), channel_id=1, source_target_pairs={{0,1},{1,2},{2,3},{3,4},{4,5},{5,6},{6,7},{8,9},{9,10},{10,11},{11... | collective-permute-start | bytes 98312 | tf_op jit(solution)/shard_map/ppermute | solution.py:48
  140.5 13.1 %collective-permute-start.5 = (bf16[16,16,64]{2,1,0:T(8,128)(2,1)S(1)}, bf16[16,16,64]{2,1,0:T(8,128)(2,1)S(1)}, u32[]{:S(2)}, u32[]{:S(2)}) collective-permute-start(bf16[16,16,64]{2,1,0:T(8,128)(2,1)S(1)} %get-tuple-element.36), channel_id=1, source_target_pairs={{1,0},{2,1},{3,2},{4,3},{5,4},{6,5},{7,6},{9,8},{10,9},{11,10},{12... | collective-permute-start | bytes 98312 | tf_op jit(solution)/shard_map/ppermute | solution.py:49
  142.4 11.8 %collective-permute-start.3 = (bf16[16,1,1024]{2,1,0:T(2,128)(2,1)S(1)}, bf16[16,1,1024]{2,1,0:T(2,128)(2,1)S(1)}, u32[]{:S(2)}, u32[]{:S(2)}) collective-permute-start(bf16[16,1,1024]{2,1,0:T(2,128)(2,1)S(1)} %get-tuple-element.35), channel_id=1, source_target_pairs={{8,0},{16,8},{24,16},{32,24},{40,32},{48,40},{56,48},{9,1},{17,9},... | collective-permute-start | bytes 98312 | tf_op jit(solution)/shard_map/ppermute | solution.py:30
  143.7 10.6 %collective-permute-start = (bf16[16,1,1024]{2,1,0:T(2,128)(2,1)S(1)}, bf16[16,1,1024]{2,1,0:T(2,128)(2,1)S(1)}, u32[]{:S(2)}, u32[]{:S(2)}) collective-permute-start(bf16[16,1,1024]{2,1,0:T(2,128)(2,1)S(1)} %get-tuple-element.34), channel_id=1, source_target_pairs={{0,8},{8,16},{16,24},{24,32},{32,40},{40,48},{48,56},{1,9},{9,17},... | collective-permute-start | bytes 98312 | tf_op jit(solution)/shard_map/ppermute | solution.py:29
  147.8 6.5 %collective-permute-start.2 = (bf16[1,16,1024]{2,1,0:T(8,128)(2,1)S(1)}, bf16[1,16,1024]{2,1,0:T(8,128)(2,1)S(1)}, u32[]{:S(2)}, u32[]{:S(2)}) collective-permute-start(bf16[1,16,1024]{2,1,0:T(8,128)(2,1)S(1)} %slice.72), channel_id=1, source_target_pairs={{64,0},{128,64},{192,128},{65,1},{129,65},{193,129},{66,2},{130,66... | collective-permute-start | bytes 98312 | tf_op jit(solution)/shard_map/ppermute | solution.py:30
  149.2 5.0 %collective-permute-start.1 = (bf16[1,16,1024]{2,1,0:T(8,128)(2,1)S(1)}, bf16[1,16,1024]{2,1,0:T(8,128)(2,1)S(1)}, u32[]{:S(2)}, u32[]{:S(2)}) collective-permute-start(bf16[1,16,1024]{2,1,0:T(8,128)(2,1)S(1)} %slice.70), channel_id=1, source_target_pairs={{0,64},{64,128},{128,192},{1,65},{65,129},{129,193},{2,66},{66,130... | collective-permute-start | bytes 98312 | tf_op jit(solution)/shard_map/ppermute | solution.py:29
  229.5 16.9 %copy-start.2 = (f32[64,64]{1,0:T(8,128)}, f32[64,64]{1,0:T(8,128)S(1)}, u32[]{:S(2)}) copy-start(f32[64,64]{1,0:T(8,128)S(1)} %copy.44) | copy-start | bytes 49156
where the time goes:
time: 253 us; the launch traced here: 252 us
  blocking collectives  69.8 us (28%)
  local copies, waits for them, and re-layouts  57.5 us (23%)
  starting transfers between devices  42 us (17%)
  other arithmetic  32.9 us (13%)
  matrix products  25.1 us (10%)
  waiting for transfers between devices  23.5 us (9%)
    psum x4, blocking collectives, over_axes(): value = lax.psum(value, axis)  69.8 us
    reshape x1, local copies, waits for them, and re-layouts, average_cells(): view = fine_data.reshape(row_count * FIELDS * EDGE, 2, EDGE, 2 * PATCH)  27.2 us
    all_to_all x1, waiting for transfers between devices, shards(): lax.all_to_all(payload, ('gx', 'gy'), split_axis=0, concat_axis=0, tiled=...  23.5 us
    dot_general x1, matrix products, average_cells(): means = jnp.dot(pair_y.reshape(-1, PATCH), pairing, precision=HIGHEST)  17.3 us
    convert_element_type x2, local copies, waits for them, and re-layouts, average_cells(): return means.reshape(row_count, FIELDS, CELLS).astype(jnp.bfloat16)  17 us
    all_to_all x1, starting transfers between devices, shards(): lax.all_to_all(sent_snapshot, ('gx', 'gy'), split_axis=0, concat_axis=0,...  11.9 us
    all_to_all x1, starting transfers between devices, shards(): lax.all_to_all(payload, ('gx', 'gy'), split_axis=0, concat_axis=0, tiled=...  9.4 us
    ppermute x1, starting transfers between devices, extended_2(): before = lax.ppermute(last, axis, up)  8.21 us
  transfers between devices with their start and end apart: 8, of which 1 were waited for; matrix products, arithmetic and copies ran while one was open for 32% of the time, Pallas kernels for 0%

commit v1 on v0

--- a/solution.py
+++ b/solution.py
@@ -3,6 +3,8 @@
 from jax import lax
 from jax.sharding import Mesh
 from jax.sharding import PartitionSpec as P
+from jax.experimental import pallas as pl
+from jax.experimental.pallas import tpu as pltpu
 
 SNAPS = 16
 FIELDS = 4
@@ -57,17 +59,48 @@
     return value
 
 
+def pairing_matrix():
+    fine = jnp.arange(2 * PATCH * PATCH, dtype=jnp.int32)
+    fine_y = fine % (PATCH * PATCH) // PATCH
+    fine_z = fine % PATCH
+    coarse = jnp.arange(EDGE * EDGE, dtype=jnp.int32)
+    hit = ((fine_y // 2 * EDGE + fine_z // 2)[:, None] == coarse[None, :])
+    return jnp.where(hit, 0.125, 0.0).astype(jnp.bfloat16)
+
+
+PAIRS_PER_STEP = 4
+
+
+def average_kernel(fine_ref, pairing_ref, out_ref):
+    rows = fine_ref.shape[0]
+    span = 2 * PATCH * PATCH
+    stacked = jnp.concatenate(
+        [fine_ref[:, i * span : (i + 1) * span] for i in range(PAIRS_PER_STEP)], axis=0
+    )
+    means = jnp.dot(stacked, pairing_ref[...], preferred_element_type=jnp.float32)
+    width = EDGE * EDGE
+    for i in range(PAIRS_PER_STEP):
+        out_ref[:, i * width : (i + 1) * width] = means[i * rows : (i + 1) * rows].astype(out_ref.dtype)
+
+
 def average_cells(fine_data):
     row_count = fine_data.shape[0]
-    view = fine_data.reshape(row_count * FIELDS * EDGE, 2, EDGE, 2 * PATCH)
-    pair_x = view[:, 0].astype(jnp.float32) + view[:, 1].astype(jnp.float32)
-    pair_y = pair_x[:, :, :PATCH] + pair_x[:, :, PATCH:]
-    pairing = (
-        jnp.arange(PATCH, dtype=jnp.int32)[:, None] // 2
-        == jnp.arange(EDGE, dtype=jnp.int32)[None, :]
-    ).astype(jnp.float32) * 0.125
-    means = jnp.dot(pair_y.reshape(-1, PATCH), pairing, precision=HIGHEST)
-    return means.reshape(row_count, FIELDS, CELLS).astype(jnp.bfloat16)
+    rows = row_count * FIELDS
+    flat = fine_data.reshape(rows, PATCH * PATCH * PATCH)
+    span = 2 * PATCH * PATCH * PAIRS_PER_STEP
+    width = EDGE * EDGE * PAIRS_PER_STEP
+    steps = EDGE // PAIRS_PER_STEP
+    means = pl.pallas_call(
+        average_kernel,
+        grid=(steps,),
+        in_specs=[
+            pl.BlockSpec((rows, span), lambda g: (0, g)),
+            pl.BlockSpec((2 * PATCH * PATCH, EDGE * EDGE), lambda g: (0, 0)),
+        ],
+        out_specs=pl.BlockSpec((rows, width), lambda g: (0, g)),
+        out_shape=jax.ShapeDtypeStruct((rows, CELLS), jnp.bfloat16),
+    )(flat, pairing_matrix())
+    return means.reshape(row_count, FIELDS, CELLS)
 
 
 def seven_point(center, around_xy, around_z, stride):
@@ -123,10 +156,8 @@
         CELLS, COLS
     )
     partial_cross = jnp.dot(data_wide.T, data_image, precision=HIGHEST)
-    gram_total, cross_total = (
-        over_axes(partial_gram, GX_GY_GZ),
-        over_axes(partial_cross, GX_GY_GZ),
-    )
+    gram_total = lax.psum(partial_gram, GX_GY_GZ)
+    cross_total = lax.psum(partial_cross, GX_GY_GZ)
     gram_matrix = gram_total / total_cells
     coeffs = factor_basis(gram_matrix, prior_basis)
     mode_basis = jnp.dot(data_wide, coeffs, precision=HIGHEST)

time: 253 us -> 205 us (0.81)
  local copies, waits for them, and re-layouts: 57.5 us -> 28.5 us
  matrix products: 25.1 us -> 5.85 us
  other arithmetic: 32.9 us -> 19.8 us
  blocking collectives: 69.8 us -> 77.4 us
  Pallas kernels: 0 us -> 6.59 us
    dot_general x1 -> x0, matrix products: 17.3 us -> none  [average_cells(): means = jnp.dot(pair_y.reshape(-1, PATCH), pairing, precision=HIGHEST)]
    convert_element_type x2 -> x0, local copies, waits for them, and re-layouts: 17 us -> none  [average_cells(): return means.reshape(row_count, FIELDS, CELLS).astype(jnp.bfloat16)]
    add x2 -> x1, other arithmetic: 14.4 us -> 0.02 us  [pairing_matrix(): hit = (fine_y // 2 * EDGE + fine_z // 2)[:, None] == coarse[None, :]]
    reshape x1 -> x2, local copies, waits for them, and re-layouts: 27.2 us -> 14.1 us  [the longest x1 12.7 us: average_cells(): flat = fine_data.reshape(rows, PATCH * PATCH * PATCH)]
    psum x4 -> x1, blocking collectives: 69.8 us -> 77.4 us  [shards(): gram_total = lax.psum(partial_gram, GX_GY_GZ)]
    pallas_call x0 -> x1, Pallas kernels: none -> 6.59 us  [average_cells(): pl.pallas_call(average_kernel, grid=(steps,), in_specs=[pl.BlockSpec((row...]
  transfers between devices with their start and end apart: 8 -> 8, of which waited for: 1 -> 1; matrix products, arithmetic and copies ran while one was open for 32% -> 10% of each run, Pallas kernels for 0% -> 3%
where the time goes in v1:
time: 205 us
  blocking collectives  77.4 us (38%)
  starting transfers between devices  41.8 us (20%)
  local copies, waits for them, and re-layouts  28.5 us (14%)
  waiting for transfers between devices  23.7 us (12%)
  other arithmetic  19.8 us (10%)
  Pallas kernels  6.59 us (3%)
  matrix products  5.85 us (3%)
    psum x1, blocking collectives, shards(): gram_total = lax.psum(partial_gram, GX_GY_GZ)  77.4 us
    all_to_all x1, waiting for transfers between devices, shards(): lax.all_to_all(payload, ('gx', 'gy'), split_axis=0, concat_axis=0, tiled=...  23.7 us
    reshape x1, local copies, waits for them, and re-layouts, average_cells(): flat = fine_data.reshape(rows, PATCH * PATCH * PATCH)  12.7 us
    all_to_all x1, starting transfers between devices, shards(): lax.all_to_all(sent_snapshot, ('gx', 'gy'), split_axis=0, concat_axis=0,...  11.9 us
    all_to_all x1, starting transfers between devices, shards(): lax.all_to_all(payload, ('gx', 'gy'), split_axis=0, concat_axis=0, tiled=...  9.22 us
    ppermute x1, starting transfers between devices, extended_2(): before = lax.ppermute(last, axis, up)  8.21 us
    ppermute x2, starting transfers between devices, extended(): lax.ppermute(last, axis, up)  7.98 us
    pallas_call x1, Pallas kernels, average_cells(): pl.pallas_call(average_kernel, grid=(steps,), in_specs=[pl.BlockSpec((row...  6.59 us
  transfers between devices with their start and end apart: 8, of which 1 were waited for; matrix products, arithmetic and copies ran while one was open for 10% of the time, Pallas kernels for 3%

profile of v1, /device:TPU:1, one launch (start us, length us, event | category | flops | bytes accessed | tf_op | source)
XLA Modules:
  0.0 204.6 jit_solution(1054657924487829620)
XLA Ops:
  0.6 0.7 compare_select_fusion.9
  1.5 0.7 compare_select_fusion.8
  2.4 1.4 gather_fusion
  3.7 0.7 copy.46
  4.4 11.9 %all-to-all-start = ((s32[32,1,1]{2,1,0:T(1,128)}), s32[32,1,1]{2,1,0:T(1,128)S(1)}, u32[]{:S(2)}, u32[]{:S(2)}) async-start(s32[32,1,1]{2,1,0:T(1,128)} %copy.46), calls=%async_computation | async-start | bytes 32768 | tf_op jit(solution)/shard_map/all_to_all | solution.py:142
  16.4 12.7 %reshape.258.fine_ref = bf16[128,32768]{1,0:T(8,128)(2,1)} reshape(bf16[32,4,32768]{2,1,0:T(4,128)(2,1)} %param.4) | data formatting | bytes 16777216 | tf_op jit(solution)/shard_map/reshape | solution.py:89
  29.0 1.3 select_convert_fusion.pairing_ref
  30.3 6.6 %shard_map.75 = bf16[128,4096]{1,0:T(8,128)(2,1)} custom-call(bf16[128,32768]{1,0:T(8,128)(2,1)} %reshape.258.fine_ref, bf16[2048,256]{1,0:T(8,128)(2,1)} %select_convert_fusion.pairing_ref), custom_call_target="tpu_custom_call" | custom-call | tf_op jit(solution)/shard_map/pallas_call | solution.py:93
  36.9 1.5 reshape.259
  38.4 1.4 gather_fusion.1
  39.8 1.6 broadcast_select_fusion
  41.4 9.2 %all-to-all-start.1 = ((bf16[32,4,4096]{2,1,0:T(4,128)(2,1)}), bf16[32,4,4096]{2,1,0:T(4,128)(2,1)S(1)}, u32[]{:S(2)}, u32[]{:S(2)}) async-start(bf16[32,4,4096]{2,1,0:T(4,128)(2,1)} %broadcast_select_fusion), calls=%async_computation.1 | async-start | bytes 2097152 | tf_op jit(solution)/shard_map/all_to_all | solution.py:141
  51.6 23.7 %all-to-all-done.1 = bf16[32,4,4096]{2,1,0:T(4,128)(2,1)S(1)} async-done(((bf16[32,4,4096]{2,1,0:T(4,128)(2,1)}), bf16[32,4,4096]{2,1,0:T(4,128)(2,1)S(1)}, u32[]{:S(2)}, u32[]{:S(2)}) %all-to-all-start.1) | async-done | bytes 1048608 | tf_op jit(solution)/shard_map/all_to_all | solution.py:141
  75.2 1.0 gather_fusion.2
  76.7 0.8 copy-done.1
  78.1 0.7 reshape.260
  79.0 8.2 %collective-permute-start.4 = (bf16[16,16,64]{2,1,0:T(8,128)(2,1)S(1)}, bf16[16,16,64]{2,1,0:T(8,128)(2,1)S(1)}, u32[]{:S(2)}, u32[]{:S(2)}) collective-permute-start(bf16[16,16,64]{2,1,0:T(8,128)(2,1)S(1)} %get-tuple-element.35), channel_id=1, source_target_pairs={{0,1},{1,2},{2,3},{3,4},{4,5},{5,6},{6,7},{8,9},{9,10},{10,11},{11... | collective-permute-start | bytes 98312 | tf_op jit(solution)/shard_map/ppermute | solution.py:50
  87.4 1.9 collective-permute-start.5
  89.3 1.3 collective-permute-start.3
  90.6 4.0 %collective-permute-start = (bf16[16,1,1024]{2,1,0:T(2,128)(2,1)S(1)}, bf16[16,1,1024]{2,1,0:T(2,128)(2,1)S(1)}, u32[]{:S(2)}, u32[]{:S(2)}) collective-permute-start(bf16[16,1,1024]{2,1,0:T(2,128)(2,1)S(1)} %get-tuple-element.32), channel_id=1, source_target_pairs={{0,8},{8,16},{16,24},{24,32},{32,40},{40,48},{48,56},{1,9},{9,17},... | collective-permute-start | bytes 98312 | tf_op jit(solution)/shard_map/ppermute | solution.py:31
  94.9 1.3 collective-permute-start.2
  96.4 4.0 %collective-permute-start.1 = (bf16[1,16,1024]{2,1,0:T(8,128)(2,1)S(1)}, bf16[1,16,1024]{2,1,0:T(8,128)(2,1)S(1)}, u32[]{:S(2)}, u32[]{:S(2)}) collective-permute-start(bf16[1,16,1024]{2,1,0:T(8,128)(2,1)S(1)} %slice.54), channel_id=1, source_target_pairs={{0,64},{64,128},{128,192},{1,65},{65,129},{129,193},{2,66},{66,130... | collective-permute-start | bytes 98312 | tf_op jit(solution)/shard_map/ppermute | solution.py:31
  101.8 1.4 fusion.2
  103.3 1.7 reshape.261
  105.0 1.8 fusion.44
  106.8 77.4 %all-reduce.2 = (f32[64,64]{0,1:T(8,128)S(1)}, f32[64,64]{0,1:T(8,128)S(1)}) all-reduce(f32[64,64]{0,1:T(8,128)S(1)} %fusion.43, f32[64,64]{0,1:T(8,128)S(1)} %fusion.44), channel_id=1, replica_groups=mesh['gx'=4,'gy'=8,'gz_0'=4,'gz_1'=2] {'gx','gy','gz_0','gz_1'}, use_global_device_ids=true, to_apply=%region_4.5 | all-reduce | flops 8192 | bytes 65536 | tf_op jit(solution)/shard_map/psum | solution.py:159
  184.2 5.8 %cholesky.16 = f32[64,64]{1,0:T(8,128)S(1)} custom-call(f32[64,64]{1,0:T(8,128)S(1)} %fusion.10), custom_call_target="Cholesky" | custom-call | tf_op jit(solution)/shard_map/jit(cholesky)/cholesky | solution.py:113
  191.4 4.9 %custom-call.6 = f32[1,64,64]{1,2,0:T(8,128)S(1)} custom-call(f32[1,64,64]{2,1,0:T(8,128)S(1)} %fusion.7), custom_call_target="InvertDiagBlocksLowerTriangular" | custom-call | tf_op jit(solution)/shard_map/triangular_solve | solution.py:114
  197.0 2.3 %convolution_convert_fusion = bf16[4096,32]{0,1:T(8,128)(2,1)S(1)} fusion(f32[4096,64]{1,0:T(8,128)S(1)} %reshape.261, f32[64,32]{0,1:T(8,128)S(1)} %fusion.8), kind=kOutput, calls=%fused_computation.3 | convolution fusion | flops 100794368 | bytes 1318912 | tf_op jit(solution)/shard_map/dot_general | solution.py:164
  199.7 1.7 convert_element_type.34
  201.9 1.7 convert_element_type.39
  203.8 0.8 fusion.45
  (56 shorter events, 7.7 us)
Async XLA Ops:
  0.6 195.7 %copy-start = (f32[64,32]{0,1:T(8,128)S(1)}, f32[64,32]{0,1:T(8,128)}, u32[]{:S(2)}) copy-start(f32[64,32]{0,1:T(8,128)} %param.7) | copy-start | bytes 24580
  4.4 36.9 %all-to-all-start = ((s32[32,1,1]{2,1,0:T(1,128)}), s32[32,1,1]{2,1,0:T(1,128)S(1)}, u32[]{:S(2)}, u32[]{:S(2)}) async-start(s32[32,1,1]{2,1,0:T(1,128)} %copy.46), calls=%async_computation | async-start | bytes 32768 | tf_op jit(solution)/shard_map/all_to_all | solution.py:142
  41.4 33.9 %all-to-all-start.1 = ((bf16[32,4,4096]{2,1,0:T(4,128)(2,1)}), bf16[32,4,4096]{2,1,0:T(4,128)(2,1)S(1)}, u32[]{:S(2)}, u32[]{:S(2)}) async-start(bf16[32,4,4096]{2,1,0:T(4,128)(2,1)} %broadcast_select_fusion), calls=%async_computation.1 | async-start | bytes 2097152 | tf_op jit(solution)/shard_map/all_to_all | solution.py:141
  76.7 0.8 copy-start.1
  79.0 17.4 %collective-permute-start.4 = (bf16[16,16,64]{2,1,0:T(8,128)(2,1)S(1)}, bf16[16,16,64]{2,1,0:T(8,128)(2,1)S(1)}, u32[]{:S(2)}, u32[]{:S(2)}) collective-permute-start(bf16[16,16,64]{2,1,0:T(8,128)(2,1)S(1)} %get-tuple-element.35), channel_id=1, source_target_pairs={{0,1},{1,2},{2,3},{3,4},{4,5},{5,6},{6,7},{8,9},{9,10},{10,11},{11... | collective-permute-start | bytes 98312 | tf_op jit(solution)/shard_map/ppermute | solution.py:50
  87.4 13.3 %collective-permute-start.5 = (bf16[16,16,64]{2,1,0:T(8,128)(2,1)S(1)}, bf16[16,16,64]{2,1,0:T(8,128)(2,1)S(1)}, u32[]{:S(2)}, u32[]{:S(2)}) collective-permute-start(bf16[16,16,64]{2,1,0:T(8,128)(2,1)S(1)} %get-tuple-element.34), channel_id=1, source_target_pairs={{1,0},{2,1},{3,2},{4,3},{5,4},{6,5},{7,6},{9,8},{10,9},{11,10},{12... | collective-permute-start | bytes 98312 | tf_op jit(solution)/shard_map/ppermute | solution.py:51
  89.3 12.1 %collective-permute-start.3 = (bf16[16,1,1024]{2,1,0:T(2,128)(2,1)S(1)}, bf16[16,1,1024]{2,1,0:T(2,128)(2,1)S(1)}, u32[]{:S(2)}, u32[]{:S(2)}) collective-permute-start(bf16[16,1,1024]{2,1,0:T(2,128)(2,1)S(1)} %get-tuple-element.33), channel_id=1, source_target_pairs={{8,0},{16,8},{24,16},{32,24},{40,32},{48,40},{56,48},{9,1},{17,9},... | collective-permute-start | bytes 98312 | tf_op jit(solution)/shard_map/ppermute | solution.py:32
  90.6 10.8 %collective-permute-start = (bf16[16,1,1024]{2,1,0:T(2,128)(2,1)S(1)}, bf16[16,1,1024]{2,1,0:T(2,128)(2,1)S(1)}, u32[]{:S(2)}, u32[]{:S(2)}) collective-permute-start(bf16[16,1,1024]{2,1,0:T(2,128)(2,1)S(1)} %get-tuple-element.32), channel_id=1, source_target_pairs={{0,8},{8,16},{16,24},{24,32},{32,40},{40,48},{48,56},{1,9},{9,17},... | collective-permute-start | bytes 98312 | tf_op jit(solution)/shard_map/ppermute | solution.py:31
  94.9 6.6 %collective-permute-start.2 = (bf16[1,16,1024]{2,1,0:T(8,128)(2,1)S(1)}, bf16[1,16,1024]{2,1,0:T(8,128)(2,1)S(1)}, u32[]{:S(2)}, u32[]{:S(2)}) collective-permute-start(bf16[1,16,1024]{2,1,0:T(8,128)(2,1)S(1)} %slice.56), channel_id=1, source_target_pairs={{64,0},{128,64},{192,128},{65,1},{129,65},{193,129},{66,2},{130,66... | collective-permute-start | bytes 98312 | tf_op jit(solution)/shard_map/ppermute | solution.py:32
  96.4 5.0 %collective-permute-start.1 = (bf16[1,16,1024]{2,1,0:T(8,128)(2,1)S(1)}, bf16[1,16,1024]{2,1,0:T(8,128)(2,1)S(1)}, u32[]{:S(2)}, u32[]{:S(2)}) collective-permute-start(bf16[1,16,1024]{2,1,0:T(8,128)(2,1)S(1)} %slice.54), channel_id=1, source_target_pairs={{0,64},{64,128},{128,192},{1,65},{65,129},{129,193},{2,66},{66,130... | collective-permute-start | bytes 98312 | tf_op jit(solution)/shard_map/ppermute | solution.py:31
  105.0 91.6 %copy-start.2 = (bf16[64,4096]{1,0:T(8,128)(2,1)S(1)}, bf16[64,4096]{1,0:T(8,128)(2,1)}, u32[]{:S(2)}) copy-start(bf16[64,4096]{1,0:T(8,128)(2,1)} %copy-done.1) | copy-start | bytes 1572868
  184.2 15.5 %copy-start.3 = (f32[64,64]{1,0:T(8,128)}, f32[64,64]{1,0:T(8,128)S(1)}, u32[]{:S(2)}) copy-start(f32[64,64]{1,0:T(8,128)S(1)} %copy.55) | copy-start | bytes 49156

commit v2 on v1

--- a/solution.py
+++ b/solution.py
@@ -1,3 +1,5 @@
+import functools
+
 import jax
 import jax.numpy as jnp
 from jax import lax
@@ -116,6 +118,75 @@
     )
 
 
+def tree_sum(values):
+    while len(values) > 1:
+        values = [values[i] + values[i + 1] for i in range(0, len(values), 2)]
+    return values[0]
+
+
+def allreduce_kernel(sizes, part_ref, out_ref, acc, *rest):
+    bufs, (send_sems, recv_sems) = rest[: len(sizes)], rest[len(sizes) :]
+    me = [lax.axis_index(axis) for axis in GX_GY_GZ]
+
+    def peer(dim, step):
+        device = list(me)
+        device[dim] = lax.rem(me[dim] + step, sizes[dim])
+        return tuple(device)
+
+    barrier = pltpu.get_barrier_semaphore()
+    count = 0
+    for dim, size in enumerate(sizes):
+        for step in range(1, size):
+            pl.semaphore_signal(
+                barrier, inc=1, device_id=peer(dim, step), device_id_type=pl.DeviceIdType.MESH
+            )
+            count += 1
+    pl.semaphore_wait(barrier, count)
+    acc[...] = part_ref[...]
+    slot = 0
+    for dim, size in enumerate(sizes):
+        if size == 1:
+            continue
+        buf = bufs[dim]
+        copies = []
+        for step in range(1, size):
+            copy = pltpu.make_async_remote_copy(
+                src_ref=acc,
+                dst_ref=buf.at[step - 1],
+                send_sem=send_sems.at[slot],
+                recv_sem=recv_sems.at[slot],
+                device_id=peer(dim, step),
+                device_id_type=pl.DeviceIdType.MESH,
+            )
+            copy.start()
+            copies.append(copy)
+            slot += 1
+        for copy in copies:
+            copy.wait()
+        own = acc[...]
+        values = []
+        for source in range(size):
+            held = jnp.maximum(lax.rem(me[dim] - source + size, size) - 1, 0)
+            values.append(jnp.where(me[dim] == source, own, buf[held]))
+        acc[...] = tree_sum(values)
+    out_ref[...] = acc[...]
+
+
+def allreduce(part):
+    sizes = tuple(lax.axis_size(axis) for axis in GX_GY_GZ)
+    copies = sum(size - 1 for size in sizes)
+    return pl.pallas_call(
+        functools.partial(allreduce_kernel, sizes),
+        out_shape=jax.ShapeDtypeStruct(part.shape, part.dtype),
+        in_specs=[pl.BlockSpec(memory_space=pltpu.VMEM)],
+        out_specs=pl.BlockSpec(memory_space=pltpu.VMEM),
+        scratch_shapes=[pltpu.VMEM(part.shape, part.dtype)]
+        + [pltpu.VMEM((max(size - 1, 1),) + part.shape, part.dtype) for size in sizes]
+        + [pltpu.SemaphoreType.DMA((copies,)), pltpu.SemaphoreType.DMA((copies,))],
+        compiler_params=pltpu.CompilerParams(collective_id=0, has_side_effects=True),
+    )(part)
+
+
 def shards(patch_fields, slot_snapshot, slot_brick, prior_basis):
     size_x = lax.axis_size("gx")
     size_y = lax.axis_size("gy")
@@ -156,8 +227,8 @@
         CELLS, COLS
     )
     partial_cross = jnp.dot(data_wide.T, data_image, precision=HIGHEST)
-    gram_total = lax.psum(partial_gram, GX_GY_GZ)
-    cross_total = lax.psum(partial_cross, GX_GY_GZ)
+    totals = allreduce(jnp.concatenate([partial_gram, partial_cross], axis=1))
+    gram_total, cross_total = totals[:, :COLS], totals[:, COLS:]
     gram_matrix = gram_total / total_cells
     coeffs = factor_basis(gram_matrix, prior_basis)
     mode_basis = jnp.dot(data_wide, coeffs, precision=HIGHEST)

time: 205 us -> 154 us (0.75)
  blocking collectives: 77.4 us -> 0 us
  Pallas kernels: 6.59 us -> 31.5 us
    psum x1 -> x0, blocking collectives: 77.4 us -> none  [shards(): gram_total = lax.psum(partial_gram, GX_GY_GZ)]
    pallas_call x0 -> x1, Pallas kernels: none -> 24.9 us  [allreduce(): pl.pallas_call(functools.partial(allreduce_kernel, sizes), out_shape=jax....]
  transfers between devices with their start and end apart: 8 -> 8, of which waited for: 1 -> 1; matrix products, arithmetic and copies ran while one was open for 10% -> 14% of each run, Pallas kernels for 3% -> 4%
where the time goes in v2:
time: 154 us; the launch traced here: 153 us
  starting transfers between devices  42 us (27%)
  Pallas kernels  31.5 us (20%)
  local copies, waits for them, and re-layouts  29.5 us (19%)
  waiting for transfers between devices  23.7 us (15%)
  other arithmetic  20.5 us (13%)
  matrix products  4.97 us (3%)
    pallas_call x1, Pallas kernels, allreduce(): pl.pallas_call(functools.partial(allreduce_kernel, sizes), out_shape=jax....  24.9 us
    all_to_all x1, waiting for transfers between devices, shards(): lax.all_to_all(payload, ('gx', 'gy'), split_axis=0, concat_axis=0, tiled=...  23.7 us
    reshape x1, local copies, waits for them, and re-layouts, average_cells(): flat = fine_data.reshape(rows, PATCH * PATCH * PATCH)  12.7 us
    all_to_all x1, starting transfers between devices, shards(): lax.all_to_all(sent_snapshot, ('gx', 'gy'), split_axis=0, concat_axis=0,...  11.9 us
    all_to_all x1, starting transfers between devices, shards(): lax.all_to_all(payload, ('gx', 'gy'), split_axis=0, concat_axis=0, tiled=...  9.22 us
    ppermute x1, starting transfers between devices, extended_2(): before = lax.ppermute(last, axis, up)  8.2 us
    ppermute x2, starting transfers between devices, extended(): lax.ppermute(last, axis, up)  8.16 us
    pallas_call x1, Pallas kernels, average_cells(): pl.pallas_call(average_kernel, grid=(steps,), in_specs=[pl.BlockSpec((row...  6.59 us
  transfers between devices with their start and end apart: 8, of which 1 were waited for; matrix products, arithmetic and copies ran while one was open for 14% of the time, Pallas kernels for 4%

profile of v2, /device:TPU:1, one launch (start us, length us, event | category | flops | bytes accessed | tf_op | source)
XLA Modules:
  0.0 153.1 jit_solution(16346521785139003733)
XLA Ops:
  2.4 1.4 gather_fusion
  3.7 0.7 copy.48
  4.4 11.9 %all-to-all-start = ((s32[32,1,1]{2,1,0:T(1,128)}), s32[32,1,1]{2,1,0:T(1,128)S(1)}, u32[]{:S(2)}, u32[]{:S(2)}) async-start(s32[32,1,1]{2,1,0:T(1,128)} %copy.48), calls=%async_computation | async-start | bytes 32768 | tf_op jit(solution)/shard_map/all_to_all | solution.py:213
  16.4 12.7 %reshape.258.fine_ref = bf16[128,32768]{1,0:T(8,128)(2,1)} reshape(bf16[32,4,32768]{2,1,0:T(4,128)(2,1)} %param.4) | data formatting | bytes 16777216 | tf_op jit(solution)/shard_map/reshape | solution.py:91
  29.0 1.3 select_convert_fusion.pairing_ref
  30.3 6.6 %shard_map.75 = bf16[128,4096]{1,0:T(8,128)(2,1)} custom-call(bf16[128,32768]{1,0:T(8,128)(2,1)} %reshape.258.fine_ref, bf16[2048,256]{1,0:T(8,128)(2,1)} %select_convert_fusion.pairing_ref), custom_call_target="tpu_custom_call" | custom-call | tf_op jit(solution)/shard_map/pallas_call | solution.py:95
  36.9 1.5 reshape.259
  38.4 1.4 gather_fusion.1
  39.8 1.6 %broadcast_select_fusion = bf16[32,4,4096]{2,1,0:T(4,128)(2,1)} fusion(bf16[32,4,4096]{2,1,0:T(4,128)(2,1)S(1)} %gather_fusion.1, pred[32]{0:T(512)(128)(4,1)S(1)} %compare_and_fusion), kind=kLoop, calls=%fused_computation.17 | loop fusion | flops 524288 | bytes 2097184 | tf_op jit(solution)/shard_map/jit(_take)/select_n | solution.py:210
  41.4 9.2 %all-to-all-start.1 = ((bf16[32,4,4096]{2,1,0:T(4,128)(2,1)}), bf16[32,4,4096]{2,1,0:T(4,128)(2,1)S(1)}, u32[]{:S(2)}, u32[]{:S(2)}) async-start(bf16[32,4,4096]{2,1,0:T(4,128)(2,1)} %broadcast_select_fusion), calls=%async_computation.1 | async-start | bytes 2097152 | tf_op jit(solution)/shard_map/all_to_all | solution.py:212
  51.6 23.7 %all-to-all-done.1 = bf16[32,4,4096]{2,1,0:T(4,128)(2,1)S(1)} async-done(((bf16[32,4,4096]{2,1,0:T(4,128)(2,1)}), bf16[32,4,4096]{2,1,0:T(4,128)(2,1)S(1)}, u32[]{:S(2)}, u32[]{:S(2)}) %all-to-all-start.1) | async-done | bytes 1048608 | tf_op jit(solution)/shard_map/all_to_all | solution.py:212
  75.3 1.0 gather_fusion.2
  76.7 0.8 copy-done.1
  78.1 0.7 reshape.260
  79.0 8.2 %collective-permute-start.4 = (bf16[16,16,64]{2,1,0:T(8,128)(2,1)S(1)}, bf16[16,16,64]{2,1,0:T(8,128)(2,1)S(1)}, u32[]{:S(2)}, u32[]{:S(2)}) collective-permute-start(bf16[16,16,64]{2,1,0:T(8,128)(2,1)S(1)} %get-tuple-element.33), channel_id=1, source_target_pairs={{0,1},{1,2},{2,3},{3,4},{4,5},{5,6},{6,7},{8,9},{9,10},{10,11},{11... | collective-permute-start | bytes 98312 | tf_op jit(solution)/shard_map/ppermute | solution.py:52
  87.4 1.9 %collective-permute-start.5 = (bf16[16,16,64]{2,1,0:T(8,128)(2,1)S(1)}, bf16[16,16,64]{2,1,0:T(8,128)(2,1)S(1)}, u32[]{:S(2)}, u32[]{:S(2)}) collective-permute-start(bf16[16,16,64]{2,1,0:T(8,128)(2,1)S(1)} %get-tuple-element.32), channel_id=1, source_target_pairs={{1,0},{2,1},{3,2},{4,3},{5,4},{6,5},{7,6},{9,8},{10,9},{11,10},{12... | collective-permute-start | bytes 98312 | tf_op jit(solution)/shard_map/ppermute | solution.py:53
  89.3 1.3 collective-permute-start.3
  90.6 4.0 %collective-permute-start = (bf16[16,1,1024]{2,1,0:T(2,128)(2,1)S(1)}, bf16[16,1,1024]{2,1,0:T(2,128)(2,1)S(1)}, u32[]{:S(2)}, u32[]{:S(2)}) collective-permute-start(bf16[16,1,1024]{2,1,0:T(2,128)(2,1)S(1)} %get-tuple-element.30), channel_id=1, source_target_pairs={{0,8},{8,16},{16,24},{24,32},{32,40},{40,48},{48,56},{1,9},{9,17},... | collective-permute-start | bytes 98312 | tf_op jit(solution)/shard_map/ppermute | solution.py:33
  94.9 1.3 collective-permute-start.2
  96.4 4.2 %collective-permute-start.1 = (bf16[1,16,1024]{2,1,0:T(8,128)(2,1)S(1)}, bf16[1,16,1024]{2,1,0:T(8,128)(2,1)S(1)}, u32[]{:S(2)}, u32[]{:S(2)}) collective-permute-start(bf16[1,16,1024]{2,1,0:T(8,128)(2,1)S(1)} %slice.60), channel_id=1, source_target_pairs={{0,64},{64,128},{128,192},{1,65},{65,129},{129,193},{2,66},{66,130... | collective-permute-start | bytes 98312 | tf_op jit(solution)/shard_map/ppermute | solution.py:33
  102.0 1.4 fusion.2
  103.4 1.7 %reshape.261 = f32[4096,64]{1,0:T(8,128)S(1)} reshape(f32[16,16,1024]{2,1,0:T(8,128)} %fusion.2) | data formatting | bytes 2097152 | tf_op jit(solution)/shard_map/reshape | solution.py:226
  105.1 0.9 fusion.45
  106.0 0.7 pad_maximum_fusion.part_ref
  106.7 24.9 %shard_map.76 = f32[64,128]{1,0:T(8,128)} custom-call(f32[64,128]{1,0:T(8,128)} %pad_maximum_fusion.part_ref), custom_call_target="tpu_custom_call" | custom-call | tf_op jit(solution)/shard_map/pallas_call | solution.py:178
  131.6 0.9 fusion.43
  132.7 5.8 %cholesky.16 = f32[64,64]{1,0:T(8,128)S(1)} custom-call(f32[64,64]{1,0:T(8,128)S(1)} %fusion.10), custom_call_target="Cholesky" | custom-call | tf_op jit(solution)/shard_map/jit(cholesky)/cholesky | solution.py:115
  139.9 4.9 %custom-call.6 = f32[1,64,64]{1,2,0:T(8,128)S(1)} custom-call(f32[1,64,64]{2,1,0:T(8,128)S(1)} %fusion.7), custom_call_target="InvertDiagBlocksLowerTriangular" | custom-call | tf_op jit(solution)/shard_map/triangular_solve | solution.py:116
  145.5 2.3 %convolution_convert_fusion = bf16[4096,32]{0,1:T(8,128)(2,1)S(1)} fusion(f32[4096,64]{1,0:T(8,128)S(1)} %reshape.261, f32[64,32]{0,1:T(8,128)S(1)} %fusion.8), kind=kOutput, calls=%fused_computation.3 | convolution fusion | flops 100794368 | bytes 1318912 | tf_op jit(solution)/shard_map/dot_general | solution.py:235
  148.2 1.7 %convert_element_type.37 = bf16[16,16,512]{2,1,0:T(8,128)(2,1)} reshape(bf16[4096,32]{1,0:T(8,128)(2,1)S(1)} %copy.54) | data formatting | bytes 524288 | tf_op jit(solution)/shard_map/convert_element_type | solution.py:238
  150.4 1.7 %convert_element_type.39 = bf16[16,16,512]{2,1,0:T(8,128)(2,1)} reshape(bf16[4096,32]{1,0:T(8,128)(2,1)S(1)} %copy.55) | data formatting | bytes 524288 | tf_op jit(solution)/shard_map/convert_element_type | solution.py:239
  152.4 0.8 fusion.46
  (60 shorter events, 9.2 us)
Async XLA Ops:
  0.6 144.2 %copy-start = (f32[64,32]{0,1:T(8,128)S(1)}, f32[64,32]{0,1:T(8,128)}, u32[]{:S(2)}) copy-start(f32[64,32]{0,1:T(8,128)} %param.7) | copy-start | bytes 24580
  4.4 36.9 %all-to-all-start = ((s32[32,1,1]{2,1,0:T(1,128)}), s32[32,1,1]{2,1,0:T(1,128)S(1)}, u32[]{:S(2)}, u32[]{:S(2)}) async-start(s32[32,1,1]{2,1,0:T(1,128)} %copy.48), calls=%async_computation | async-start | bytes 32768 | tf_op jit(solution)/shard_map/all_to_all | solution.py:213
  41.4 33.9 %all-to-all-start.1 = ((bf16[32,4,4096]{2,1,0:T(4,128)(2,1)}), bf16[32,4,4096]{2,1,0:T(4,128)(2,1)S(1)}, u32[]{:S(2)}, u32[]{:S(2)}) async-start(bf16[32,4,4096]{2,1,0:T(4,128)(2,1)} %broadcast_select_fusion), calls=%async_computation.1 | async-start | bytes 2097152 | tf_op jit(solution)/shard_map/all_to_all | solution.py:212
  76.7 0.8 copy-start.1
  79.0 17.4 %collective-permute-start.4 = (bf16[16,16,64]{2,1,0:T(8,128)(2,1)S(1)}, bf16[16,16,64]{2,1,0:T(8,128)(2,1)S(1)}, u32[]{:S(2)}, u32[]{:S(2)}) collective-permute-start(bf16[16,16,64]{2,1,0:T(8,128)(2,1)S(1)} %get-tuple-element.33), channel_id=1, source_target_pairs={{0,1},{1,2},{2,3},{3,4},{4,5},{5,6},{6,7},{8,9},{9,10},{10,11},{11... | collective-permute-start | bytes 98312 | tf_op jit(solution)/shard_map/ppermute | solution.py:52
  87.4 13.5 %collective-permute-start.5 = (bf16[16,16,64]{2,1,0:T(8,128)(2,1)S(1)}, bf16[16,16,64]{2,1,0:T(8,128)(2,1)S(1)}, u32[]{:S(2)}, u32[]{:S(2)}) collective-permute-start(bf16[16,16,64]{2,1,0:T(8,128)(2,1)S(1)} %get-tuple-element.32), channel_id=1, source_target_pairs={{1,0},{2,1},{3,2},{4,3},{5,4},{6,5},{7,6},{9,8},{10,9},{11,10},{12... | collective-permute-start | bytes 98312 | tf_op jit(solution)/shard_map/ppermute | solution.py:53
  89.3 12.3 %collective-permute-start.3 = (bf16[16,1,1024]{2,1,0:T(2,128)(2,1)S(1)}, bf16[16,1,1024]{2,1,0:T(2,128)(2,1)S(1)}, u32[]{:S(2)}, u32[]{:S(2)}) collective-permute-start(bf16[16,1,1024]{2,1,0:T(2,128)(2,1)S(1)} %get-tuple-element.31), channel_id=1, source_target_pairs={{8,0},{16,8},{24,16},{32,24},{40,32},{48,40},{56,48},{9,1},{17,9},... | collective-permute-start | bytes 98312 | tf_op jit(solution)/shard_map/ppermute | solution.py:34
  90.6 11.0 %collective-permute-start = (bf16[16,1,1024]{2,1,0:T(2,128)(2,1)S(1)}, bf16[16,1,1024]{2,1,0:T(2,128)(2,1)S(1)}, u32[]{:S(2)}, u32[]{:S(2)}) collective-permute-start(bf16[16,1,1024]{2,1,0:T(2,128)(2,1)S(1)} %get-tuple-element.30), channel_id=1, source_target_pairs={{0,8},{8,16},{16,24},{24,32},{32,40},{40,48},{48,56},{1,9},{9,17},... | collective-permute-start | bytes 98312 | tf_op jit(solution)/shard_map/ppermute | solution.py:33
  94.9 6.8 %collective-permute-start.2 = (bf16[1,16,1024]{2,1,0:T(8,128)(2,1)S(1)}, bf16[1,16,1024]{2,1,0:T(8,128)(2,1)S(1)}, u32[]{:S(2)}, u32[]{:S(2)}) collective-permute-start(bf16[1,16,1024]{2,1,0:T(8,128)(2,1)S(1)} %slice.62), channel_id=1, source_target_pairs={{64,0},{128,64},{192,128},{65,1},{129,65},{193,129},{66,2},{130,66... | collective-permute-start | bytes 98312 | tf_op jit(solution)/shard_map/ppermute | solution.py:34
  96.4 5.2 %collective-permute-start.1 = (bf16[1,16,1024]{2,1,0:T(8,128)(2,1)S(1)}, bf16[1,16,1024]{2,1,0:T(8,128)(2,1)S(1)}, u32[]{:S(2)}, u32[]{:S(2)}) collective-permute-start(bf16[1,16,1024]{2,1,0:T(8,128)(2,1)S(1)} %slice.60), channel_id=1, source_target_pairs={{0,64},{64,128},{128,192},{1,65},{65,129},{129,193},{2,66},{66,130... | collective-permute-start | bytes 98312 | tf_op jit(solution)/shard_map/ppermute | solution.py:33
  105.1 39.9 %copy-start.2 = (bf16[64,4096]{1,0:T(8,128)(2,1)S(1)}, bf16[64,4096]{1,0:T(8,128)(2,1)}, u32[]{:S(2)}) copy-start(bf16[64,4096]{1,0:T(8,128)(2,1)} %copy-done.1) | copy-start | bytes 1572868
  132.7 15.5 %copy-start.3 = (f32[64,64]{1,0:T(8,128)}, f32[64,64]{1,0:T(8,128)S(1)}, u32[]{:S(2)}) copy-start(f32[64,64]{1,0:T(8,128)S(1)} %copy.57) | copy-start | bytes 49156

commit v3 on v2

--- a/solution.py
+++ b/solution.py
@@ -187,6 +187,63 @@
     )(part)
 
 
+def exchange_kernel(plane, size_y, payload_ref, ids_ref, out_ref, out_ids_ref, send_sems, recv_sems, local_sems):
+    me = lax.axis_index("gx") * size_y + lax.axis_index("gy")
+    rest = tuple(lax.axis_index(axis) for axis in GZ)
+
+    def device(step):
+        target = lax.rem(me + step, plane)
+        return (target // size_y, lax.rem(target, size_y)) + rest
+
+    barrier = pltpu.get_barrier_semaphore()
+    for step in range(1, plane):
+        pl.semaphore_signal(barrier, inc=1, device_id=device(step), device_id_type=pl.DeviceIdType.MESH)
+    pl.semaphore_wait(barrier, plane - 1)
+    pairs = ((payload_ref, out_ref), (ids_ref, out_ids_ref))
+    copies = []
+    for index, (src, dst) in enumerate(pairs):
+        copy = pltpu.make_async_copy(src.at[me], dst.at[me], local_sems.at[index])
+        copy.start()
+        copies.append(copy)
+    for step in range(1, plane):
+        target = lax.rem(me + step, plane)
+        for index, (src, dst) in enumerate(pairs):
+            slot = 2 * (step - 1) + index
+            copy = pltpu.make_async_remote_copy(
+                src_ref=src.at[target],
+                dst_ref=dst.at[me],
+                send_sem=send_sems.at[slot],
+                recv_sem=recv_sems.at[slot],
+                device_id=device(step),
+                device_id_type=pl.DeviceIdType.MESH,
+            )
+            copy.start()
+            copies.append(copy)
+    for copy in copies:
+        copy.wait()
+
+
+def exchange(payload, ids):
+    size_y = lax.axis_size("gy")
+    plane = lax.axis_size("gx") * size_y
+    vmem = pl.BlockSpec(memory_space=pltpu.VMEM)
+    return pl.pallas_call(
+        functools.partial(exchange_kernel, plane, size_y),
+        out_shape=(
+            jax.ShapeDtypeStruct(payload.shape, payload.dtype),
+            jax.ShapeDtypeStruct(ids.shape, ids.dtype),
+        ),
+        in_specs=[vmem, vmem],
+        out_specs=(vmem, vmem),
+        scratch_shapes=[
+            pltpu.SemaphoreType.DMA((2 * (plane - 1),)),
+            pltpu.SemaphoreType.DMA((2 * (plane - 1),)),
+            pltpu.SemaphoreType.DMA((2,)),
+        ],
+        compiler_params=pltpu.CompilerParams(collective_id=1, has_side_effects=True),
+    )(payload, ids)
+
+
 def shards(patch_fields, slot_snapshot, slot_brick, prior_basis):
     size_x = lax.axis_size("gx")
     size_y = lax.axis_size("gy")
@@ -208,10 +265,9 @@
     source = jnp.sum(jnp.where(slot_hits, slot_ids[:, None], 0), axis=0)
     sent_snapshot = jnp.where(filled, jnp.take(slot_snapshot, source), -1)
     payload = jnp.take(average_cells(patch_fields), source, axis=0)
-    received, received_snapshot = (
-        lax.all_to_all(payload, ("gx", "gy"), split_axis=0, concat_axis=0, tiled=True),
-        lax.all_to_all(sent_snapshot, ("gx", "gy"), split_axis=0, concat_axis=0, tiled=True),
-    )
+    sent_ids = jnp.broadcast_to(sent_snapshot[:, None, None], (slot_count, 8, 128))
+    received, received_ids = exchange(payload, sent_ids)
+    received_snapshot = received_ids[:, 0, 0]
     snapshots = jnp.arange(SNAPS, dtype=jnp.int32)
     chosen = jnp.sum(
         jnp.where(received_snapshot[None, :] == snapshots[:, None], slot_ids[None, :], 0), axis=1

time: 154 us -> 149 us (0.968)
  Pallas kernels: 31.5 us -> 71.2 us
  starting transfers between devices: 42 us -> 17.2 us
  waiting for transfers between devices: 23.7 us -> 0.02 us
  local copies, waits for them, and re-layouts: 29.5 us -> 32 us
  matrix products: 4.97 us -> 6.9 us
    pallas_call x0 -> x1, Pallas kernels: none -> 39.9 us  [exchange(): pl.pallas_call(functools.partial(exchange_kernel, plane, size_y), out_sha...]
    all_to_all x2 -> x0, waiting for transfers between devices: 23.7 us -> none  [the longest x1 23.7 us: shards(): lax.all_to_all(payload, ('gx', 'gy'), split_axis=0, concat_axis=0, tiled=...]
    all_to_all x2 -> x0, starting transfers between devices: 21.1 us -> none  [the longest x1 11.9 us: shards(): lax.all_to_all(sent_snapshot, ('gx', 'gy'), split_axis=0, concat_axis=0,...]
    ppermute x1, starting transfers between devices: 8.2 us -> 4.55 us  [extended_2(): before = lax.ppermute(last, axis, up)]
    dot_general x1, matrix products: 0.43 us -> 2.36 us  [shards(): mode_basis = jnp.dot(data_wide, coeffs, precision=HIGHEST)]
    gather x2 -> x3, local copies, waits for them, and re-layouts: 1.11 us -> 2.81 us  [shards(): arrived = jnp.take(received, chosen, axis=0)]
    slice x0 -> x1, local copies, waits for them, and re-layouts: none -> 1.58 us  [shards(): received_snapshot = received_ids[:, 0, 0]]
  transfers between devices with their start and end apart: 8 -> 6, of which waited for: 1 -> 0; matrix products, arithmetic and copies ran while one was open for 14% -> 2% of each run, Pallas kernels for 4% -> 0%
where the time goes in v3:
time: 149 us; the launch traced here: 148 us
  Pallas kernels  71.2 us (48%)
  local copies, waits for them, and re-layouts  32 us (21%)
  other arithmetic  19.8 us (13%)
  starting transfers between devices  17.2 us (12%)
  matrix products  6.9 us (5%)
    pallas_call x1, Pallas kernels, exchange(): pl.pallas_call(functools.partial(exchange_kernel, plane, size_y), out_sha...  39.9 us
    pallas_call x1, Pallas kernels, allreduce(): pl.pallas_call(functools.partial(allreduce_kernel, sizes), out_shape=jax....  24.8 us
    reshape x1, local copies, waits for them, and re-layouts, average_cells(): flat = fine_data.reshape(rows, PATCH * PATCH * PATCH)  12.7 us
    ppermute x2, starting transfers between devices, extended(): lax.ppermute(last, axis, up)  8.16 us
    pallas_call x1, Pallas kernels, average_cells(): pl.pallas_call(average_kernel, grid=(steps,), in_specs=[pl.BlockSpec((row...  6.58 us
    another operation x3, other arithmetic, factor_basis(): lower_factor = jnp.linalg.cholesky(gram_matrix)  6.52 us
    another operation x2, other arithmetic, factor_basis(): lax.linalg.triangular_solve(lower_factor, prior_basis, left_side=True, lo...  5.55 us
    ppermute x1, starting transfers between devices, extended_2(): before = lax.ppermute(last, axis, up)  4.55 us
  transfers between devices with their start and end apart: 6, of which 0 were waited for; matrix products, arithmetic and copies ran while one was open for 2% of the time, Pallas kernels for 0%

profile of v3, /device:TPU:1, one launch (start us, length us, event | category | flops | bytes accessed | tf_op | source)
XLA Modules:
  0.0 148.2 jit_solution(17894286338242254590)
XLA Ops:
  2.4 12.7 %reshape.233.fine_ref = bf16[128,32768]{1,0:T(8,128)(2,1)} reshape(bf16[32,4,32768]{2,1,0:T(4,128)(2,1)} %param.4) | data formatting | bytes 16777216 | tf_op jit(solution)/shard_map/reshape | solution.py:91
  15.0 1.3 select_convert_fusion.pairing_ref
  16.3 6.6 %shard_map.75 = bf16[128,4096]{1,0:T(8,128)(2,1)} custom-call(bf16[128,32768]{1,0:T(8,128)(2,1)} %reshape.233.fine_ref, bf16[2048,256]{1,0:T(8,128)(2,1)} %select_convert_fusion.pairing_ref), custom_call_target="tpu_custom_call" | custom-call | tf_op jit(solution)/shard_map/pallas_call | solution.py:95
  22.9 1.5 reshape.234
  24.4 0.7 gather_fusion.1
  25.1 1.5 gather_fusion
  26.6 1.6 %broadcast_select_fusion.payload_ref = bf16[32,4,4096]{2,1,0:T(4,128)(2,1)} fusion(bf16[32,4,4096]{2,1,0:T(4,128)(2,1)S(1)} %gather_fusion, pred[32]{0:T(512)(128)(4,1)S(1)} %get-tuple-element.21), kind=kLoop, calls=%fused_computation.17 | loop fusion | flops 524288 | bytes 2097184 | tf_op jit(solution)/shard_map/jit(_take)/select_n | solution.py:267
  28.2 0.8 broadcast_in_dim.99.ids_ref
  28.9 39.9 %shard_map.76 = (bf16[32,4,4096]{2,1,0:T(4,128)(2,1)}, s32[32,8,128]{2,1,0:T(8,128)}) custom-call(bf16[32,4,4096]{2,1,0:T(4,128)(2,1)} %broadcast_select_fusion.payload_ref, s32[32,8,128]{2,1,0:T(8,128)} %broadcast_in_dim.99.ids_ref), custom_call_target="tpu_custom_call" | custom-call | tf_op jit(solution)/shard_map/pallas_call | solution.py:230
  68.8 1.6 %slice_reduce_fusion = s32[32]{0:T(128)S(1)} fusion(s32[32,8,128]{2,1,0:T(8,128)} %get-tuple-element.6), kind=kLoop, calls=%fused_computation.39 | loop fusion | bytes 256 | tf_op jit(solution)/shard_map/slice | solution.py:270
  70.5 2.2 %gather_fusion.2 = bf16[16,4,4096]{2,1,0:T(4,128)(2,1)S(1)} fusion(bf16[32,4,4096]{2,1,0:T(4,128)(2,1)} %get-tuple-element.7, s32[1024]{0:T(1024)S(1)} %pad_clamp_fusion), kind=kCustom, calls=%fused_computation.2 | custom fusion | bytes 1048640 | tf_op jit(solution)/shard_map/jit(_take)/gather | solution.py:275
  73.7 0.7 reshape.235
  74.4 0.7 fusion.43
  75.1 4.6 %collective-permute-start.4 = (bf16[16,16,64]{2,1,0:T(8,128)(2,1)}, bf16[16,16,64]{2,1,0:T(8,128)(2,1)S(1)}, u32[]{:S(2)}, u32[]{:S(2)}) collective-permute-start(bf16[16,16,64]{2,1,0:T(8,128)(2,1)} %get-tuple-element.27), channel_id=1, source_target_pairs={{0,1},{1,2},{2,3},{3,4},{4,5},{5,6},{6,7},{8,9},{9,10},{10,11},{11... | collective-permute-start | bytes 98312 | tf_op jit(solution)/shard_map/ppermute | solution.py:52
  79.7 1.9 %collective-permute-start.5 = (bf16[16,16,64]{2,1,0:T(8,128)(2,1)S(1)}, bf16[16,16,64]{2,1,0:T(8,128)(2,1)S(1)}, u32[]{:S(2)}, u32[]{:S(2)}) collective-permute-start(bf16[16,16,64]{2,1,0:T(8,128)(2,1)S(1)} %get-tuple-element.26), channel_id=1, source_target_pairs={{1,0},{2,1},{3,2},{4,3},{5,4},{6,5},{7,6},{9,8},{10,9},{11,10},{12... | collective-permute-start | bytes 98312 | tf_op jit(solution)/shard_map/ppermute | solution.py:53
  81.6 0.8 fusion.42
  82.4 1.3 collective-permute-start.3
  83.6 4.0 %collective-permute-start = (bf16[16,1,1024]{2,1,0:T(2,128)(2,1)}, bf16[16,1,1024]{2,1,0:T(2,128)(2,1)S(1)}, u32[]{:S(2)}, u32[]{:S(2)}) collective-permute-start(bf16[16,1,1024]{2,1,0:T(2,128)(2,1)} %get-tuple-element.24), channel_id=1, source_target_pairs={{0,8},{8,16},{16,24},{24,32},{32,40},{40,48},{48,56},{1,9},{9,17},... | collective-permute-start | bytes 98312 | tf_op jit(solution)/shard_map/ppermute | solution.py:33
  87.8 1.3 collective-permute-start.2
  89.6 4.2 %collective-permute-start.1 = (bf16[1,16,1024]{2,1,0:T(8,128)(2,1)S(1)}, bf16[1,16,1024]{2,1,0:T(8,128)(2,1)S(1)}, u32[]{:S(2)}, u32[]{:S(2)}) collective-permute-start(bf16[1,16,1024]{2,1,0:T(8,128)(2,1)S(1)} %slice.64), channel_id=1, source_target_pairs={{0,64},{64,128},{128,192},{1,65},{65,129},{129,193},{2,66},{66,130... | collective-permute-start | bytes 98312 | tf_op jit(solution)/shard_map/ppermute | solution.py:33
  95.2 1.5 fusion.2
  96.7 1.7 %reshape.236 = f32[4096,64]{1,0:T(8,128)S(1)} reshape(f32[16,16,1024]{2,1,0:T(8,128)} %fusion.2) | data formatting | bytes 2097152 | tf_op jit(solution)/shard_map/reshape | solution.py:282
  98.4 0.9 fusion.46
  100.0 24.8 %shard_map.77 = f32[64,128]{1,0:T(8,128)} custom-call(f32[64,128]{1,0:T(8,128)} %pad_maximum_fusion.part_ref), custom_call_target="tpu_custom_call" | custom-call | tf_op jit(solution)/shard_map/pallas_call | solution.py:178
  124.8 0.9 fusion.44
  125.9 5.8 %cholesky.16 = f32[64,64]{1,0:T(8,128)S(1)} custom-call(f32[64,64]{1,0:T(8,128)S(1)} %fusion.11), custom_call_target="Cholesky" | custom-call | tf_op jit(solution)/shard_map/jit(cholesky)/cholesky | solution.py:115
  133.1 4.9 %custom-call.6 = f32[1,64,64]{1,2,0:T(8,128)S(1)} custom-call(f32[1,64,64]{2,1,0:T(8,128)S(1)} %fusion.8), custom_call_target="InvertDiagBlocksLowerTriangular" | custom-call | tf_op jit(solution)/shard_map/triangular_solve | solution.py:116
  138.1 2.4 %convolution_convert_fusion.1 = bf16[4096,32]{0,1:T(8,128)(2,1)S(1)} fusion(f32[64,32]{0,1:T(8,128)S(1)} %fusion.9, bf16[64,4096]{0,1:T(8,128)(2,1)} %copy-done.2, pred[64]{0:T(512)(128)(4,1)S(1)} %broadcast_in_dim.105), kind=kOutput, calls=%fused_computation.4 | convolution fusion | flops 101056512 | bytes 794688 | tf_op jit(solution)/shard_map/dot_general | solution.py:290
  140.5 2.3 %convolution_convert_fusion = bf16[4096,32]{0,1:T(8,128)(2,1)S(1)} fusion(f32[4096,64]{1,0:T(8,128)S(1)} %reshape.236, f32[64,32]{0,1:T(8,128)S(1)} %fusion.9), kind=kOutput, calls=%fused_computation.3 | convolution fusion | flops 100794368 | bytes 1318912 | tf_op jit(solution)/shard_map/dot_general | solution.py:291
  143.3 1.7 %convert_element_type.37 = bf16[16,16,512]{2,1,0:T(8,128)(2,1)} reshape(bf16[4096,32]{1,0:T(8,128)(2,1)S(1)} %copy.22) | data formatting | bytes 524288 | tf_op jit(solution)/shard_map/convert_element_type | solution.py:294
  145.5 1.7 %convert_element_type.39 = bf16[16,16,512]{2,1,0:T(8,128)(2,1)} reshape(bf16[4096,32]{1,0:T(8,128)(2,1)S(1)} %copy.23) | data formatting | bytes 524288 | tf_op jit(solution)/shard_map/convert_element_type | solution.py:295
  147.4 0.8 fusion.47
  (54 shorter events, 8.4 us)
Async XLA Ops:
  0.6 137.3 %copy-start = (f32[64,32]{0,1:T(8,128)S(1)}, f32[64,32]{0,1:T(8,128)}, u32[]{:S(2)}) copy-start(f32[64,32]{0,1:T(8,128)} %param.7) | copy-start | bytes 24580
  22.9 1.5 %copy-start.1 = (s32[32]{0:T(128)S(1)}, s32[32]{0:T(128)}, u32[]{:S(2)}) copy-start(s32[32]{0:T(128)} %param.5) | copy-start | bytes 388
  73.4 1.0 copy-start.2
  75.1 14.5 %collective-permute-start.4 = (bf16[16,16,64]{2,1,0:T(8,128)(2,1)}, bf16[16,16,64]{2,1,0:T(8,128)(2,1)S(1)}, u32[]{:S(2)}, u32[]{:S(2)}) collective-permute-start(bf16[16,16,64]{2,1,0:T(8,128)(2,1)} %get-tuple-element.27), channel_id=1, source_target_pairs={{0,1},{1,2},{2,3},{3,4},{4,5},{5,6},{6,7},{8,9},{9,10},{10,11},{11... | collective-permute-start | bytes 98312 | tf_op jit(solution)/shard_map/ppermute | solution.py:52
  79.7 14.4 %collective-permute-start.5 = (bf16[16,16,64]{2,1,0:T(8,128)(2,1)S(1)}, bf16[16,16,64]{2,1,0:T(8,128)(2,1)S(1)}, u32[]{:S(2)}, u32[]{:S(2)}) collective-permute-start(bf16[16,16,64]{2,1,0:T(8,128)(2,1)S(1)} %get-tuple-element.26), channel_id=1, source_target_pairs={{1,0},{2,1},{3,2},{4,3},{5,4},{6,5},{7,6},{9,8},{10,9},{11,10},{12... | collective-permute-start | bytes 98312 | tf_op jit(solution)/shard_map/ppermute | solution.py:53
  82.4 12.5 %collective-permute-start.3 = (bf16[16,1,1024]{2,1,0:T(2,128)(2,1)}, bf16[16,1,1024]{2,1,0:T(2,128)(2,1)S(1)}, u32[]{:S(2)}, u32[]{:S(2)}) collective-permute-start(bf16[16,1,1024]{2,1,0:T(2,128)(2,1)} %get-tuple-element.25), channel_id=1, source_target_pairs={{8,0},{16,8},{24,16},{32,24},{40,32},{48,40},{56,48},{9,1},{17,9},... | collective-permute-start | bytes 98312 | tf_op jit(solution)/shard_map/ppermute | solution.py:34
  83.6 11.2 %collective-permute-start = (bf16[16,1,1024]{2,1,0:T(2,128)(2,1)}, bf16[16,1,1024]{2,1,0:T(2,128)(2,1)S(1)}, u32[]{:S(2)}, u32[]{:S(2)}) collective-permute-start(bf16[16,1,1024]{2,1,0:T(2,128)(2,1)} %get-tuple-element.24), channel_id=1, source_target_pairs={{0,8},{8,16},{16,24},{24,32},{32,40},{40,48},{48,56},{1,9},{9,17},... | collective-permute-start | bytes 98312 | tf_op jit(solution)/shard_map/ppermute | solution.py:33
  87.8 7.1 %collective-permute-start.2 = (bf16[1,16,1024]{2,1,0:T(8,128)(2,1)S(1)}, bf16[1,16,1024]{2,1,0:T(8,128)(2,1)S(1)}, u32[]{:S(2)}, u32[]{:S(2)}) collective-permute-start(bf16[1,16,1024]{2,1,0:T(8,128)(2,1)S(1)} %slice.66), channel_id=1, source_target_pairs={{64,0},{128,64},{192,128},{65,1},{129,65},{193,129},{66,2},{130,66... | collective-permute-start | bytes 98312 | tf_op jit(solution)/shard_map/ppermute | solution.py:34
  89.6 5.2 %collective-permute-start.1 = (bf16[1,16,1024]{2,1,0:T(8,128)(2,1)S(1)}, bf16[1,16,1024]{2,1,0:T(8,128)(2,1)S(1)}, u32[]{:S(2)}, u32[]{:S(2)}) collective-permute-start(bf16[1,16,1024]{2,1,0:T(8,128)(2,1)S(1)} %slice.64), channel_id=1, source_target_pairs={{0,64},{64,128},{128,192},{1,65},{65,129},{129,193},{2,66},{66,130... | collective-permute-start | bytes 98312 | tf_op jit(solution)/shard_map/ppermute | solution.py:33
  125.8 16.9 %copy-start.3 = (f32[64,64]{1,0:T(8,128)}, f32[64,64]{1,0:T(8,128)S(1)}, u32[]{:S(2)}) copy-start(f32[64,64]{1,0:T(8,128)S(1)} %copy.25) | copy-start | bytes 49156

commit v4 on v3

--- a/solution.py
+++ b/solution.py
@@ -74,35 +74,36 @@
 
 
 def average_kernel(fine_ref, pairing_ref, out_ref):
-    rows = fine_ref.shape[0]
+    slots = fine_ref.shape[0]
+    rows = slots * FIELDS
     span = 2 * PATCH * PATCH
     stacked = jnp.concatenate(
-        [fine_ref[:, i * span : (i + 1) * span] for i in range(PAIRS_PER_STEP)], axis=0
+        [fine_ref[:, :, i * span : (i + 1) * span].reshape(rows, span) for i in range(PAIRS_PER_STEP)],
+        axis=0,
     )
     means = jnp.dot(stacked, pairing_ref[...], preferred_element_type=jnp.float32)
     width = EDGE * EDGE
     for i in range(PAIRS_PER_STEP):
-        out_ref[:, i * width : (i + 1) * width] = means[i * rows : (i + 1) * rows].astype(out_ref.dtype)
+        out_ref[:, :, i * width : (i + 1) * width] = (
+            means[i * rows : (i + 1) * rows].reshape(slots, FIELDS, width).astype(out_ref.dtype)
+        )
 
 
 def average_cells(fine_data):
     row_count = fine_data.shape[0]
-    rows = row_count * FIELDS
-    flat = fine_data.reshape(rows, PATCH * PATCH * PATCH)
     span = 2 * PATCH * PATCH * PAIRS_PER_STEP
     width = EDGE * EDGE * PAIRS_PER_STEP
     steps = EDGE // PAIRS_PER_STEP
-    means = pl.pallas_call(
+    return pl.pallas_call(
         average_kernel,
         grid=(steps,),
         in_specs=[
-            pl.BlockSpec((rows, span), lambda g: (0, g)),
+            pl.BlockSpec((row_count, FIELDS, span), lambda g: (0, 0, g)),
             pl.BlockSpec((2 * PATCH * PATCH, EDGE * EDGE), lambda g: (0, 0)),
         ],
-        out_specs=pl.BlockSpec((rows, width), lambda g: (0, g)),
-        out_shape=jax.ShapeDtypeStruct((rows, CELLS), jnp.bfloat16),
-    )(flat, pairing_matrix())
-    return means.reshape(row_count, FIELDS, CELLS)
+        out_specs=pl.BlockSpec((row_count, FIELDS, width), lambda g: (0, 0, g)),
+        out_shape=jax.ShapeDtypeStruct((row_count, FIELDS, CELLS), jnp.bfloat16),
+    )(fine_data, pairing_matrix())
 
 
 def seven_point(center, around_xy, around_z, stride):
@@ -124,38 +125,54 @@
     return values[0]
 
 
-def allreduce_kernel(sizes, part_ref, out_ref, acc, *rest):
-    bufs, (send_sems, recv_sems) = rest[: len(sizes)], rest[len(sizes) :]
-    me = [lax.axis_index(axis) for axis in GX_GY_GZ]
-
-    def peer(dim, step):
-        device = list(me)
-        device[dim] = lax.rem(me[dim] + step, sizes[dim])
-        return tuple(device)
-
+REDUCE_GROUPS = (("gx", "gz_1"), ("gy",), ("gz_0",))
+
+
+def allreduce_kernel(groups, part_ref, out_ref, acc, *rest):
+    bufs, (send_sems, recv_sems) = rest[: len(groups)], rest[len(groups) :]
+    me = {axis: lax.axis_index(axis) for group in groups for axis, _ in group}
+
+    def linear(group):
+        index = 0
+        for axis, size in group:
+            index = index * size + me[axis]
+        return index
+
+    def peer(group, step):
+        count = 1
+        for _, size in group:
+            count *= size
+        target = lax.rem(linear(group) + step, count)
+        device = dict(me)
+        for axis, size in reversed(group):
+            device[axis] = lax.rem(target, size)
+            target = target // size
+        return tuple(device[axis] for axis in GX_GY_GZ)
+
+    counts = []
+    for group in groups:
+        count = 1
+        for _, size in group:
+            count *= size
+        counts.append(count)
     barrier = pltpu.get_barrier_semaphore()
-    count = 0
-    for dim, size in enumerate(sizes):
-        for step in range(1, size):
+    for group, count in zip(groups, counts):
+        for step in range(1, count):
             pl.semaphore_signal(
-                barrier, inc=1, device_id=peer(dim, step), device_id_type=pl.DeviceIdType.MESH
+                barrier, inc=1, device_id=peer(group, step), device_id_type=pl.DeviceIdType.MESH
             )
-            count += 1
-    pl.semaphore_wait(barrier, count)
+    pl.semaphore_wait(barrier, sum(counts) - len(counts))
     acc[...] = part_ref[...]
     slot = 0
-    for dim, size in enumerate(sizes):
-        if size == 1:
-            continue
-        buf = bufs[dim]
+    for group, count, buf in zip(groups, counts, bufs):
         copies = []
-        for step in range(1, size):
+        for step in range(1, count):
             copy = pltpu.make_async_remote_copy(
                 src_ref=acc,
                 dst_ref=buf.at[step - 1],
                 send_sem=send_sems.at[slot],
                 recv_sem=recv_sems.at[slot],
-                device_id=peer(dim, step),
+                device_id=peer(group, step),
                 device_id_type=pl.DeviceIdType.MESH,
             )
             copy.start()
@@ -164,24 +181,28 @@
         for copy in copies:
             copy.wait()
         own = acc[...]
+        mine = linear(group)
         values = []
-        for source in range(size):
-            held = jnp.maximum(lax.rem(me[dim] - source + size, size) - 1, 0)
-            values.append(jnp.where(me[dim] == source, own, buf[held]))
+        for source in range(count):
+            held = jnp.maximum(lax.rem(mine - source + count, count) - 1, 0)
+            values.append(jnp.where(mine == source, own, buf[held]))
         acc[...] = tree_sum(values)
     out_ref[...] = acc[...]
 
 
 def allreduce(part):
-    sizes = tuple(lax.axis_size(axis) for axis in GX_GY_GZ)
-    copies = sum(size - 1 for size in sizes)
+    groups = tuple(
+        tuple((axis, lax.axis_size(axis)) for axis in group) for group in REDUCE_GROUPS
+    )
+    counts = [functools.reduce(lambda a, b: a * b, [size for _, size in group]) for group in groups]
+    copies = sum(count - 1 for count in counts)
     return pl.pallas_call(
-        functools.partial(allreduce_kernel, sizes),
+        functools.partial(allreduce_kernel, groups),
         out_shape=jax.ShapeDtypeStruct(part.shape, part.dtype),
         in_specs=[pl.BlockSpec(memory_space=pltpu.VMEM)],
         out_specs=pl.BlockSpec(memory_space=pltpu.VMEM),
         scratch_shapes=[pltpu.VMEM(part.shape, part.dtype)]
-        + [pltpu.VMEM((max(size - 1, 1),) + part.shape, part.dtype) for size in sizes]
+        + [pltpu.VMEM((max(count - 1, 1),) + part.shape, part.dtype) for count in counts]
         + [pltpu.SemaphoreType.DMA((copies,)), pltpu.SemaphoreType.DMA((copies,))],
         compiler_params=pltpu.CompilerParams(collective_id=0, has_side_effects=True),
     )(part)

time: 149 us -> 137 us (0.919)
  local copies, waits for them, and re-layouts: 32 us -> 19.7 us
    reshape x2 -> x0, local copies, waits for them, and re-layouts: 14.1 us -> none  [the longest x1 12.7 us: average_cells(): flat = fine_data.reshape(rows, PATCH * PATCH * PATCH)]
where the time goes in v4:
time: 137 us
  Pallas kernels  72 us (53%)
  other arithmetic  19.8 us (14%)
  local copies, waits for them, and re-layouts  19.7 us (14%)
  starting transfers between devices  17.2 us (13%)
  matrix products  6.9 us (5%)
    pallas_call x1, Pallas kernels, exchange(): pl.pallas_call(functools.partial(exchange_kernel, plane, size_y), out_sha...  39.9 us
    pallas_call x1, Pallas kernels, allreduce(): pl.pallas_call(functools.partial(allreduce_kernel, groups), out_shape=jax...  25.5 us
    ppermute x2, starting transfers between devices, extended(): lax.ppermute(last, axis, up)  8.16 us
    pallas_call x1, Pallas kernels, average_cells(): pl.pallas_call(average_kernel, grid=(steps,), in_specs=[pl.BlockSpec((row...  6.65 us
    another operation x3, other arithmetic, factor_basis(): lower_factor = jnp.linalg.cholesky(gram_matrix)  6.52 us
    another operation x2, other arithmetic, factor_basis(): lax.linalg.triangular_solve(lower_factor, prior_basis, left_side=True, lo...  5.55 us
    ppermute x1, starting transfers between devices, extended_2(): before = lax.ppermute(last, axis, up)  4.55 us
    gather x3, local copies, waits for them, and re-layouts, shards(): arrived = jnp.take(received, chosen, axis=0)  2.81 us
  transfers between devices with their start and end apart: 6, of which 0 were waited for; matrix products, arithmetic and copies ran while one was open for 2% of the time, Pallas kernels for 0%

profile of v4, /device:TPU:1, one launch (start us, length us, event | category | flops | bytes accessed | tf_op | source)
XLA Modules:
  0.0 136.6 jit_solution(5533924579240549627)
XLA Ops:
  0.7 0.7 compare_select_fusion.8
  2.4 1.2 select_convert_fusion.pairing_ref
  3.6 1.4 gather_fusion.1
  5.0 6.6 %shard_map.75 = bf16[32,4,4096]{2,1,0:T(4,128)(2,1)} custom-call(bf16[32,4,32768]{2,1,0:T(4,128)(2,1)} %fine_ref.1, bf16[2048,256]{1,0:T(8,128)(2,1)} %select_convert_fusion.pairing_ref), custom_call_target="tpu_custom_call" | custom-call | tf_op jit(solution)/shard_map/pallas_call | solution.py:97
  11.6 2.7 %gather_fusion = bf16[32,4,4096]{2,1,0:T(4,128)(2,1)S(1)} fusion(bf16[32,4,4096]{2,1,0:T(4,128)(2,1)} %shard_map.75, s32[1024]{0:T(1024)S(1)} %pad_clamp_fusion.1), kind=kCustom, calls=%fused_computation | custom fusion | bytes 2097280 | tf_op jit(solution)/shard_map/jit(_take)/gather | solution.py:288
  14.3 1.6 %broadcast_select_fusion.payload_ref = bf16[32,4,4096]{2,1,0:T(4,128)(2,1)} fusion(bf16[32,4,4096]{2,1,0:T(4,128)(2,1)S(1)} %gather_fusion, pred[32]{0:T(512)(128)(4,1)S(1)} %get-tuple-element.21), kind=kLoop, calls=%fused_computation.17 | loop fusion | flops 524288 | bytes 2097184 | tf_op jit(solution)/shard_map/jit(_take)/select_n | solution.py:288
  15.9 0.8 broadcast_in_dim.99.ids_ref
  16.6 39.9 %shard_map.76 = (bf16[32,4,4096]{2,1,0:T(4,128)(2,1)}, s32[32,8,128]{2,1,0:T(8,128)}) custom-call(bf16[32,4,4096]{2,1,0:T(4,128)(2,1)} %broadcast_select_fusion.payload_ref, s32[32,8,128]{2,1,0:T(8,128)} %broadcast_in_dim.99.ids_ref), custom_call_target="tpu_custom_call" | custom-call | tf_op jit(solution)/shard_map/pallas_call | solution.py:251
  56.5 1.6 %slice_reduce_fusion = s32[32]{0:T(128)S(1)} fusion(s32[32,8,128]{2,1,0:T(8,128)} %get-tuple-element.6), kind=kLoop, calls=%fused_computation.39 | loop fusion | bytes 256 | tf_op jit(solution)/shard_map/slice | solution.py:291
  58.3 2.2 %gather_fusion.2 = bf16[16,4,4096]{2,1,0:T(4,128)(2,1)S(1)} fusion(bf16[32,4,4096]{2,1,0:T(4,128)(2,1)} %get-tuple-element.7, s32[1024]{0:T(1024)S(1)} %pad_clamp_fusion), kind=kCustom, calls=%fused_computation.2 | custom fusion | bytes 1048640 | tf_op jit(solution)/shard_map/jit(_take)/gather | solution.py:296
  61.4 0.7 reshape.227
  62.1 0.7 fusion.43
  62.8 4.5 %collective-permute-start.4 = (bf16[16,16,64]{2,1,0:T(8,128)(2,1)}, bf16[16,16,64]{2,1,0:T(8,128)(2,1)S(1)}, u32[]{:S(2)}, u32[]{:S(2)}) collective-permute-start(bf16[16,16,64]{2,1,0:T(8,128)(2,1)} %get-tuple-element.27), channel_id=1, source_target_pairs={{0,1},{1,2},{2,3},{3,4},{4,5},{5,6},{6,7},{8,9},{9,10},{10,11},{11... | collective-permute-start | bytes 98312 | tf_op jit(solution)/shard_map/ppermute | solution.py:52
  67.4 1.9 %collective-permute-start.5 = (bf16[16,16,64]{2,1,0:T(8,128)(2,1)S(1)}, bf16[16,16,64]{2,1,0:T(8,128)(2,1)S(1)}, u32[]{:S(2)}, u32[]{:S(2)}) collective-permute-start(bf16[16,16,64]{2,1,0:T(8,128)(2,1)S(1)} %get-tuple-element.26), channel_id=1, source_target_pairs={{1,0},{2,1},{3,2},{4,3},{5,4},{6,5},{7,6},{9,8},{10,9},{11,10},{12... | collective-permute-start | bytes 98312 | tf_op jit(solution)/shard_map/ppermute | solution.py:53
  69.3 0.8 fusion.42
  70.1 1.3 collective-permute-start.3
  71.4 4.0 %collective-permute-start = (bf16[16,1,1024]{2,1,0:T(2,128)(2,1)}, bf16[16,1,1024]{2,1,0:T(2,128)(2,1)S(1)}, u32[]{:S(2)}, u32[]{:S(2)}) collective-permute-start(bf16[16,1,1024]{2,1,0:T(2,128)(2,1)} %get-tuple-element.24), channel_id=1, source_target_pairs={{0,8},{8,16},{16,24},{24,32},{32,40},{40,48},{48,56},{1,9},{9,17},... | collective-permute-start | bytes 98312 | tf_op jit(solution)/shard_map/ppermute | solution.py:33
  75.5 1.3 collective-permute-start.2
  77.4 4.2 %collective-permute-start.1 = (bf16[1,16,1024]{2,1,0:T(8,128)(2,1)S(1)}, bf16[1,16,1024]{2,1,0:T(8,128)(2,1)S(1)}, u32[]{:S(2)}, u32[]{:S(2)}) collective-permute-start(bf16[1,16,1024]{2,1,0:T(8,128)(2,1)S(1)} %slice.64), channel_id=1, source_target_pairs={{0,64},{64,128},{128,192},{1,65},{65,129},{129,193},{2,66},{66,130... | collective-permute-start | bytes 98312 | tf_op jit(solution)/shard_map/ppermute | solution.py:33
  83.0 1.5 %fusion.2 = f32[16,16,1024]{2,1,0:T(8,128)} fusion(f32[16,16,1152]{2,1,0:T(8,128)S(1)} %convert_element_type.34, f32[18,18,1024]{2,1,0:T(8,128)S(1)} %fusion.5, bf16[16,16,1024]{2,1,0:T(8,128)(2,1)S(1)} %reshape.227), kind=kLoop, calls=%fused_computation.12 | loop fusion | flops 2097152 | bytes 7864320 | tf_op jit(solution)/shard_map/sub | solution.py:112
  84.4 1.7 %reshape.228 = f32[4096,64]{1,0:T(8,128)S(1)} reshape(f32[16,16,1024]{2,1,0:T(8,128)} %fusion.2) | data formatting | bytes 2097152 | tf_op jit(solution)/shard_map/reshape | solution.py:303
  86.1 0.9 fusion.46
  87.0 0.7 pad_maximum_fusion.part_ref
  87.7 25.5 %shard_map.77 = f32[64,128]{1,0:T(8,128)} custom-call(f32[64,128]{1,0:T(8,128)} %pad_maximum_fusion.part_ref), custom_call_target="tpu_custom_call" | custom-call | tf_op jit(solution)/shard_map/pallas_call | solution.py:199
  113.2 0.9 fusion.44
  114.3 5.8 %cholesky.16 = f32[64,64]{1,0:T(8,128)S(1)} custom-call(f32[64,64]{1,0:T(8,128)S(1)} %fusion.11), custom_call_target="Cholesky" | custom-call | tf_op jit(solution)/shard_map/jit(cholesky)/cholesky | solution.py:116
  121.5 4.9 %custom-call.6 = f32[1,64,64]{1,2,0:T(8,128)S(1)} custom-call(f32[1,64,64]{2,1,0:T(8,128)S(1)} %fusion.8), custom_call_target="InvertDiagBlocksLowerTriangular" | custom-call | tf_op jit(solution)/shard_map/triangular_solve | solution.py:117
  126.6 2.4 %convolution_convert_fusion.1 = bf16[4096,32]{0,1:T(8,128)(2,1)S(1)} fusion(f32[64,32]{0,1:T(8,128)S(1)} %fusion.9, bf16[64,4096]{0,1:T(8,128)(2,1)} %copy-done.1, pred[64]{0:T(512)(128)(4,1)S(1)} %broadcast_in_dim.105), kind=kOutput, calls=%fused_computation.4 | convolution fusion | flops 101056512 | bytes 794688 | tf_op jit(solution)/shard_map/dot_general | solution.py:311
  128.9 2.3 %convolution_convert_fusion = bf16[4096,32]{0,1:T(8,128)(2,1)S(1)} fusion(f32[4096,64]{1,0:T(8,128)S(1)} %reshape.228, f32[64,32]{0,1:T(8,128)S(1)} %fusion.9), kind=kOutput, calls=%fused_computation.3 | convolution fusion | flops 100794368 | bytes 1318912 | tf_op jit(solution)/shard_map/dot_general | solution.py:312
  131.7 1.7 %convert_element_type.37 = bf16[16,16,512]{2,1,0:T(8,128)(2,1)} reshape(bf16[4096,32]{1,0:T(8,128)(2,1)S(1)} %copy.22) | data formatting | bytes 524288 | tf_op jit(solution)/shard_map/convert_element_type | solution.py:315
  133.9 1.7 %convert_element_type.39 = bf16[16,16,512]{2,1,0:T(8,128)(2,1)} reshape(bf16[4096,32]{1,0:T(8,128)(2,1)S(1)} %copy.23) | data formatting | bytes 524288 | tf_op jit(solution)/shard_map/convert_element_type | solution.py:316
  135.9 0.8 fusion.47
  (50 shorter events, 7.0 us)
Async XLA Ops:
  0.6 125.8 %copy-start = (f32[64,32]{0,1:T(8,128)S(1)}, f32[64,32]{0,1:T(8,128)}, u32[]{:S(2)}) copy-start(f32[64,32]{0,1:T(8,128)} %param.7) | copy-start | bytes 24580
  61.1 1.0 copy-start.1
  62.8 14.5 %collective-permute-start.4 = (bf16[16,16,64]{2,1,0:T(8,128)(2,1)}, bf16[16,16,64]{2,1,0:T(8,128)(2,1)S(1)}, u32[]{:S(2)}, u32[]{:S(2)}) collective-permute-start(bf16[16,16,64]{2,1,0:T(8,128)(2,1)} %get-tuple-element.27), channel_id=1, source_target_pairs={{0,1},{1,2},{2,3},{3,4},{4,5},{5,6},{6,7},{8,9},{9,10},{10,11},{11... | collective-permute-start | bytes 98312 | tf_op jit(solution)/shard_map/ppermute | solution.py:52
  67.4 14.4 %collective-permute-start.5 = (bf16[16,16,64]{2,1,0:T(8,128)(2,1)S(1)}, bf16[16,16,64]{2,1,0:T(8,128)(2,1)S(1)}, u32[]{:S(2)}, u32[]{:S(2)}) collective-permute-start(bf16[16,16,64]{2,1,0:T(8,128)(2,1)S(1)} %get-tuple-element.26), channel_id=1, source_target_pairs={{1,0},{2,1},{3,2},{4,3},{5,4},{6,5},{7,6},{9,8},{10,9},{11,10},{12... | collective-permute-start | bytes 98312 | tf_op jit(solution)/shard_map/ppermute | solution.py:53
  70.1 12.5 %collective-permute-start.3 = (bf16[16,1,1024]{2,1,0:T(2,128)(2,1)}, bf16[16,1,1024]{2,1,0:T(2,128)(2,1)S(1)}, u32[]{:S(2)}, u32[]{:S(2)}) collective-permute-start(bf16[16,1,1024]{2,1,0:T(2,128)(2,1)} %get-tuple-element.25), channel_id=1, source_target_pairs={{8,0},{16,8},{24,16},{32,24},{40,32},{48,40},{56,48},{9,1},{17,9},... | collective-permute-start | bytes 98312 | tf_op jit(solution)/shard_map/ppermute | solution.py:34
  71.4 11.2 %collective-permute-start = (bf16[16,1,1024]{2,1,0:T(2,128)(2,1)}, bf16[16,1,1024]{2,1,0:T(2,128)(2,1)S(1)}, u32[]{:S(2)}, u32[]{:S(2)}) collective-permute-start(bf16[16,1,1024]{2,1,0:T(2,128)(2,1)} %get-tuple-element.24), channel_id=1, source_target_pairs={{0,8},{8,16},{16,24},{24,32},{32,40},{40,48},{48,56},{1,9},{9,17},... | collective-permute-start | bytes 98312 | tf_op jit(solution)/shard_map/ppermute | solution.py:33
  75.5 7.1 %collective-permute-start.2 = (bf16[1,16,1024]{2,1,0:T(8,128)(2,1)S(1)}, bf16[1,16,1024]{2,1,0:T(8,128)(2,1)S(1)}, u32[]{:S(2)}, u32[]{:S(2)}) collective-permute-start(bf16[1,16,1024]{2,1,0:T(8,128)(2,1)S(1)} %slice.66), channel_id=1, source_target_pairs={{64,0},{128,64},{192,128},{65,1},{129,65},{193,129},{66,2},{130,66... | collective-permute-start | bytes 98312 | tf_op jit(solution)/shard_map/ppermute | solution.py:34
  77.4 5.2 %collective-permute-start.1 = (bf16[1,16,1024]{2,1,0:T(8,128)(2,1)S(1)}, bf16[1,16,1024]{2,1,0:T(8,128)(2,1)S(1)}, u32[]{:S(2)}, u32[]{:S(2)}) collective-permute-start(bf16[1,16,1024]{2,1,0:T(8,128)(2,1)S(1)} %slice.64), channel_id=1, source_target_pairs={{0,64},{64,128},{128,192},{1,65},{65,129},{129,193},{2,66},{66,130... | collective-permute-start | bytes 98312 | tf_op jit(solution)/shard_map/ppermute | solution.py:33
  114.3 17.0 %copy-start.2 = (f32[64,64]{1,0:T(8,128)}, f32[64,64]{1,0:T(8,128)S(1)}, u32[]{:S(2)}) copy-start(f32[64,64]{1,0:T(8,128)S(1)} %copy.25) | copy-start | bytes 49156

commit v5 on v4

--- a/solution.py
+++ b/solution.py
@@ -265,6 +265,87 @@
     )(payload, ids)
 
 
+def halo_kernel(sizes, faces_ref, out_ref, send_sems, recv_sems):
+    me = [lax.axis_index(axis) for axis in GX_GY_GZ]
+    size_z1 = sizes[3]
+    size_z = sizes[2] * size_z1
+
+    def device(dim, step):
+        if dim < 2:
+            place = list(me)
+            place[dim] = lax.rem(me[dim] + step + sizes[dim], sizes[dim])
+            return tuple(place)
+        z = lax.rem(me[2] * size_z1 + me[3] + step + size_z, size_z)
+        return (me[0], me[1], z // size_z1, lax.rem(z, size_z1))
+
+    targets = [device(dim, step) for dim in range(3) for step in (-1, 1)]
+    barrier = pltpu.get_barrier_semaphore()
+    for target in targets:
+        pl.semaphore_signal(barrier, inc=1, device_id=target, device_id_type=pl.DeviceIdType.MESH)
+    pl.semaphore_wait(barrier, len(targets))
+    copies = []
+    for index, target in enumerate(targets):
+        copy = pltpu.make_async_remote_copy(
+            src_ref=faces_ref.at[index],
+            dst_ref=out_ref.at[index],
+            send_sem=send_sems.at[index],
+            recv_sem=recv_sems.at[index],
+            device_id=target,
+            device_id_type=pl.DeviceIdType.MESH,
+        )
+        copy.start()
+        copies.append(copy)
+    for copy in copies:
+        copy.wait()
+
+
+def halo(faces):
+    sizes = tuple(lax.axis_size(axis) for axis in GX_GY_GZ)
+    vmem = pl.BlockSpec(memory_space=pltpu.VMEM)
+    return pl.pallas_call(
+        functools.partial(halo_kernel, sizes),
+        out_shape=jax.ShapeDtypeStruct(faces.shape, faces.dtype),
+        in_specs=[vmem],
+        out_specs=vmem,
+        scratch_shapes=[
+            pltpu.SemaphoreType.DMA((faces.shape[0],)),
+            pltpu.SemaphoreType.DMA((faces.shape[0],)),
+        ],
+        compiler_params=pltpu.CompilerParams(collective_id=2, has_side_effects=True),
+    )(faces)
+
+
+def diffusion(data_block):
+    edge = data_block.shape[0]
+    cells = edge * COLS
+    faces = jnp.stack(
+        [
+            data_block[0],
+            data_block[-1],
+            data_block[:, 0],
+            data_block[:, -1],
+            data_block[:, :, :COLS].reshape(edge, cells),
+            data_block[:, :, -COLS:].reshape(edge, cells),
+        ]
+    )
+    got = halo(faces).astype(jnp.float32)
+    gx, gy, gz = lax.axis_index("gx"), lax.axis_index("gy"), lax.axis_index(GZ)
+    last = (lax.axis_size("gx") - 1, lax.axis_size("gy") - 1, lax.axis_size(GZ) - 1)
+    above_x = jnp.where(gx < last[0], got[0], 0.0)
+    below_x = jnp.where(gx > 0, got[1], 0.0)
+    above_y = jnp.where(gy < last[1], got[2], 0.0)
+    below_y = jnp.where(gy > 0, got[3], 0.0)
+    above_z = jnp.where(gz < last[2], got[4], 0.0).reshape(edge, edge, COLS)
+    below_z = jnp.where(gz > 0, got[5], 0.0).reshape(edge, edge, COLS)
+    center = data_block.astype(jnp.float32)
+    along_x = jnp.concatenate([below_x[None], center, above_x[None]], axis=0)
+    along_y = jnp.concatenate([below_y[:, None], center, above_y[:, None]], axis=1)
+    along_z = jnp.concatenate([below_z, center, above_z], axis=2)
+    total = along_x[2:] + along_x[:-2] + along_y[:, 2:] + along_y[:, :-2]
+    total = total + along_z[:, :, 2 * COLS :] + along_z[:, :, : -2 * COLS]
+    return total - 6.0 * center
+
+
 def shards(patch_fields, slot_snapshot, slot_brick, prior_basis):
     size_x = lax.axis_size("gx")
     size_y = lax.axis_size("gy")
@@ -284,8 +365,8 @@
     slot_hits = position[:, None] == slot_ids[None, :]
     filled = jnp.any(slot_hits, axis=0)
     source = jnp.sum(jnp.where(slot_hits, slot_ids[:, None], 0), axis=0)
-    sent_snapshot = jnp.where(filled, jnp.take(slot_snapshot, source), -1)
-    payload = jnp.take(average_cells(patch_fields), source, axis=0)
+    sent_snapshot = jnp.where(filled, jnp.take(slot_snapshot, source, mode="clip"), -1)
+    payload = jnp.take(average_cells(patch_fields), source, axis=0, mode="clip")
     sent_ids = jnp.broadcast_to(sent_snapshot[:, None, None], (slot_count, 8, 128))
     received, received_ids = exchange(payload, sent_ids)
     received_snapshot = received_ids[:, 0, 0]
@@ -293,16 +374,12 @@
     chosen = jnp.sum(
         jnp.where(received_snapshot[None, :] == snapshots[:, None], slot_ids[None, :], 0), axis=1
     )
-    arrived = jnp.take(received, chosen, axis=0)
+    arrived = jnp.take(received, chosen, axis=0, mode="clip")
     columns = arrived.reshape(COLS, CELLS)
     partial_gram = jnp.dot(columns, columns.T, preferred_element_type=jnp.float32)
     data_wide = columns.astype(jnp.float32).T
     data_block = columns.T.reshape(EDGE, EDGE, EDGE * COLS)
-    data_xy = extended(data_block, (("gx", 0), ("gy", 1)), 1).astype(jnp.float32)
-    data_z = extended_2(data_block, ((GZ, 2),), COLS).astype(jnp.float32)
-    data_image = seven_point(data_block.astype(jnp.float32), data_xy, data_z, COLS).reshape(
-        CELLS, COLS
-    )
+    data_image = diffusion(data_block).reshape(CELLS, COLS)
     partial_cross = jnp.dot(data_wide.T, data_image, precision=HIGHEST)
     totals = allreduce(jnp.concatenate([partial_gram, partial_cross], axis=1))
     gram_total, cross_total = totals[:, :COLS], totals[:, COLS:]

time: 137 us -> 123 us (0.90)
  starting transfers between devices: 17.2 us -> 0 us
  Pallas kernels: 72 us -> 77.7 us
  matrix products: 6.9 us -> 4.9 us
    ppermute x6 -> x0, starting transfers between devices: 17.2 us -> none  [the longest x2 8.16 us: extended(): lax.ppermute(last, axis, up)]
    pallas_call x0 -> x1, Pallas kernels: none -> 8.22 us  [halo(): pl.pallas_call(functools.partial(halo_kernel, sizes), out_shape=jax.Shape...]
    pallas_call x1, Pallas kernels: 25.5 us -> 23 us  [allreduce(): pl.pallas_call(functools.partial(allreduce_kernel, groups), out_shape=jax...]
    dot_general x1, matrix products: 2.36 us -> 0.36 us  [shards(): mode_basis = jnp.dot(data_wide, coeffs, precision=HIGHEST)]
    select_n x5 -> x2, other arithmetic: 1.89 us -> 0.04 us  [the longest x1 0.03 us: diffusion(): above_x = jnp.where(gx < last[0], got[0], 0.0)]
    gather x5 -> x3, local copies, waits for them, and re-layouts: 6.83 us -> 7.17 us  [the longest x1 3.59 us: shards(): payload = jnp.take(average_cells(patch_fields), source, axis=0, mode='clip')]
  transfers between devices with their start and end apart: 6 -> 0, of which waited for: 0 -> 0; matrix products, arithmetic and copies ran while one was open for 2% -> 0% of each run, Pallas kernels for 0% -> 0%
where the time goes in v5:
time: 123 us; the launch traced here: 122 us
  Pallas kernels  77.7 us (63%)
  local copies, waits for them, and re-layouts  19.9 us (16%)
  other arithmetic  18.6 us (15%)
  matrix products  4.9 us (4%)
    pallas_call x1, Pallas kernels, exchange(): pl.pallas_call(functools.partial(exchange_kernel, plane, size_y), out_sha...  39.9 us
    pallas_call x1, Pallas kernels, allreduce(): pl.pallas_call(functools.partial(allreduce_kernel, groups), out_shape=jax...  23 us
    pallas_call x1, Pallas kernels, halo(): pl.pallas_call(functools.partial(halo_kernel, sizes), out_shape=jax.Shape...  8.22 us
    pallas_call x1, Pallas kernels, average_cells(): pl.pallas_call(average_kernel, grid=(steps,), in_specs=[pl.BlockSpec((row...  6.64 us
    another operation x3, other arithmetic, factor_basis(): lower_factor = jnp.linalg.cholesky(gram_matrix)  6.52 us
    another operation x2, other arithmetic, factor_basis(): lax.linalg.triangular_solve(lower_factor, prior_basis, left_side=True, lo...  5.55 us
    gather x1, local copies, waits for them, and re-layouts, shards(): payload = jnp.take(average_cells(patch_fields), source, axis=0, mode='clip')  3.59 us

profile of v5, /device:TPU:1, one launch (start us, length us, event | category | flops | bytes accessed | tf_op | source)
XLA Modules:
  0.0 122.1 jit_solution(16607176654892874225)
XLA Ops:
  0.6 0.7 compare_select_fusion.4
  1.5 0.7 compare_select_fusion.3
  2.3 1.4 %gather_fusion.1 = s32[32]{0:T(128)S(1)} fusion(s32[32]{0:T(128)} %param.5, s32[1024]{0:T(1024)S(1)} %pad_clamp_fusion.1), kind=kCustom, calls=%fused_computation.1 | custom fusion | bytes 384 | tf_op jit(solution)/shard_map/jit(_take)/gather | solution.py:368
  3.7 0.8 broadcast_in_dim.83.ids_ref
  4.5 1.2 %select_convert_fusion.pairing_ref = bf16[2048,256]{1,0:T(8,128)(2,1)} fusion(s32[2048]{0:T(1024)S(1)} %fusion.32), kind=kLoop, calls=%fused_computation.5 | loop fusion | flops 1572864 | bytes 1056768 | tf_op jit(solution)/shard_map/convert_element_type | solution.py:70
  5.8 6.6 %shard_map.75 = bf16[32,4,4096]{2,1,0:T(4,128)(2,1)} custom-call(bf16[32,4,32768]{2,1,0:T(4,128)(2,1)} %fine_ref.1, bf16[2048,256]{1,0:T(8,128)(2,1)} %select_convert_fusion.pairing_ref), custom_call_target="tpu_custom_call" | custom-call | tf_op jit(solution)/shard_map/pallas_call | solution.py:97
  12.4 3.6 %gather_fusion = bf16[32,4,4096]{2,1,0:T(4,128)(2,1)} fusion(bf16[32,4,4096]{2,1,0:T(4,128)(2,1)} %shard_map.75, s32[1024]{0:T(1024)S(1)} %pad_clamp_fusion.1), kind=kCustom, calls=%fused_computation | custom fusion | bytes 2097280 | tf_op jit(solution)/shard_map/jit(_take)/gather | solution.py:369
  16.0 39.9 %shard_map.76 = (bf16[32,4,4096]{2,1,0:T(4,128)(2,1)}, s32[32,8,128]{2,1,0:T(8,128)}) custom-call(bf16[32,4,4096]{2,1,0:T(4,128)(2,1)} %gather_fusion, s32[32,8,128]{2,1,0:T(8,128)} %broadcast_in_dim.83.ids_ref), custom_call_target="tpu_custom_call" | custom-call | tf_op jit(solution)/shard_map/pallas_call | solution.py:251
  55.9 1.6 %slice_reduce_fusion = s32[32]{0:T(128)S(1)} fusion(s32[32,8,128]{2,1,0:T(8,128)} %get-tuple-element.7), kind=kLoop, calls=%fused_computation.45 | loop fusion | bytes 256 | tf_op jit(solution)/shard_map/slice | solution.py:372
  57.6 2.2 %gather_fusion.2 = bf16[16,4,4096]{2,1,0:T(4,128)(2,1)S(1)} fusion(bf16[32,4,4096]{2,1,0:T(4,128)(2,1)} %get-tuple-element.6, s32[1024]{0:T(1024)S(1)} %pad_clamp_fusion), kind=kCustom, calls=%fused_computation.2 | custom fusion | bytes 1048640 | tf_op jit(solution)/shard_map/jit(_take)/gather | solution.py:377
  59.9 0.5 copy.28
  60.7 0.7 reshape.141
  61.9 0.7 copy-done.1
  62.6 8.2 %shard_map.77 = bf16[6,16,1024]{2,1,0:T(8,128)(2,1)} custom-call(bf16[6,16,1024]{2,1,0:T(8,128)(2,1)} %copy-done.1), custom_call_target="tpu_custom_call" | custom-call | tf_op jit(solution)/shard_map/pallas_call | solution.py:305
  70.8 1.0 convert_element_type.28
  72.3 1.6 %fusion.1 = f32[16,16,1024]{2,1,0:T(8,128)} fusion(f32[16,16,1024]{2,1,0:T(8,128)S(1)} %convert_element_type.27, f32[16,16,64]{2,1,0:T(8,128)S(1)} %select_n.172, f32[16,16,64]{2,1,0:T(8,128)S(1)} %select_n.169, f32[16,1,1024]{2,1,0:T(1,128)S(1)} %copy.32, f32[16,1,1024]{2,1,0:T(1,128)S(1)} %copy.31, f32[1,16,1024]{2,1,0:T(8,128)S(1)} %get-tuple-element.31, ...), kind=kLoop, calls=%fused_computation.9 | loop fusion | flops 3407872 | bytes 2490368 | tf_op jit(solution)/shard_map/sub | solution.py:346
  73.9 1.9 %reshape.142 = f32[4096,64]{1,0:T(8,128)S(1)} reshape(f32[16,16,1024]{2,1,0:T(8,128)} %fusion.1) | data formatting | bytes 2097152 | tf_op jit(solution)/shard_map/reshape | solution.py:382
  75.8 0.9 fusion.45
  77.0 0.7 pad_maximum_fusion.6.part_ref
  77.7 23.0 %shard_map.78 = f32[64,128]{1,0:T(8,128)} custom-call(f32[64,128]{1,0:T(8,128)} %pad_maximum_fusion.6.part_ref), custom_call_target="tpu_custom_call" | custom-call | tf_op jit(solution)/shard_map/pallas_call | solution.py:199
  100.7 0.9 fusion.43
  101.8 5.8 %cholesky.16 = f32[64,64]{1,0:T(8,128)S(1)} custom-call(f32[64,64]{1,0:T(8,128)S(1)} %fusion.13), custom_call_target="Cholesky" | custom-call | tf_op jit(solution)/shard_map/jit(cholesky)/cholesky | solution.py:116
  107.7 0.6 compare_reduce_fusion
  108.3 0.7 fusion.8
  109.0 4.9 %custom-call.6 = f32[1,64,64]{1,2,0:T(8,128)S(1)} custom-call(f32[1,64,64]{2,1,0:T(8,128)S(1)} %fusion.8), custom_call_target="InvertDiagBlocksLowerTriangular" | custom-call | tf_op jit(solution)/shard_map/triangular_solve | solution.py:117
  114.3 0.8 fusion.46
  115.1 2.3 %convolution_convert_fusion = bf16[4096,32]{0,1:T(8,128)(2,1)S(1)} fusion(f32[4096,64]{1,0:T(8,128)S(1)} %reshape.142, f32[64,32]{0,1:T(8,128)S(1)} %fusion.11), kind=kOutput, calls=%fused_computation.3 | convolution fusion | flops 100794368 | bytes 1318912 | tf_op jit(solution)/shard_map/dot_general | solution.py:389
  117.4 0.5 copy.36
  117.9 1.7 %convert_element_type.32 = bf16[16,16,512]{2,1,0:T(8,128)(2,1)} reshape(bf16[4096,32]{1,0:T(8,128)(2,1)S(1)} %copy.36) | data formatting | bytes 524288 | tf_op jit(solution)/shard_map/convert_element_type | solution.py:393
  119.6 0.4 convolution_convert_fusion.1
  119.9 0.5 copy.35
  120.4 1.7 %convert_element_type.30 = bf16[16,16,512]{2,1,0:T(8,128)(2,1)} reshape(bf16[4096,32]{1,0:T(8,128)(2,1)S(1)} %copy.35) | data formatting | bytes 524288 | tf_op jit(solution)/shard_map/convert_element_type | solution.py:392
  (42 shorter events, 2.7 us)
Async XLA Ops:
  0.6 113.3 %copy-start = (f32[64,32]{0,1:T(8,128)S(1)}, f32[64,32]{0,1:T(8,128)}, u32[]{:S(2)}) copy-start(f32[64,32]{0,1:T(8,128)} %param.7) | copy-start | bytes 24580
  61.9 0.7 copy-start.1
  101.8 17.8 %copy-start.2 = (f32[64,64]{1,0:T(8,128)}, f32[64,64]{1,0:T(8,128)S(1)}, u32[]{:S(2)}) copy-start(f32[64,64]{1,0:T(8,128)S(1)} %copy.38) | copy-start | bytes 49156

commit v6 on v5

--- a/solution.py
+++ b/solution.py
@@ -112,11 +112,36 @@
     return total - 6.0 * center
 
 
+def factor_kernel(gram_ref, prior_ref, out_ref):
+    size = gram_ref.shape[0]
+    rows = lax.broadcasted_iota(jnp.int32, (size, size), 0)
+    cols = lax.broadcasted_iota(jnp.int32, (size, size), 1)
+    work = gram_ref[...]
+    upper = jnp.zeros_like(work)
+    for j in range(size):
+        pivot = jnp.sqrt(work[j : j + 1, j : j + 1])
+        column = jnp.where(rows[:, j : j + 1] >= j, work[:, j : j + 1] / pivot, 0.0)
+        row = jnp.sum(jnp.where(rows == cols, column, 0.0), axis=0, keepdims=True)
+        upper = jnp.where(rows == j, row, upper)
+        work = work - column * row
+    solved = prior_ref[...]
+    result = jnp.zeros_like(solved)
+    picks = lax.broadcasted_iota(jnp.int32, solved.shape, 0)
+    for i in reversed(range(size)):
+        value = solved[i : i + 1, :] / upper[i : i + 1, i : i + 1]
+        result = jnp.where(picks == i, value, result)
+        solved = solved - upper[:, i : i + 1] * value
+    out_ref[...] = result
+
+
 def factor_basis(gram_matrix, prior_basis):
-    lower_factor = jnp.linalg.cholesky(gram_matrix)
-    return lax.linalg.triangular_solve(
-        lower_factor, prior_basis, left_side=True, lower=True, transpose_a=True
-    )
+    vmem = pl.BlockSpec(memory_space=pltpu.VMEM)
+    return pl.pallas_call(
+        factor_kernel,
+        out_shape=jax.ShapeDtypeStruct(prior_basis.shape, prior_basis.dtype),
+        in_specs=[vmem, vmem],
+        out_specs=vmem,
+    )(gram_matrix, prior_basis)
 
 
 def tree_sum(values):
@@ -379,18 +404,25 @@
     partial_gram = jnp.dot(columns, columns.T, preferred_element_type=jnp.float32)
     data_wide = columns.astype(jnp.float32).T
     data_block = columns.T.reshape(EDGE, EDGE, EDGE * COLS)
-    data_image = diffusion(data_block).reshape(CELLS, COLS)
+    data_block_image = diffusion(data_block)
+    data_image = data_block_image.reshape(CELLS, COLS)
     partial_cross = jnp.dot(data_wide.T, data_image, precision=HIGHEST)
     totals = allreduce(jnp.concatenate([partial_gram, partial_cross], axis=1))
     gram_total, cross_total = totals[:, :COLS], totals[:, COLS:]
     gram_matrix = gram_total / total_cells
     coeffs = factor_basis(gram_matrix, prior_basis)
-    mode_basis = jnp.dot(data_wide, coeffs, precision=HIGHEST)
-    mode_image = jnp.dot(data_image, coeffs, precision=HIGHEST)
     inner = jnp.dot(cross_total / total_cells, coeffs, precision=HIGHEST)
     reduced = jnp.dot(coeffs.T, inner, precision=HIGHEST)
-    mode_fields = mode_basis.reshape(EDGE, EDGE, EDGE * MODES).astype(jnp.bfloat16)
-    diffused = mode_image.reshape(EDGE, EDGE, EDGE * MODES).astype(jnp.bfloat16)
+    depth = data_block.shape[2] // COLS
+    per_cell = jnp.eye(depth, dtype=jnp.float32)[:, None, :, None] * coeffs[None, :, None, :]
+    per_cell = per_cell.reshape(depth * COLS, depth * MODES)
+    plane = data_block.shape[0] * data_block.shape[1]
+    mode_fields = jnp.dot(
+        data_block.reshape(plane, depth * COLS).astype(jnp.float32), per_cell, precision=HIGHEST
+    )
+    diffused = jnp.dot(data_block_image.reshape(plane, depth * COLS), per_cell, precision=HIGHEST)
+    mode_fields = mode_fields.reshape(EDGE, EDGE, EDGE * MODES).astype(jnp.bfloat16)
+    diffused = diffused.reshape(EDGE, EDGE, EDGE * MODES).astype(jnp.bfloat16)
     return (gram_matrix, mode_fields, diffused, reduced)
 
 

time: 123 us -> 130 us (1.057)
  other arithmetic: 18.6 us -> 10.2 us
  Pallas kernels: 77.7 us -> 85.8 us
  matrix products: 4.9 us -> 10.5 us
  local copies, waits for them, and re-layouts: 19.9 us -> 21.4 us
    another operation x5 -> x0, other arithmetic: 12.1 us -> none  [the longest x3 6.52 us: factor_basis(): lower_factor = jnp.linalg.cholesky(gram_matrix)]
    pallas_call x0 -> x1, Pallas kernels: none -> 8.04 us  [factor_basis(): pl.pallas_call(factor_kernel, out_shape=jax.ShapeDtypeStruct(prior_basis....]
    convert_element_type x4 -> x0, local copies, waits for them, and re-layouts: 4.38 us -> none  [the longest x2 2.19 us: shards(): mode_basis.reshape(EDGE, EDGE, EDGE * MODES).astype(jnp.bfloat16)]
    mul x0 -> x1, local copies, waits for them, and re-layouts: none -> 3.49 us  [shards(): jnp.eye(depth, dtype=jnp.float32)[:, None, :, None]]
    mul x0 -> x1, other arithmetic: none -> 2.39 us  [shards(): jnp.eye(depth, dtype=jnp.float32)[:, None, :, None]]
    dot_general x2, matrix products: 2.63 us -> 4.51 us  [the longest x1 2.64 us: shards(): jnp.dot(data_block_image.reshape(plane, depth * COLS), per_cell, precisio...]
    dot_general x1, matrix products: 0.9 us -> 2.49 us  [shards(): partial_cross = jnp.dot(data_wide.T, data_image, precision=HIGHEST)]
    div x1, other arithmetic: 0.01 us -> 1.38 us  [shards(): gram_matrix = gram_total / total_cells]
where the time goes in v6:
time: 130 us; the launch traced here: 129 us
  Pallas kernels  85.8 us (66%)
  local copies, waits for them, and re-layouts  21.4 us (16%)
  matrix products  10.5 us (8%)
  other arithmetic  10.2 us (8%)
    pallas_call x1, Pallas kernels, exchange(): pl.pallas_call(functools.partial(exchange_kernel, plane, size_y), out_sha...  39.9 us
    pallas_call x1, Pallas kernels, allreduce(): pl.pallas_call(functools.partial(allreduce_kernel, groups), out_shape=jax...  23 us
    pallas_call x1, Pallas kernels, halo(): pl.pallas_call(functools.partial(halo_kernel, sizes), out_shape=jax.Shape...  8.22 us
    pallas_call x1, Pallas kernels, factor_basis(): pl.pallas_call(factor_kernel, out_shape=jax.ShapeDtypeStruct(prior_basis....  8.04 us
    pallas_call x1, Pallas kernels, average_cells(): pl.pallas_call(average_kernel, grid=(steps,), in_specs=[pl.BlockSpec((row...  6.64 us
    gather x1, local copies, waits for them, and re-layouts, shards(): payload = jnp.take(average_cells(patch_fields), source, axis=0, mode='clip')  3.59 us
    mul x1, local copies, waits for them, and re-layouts, shards(): jnp.eye(depth, dtype=jnp.float32)[:, None, :, None]  3.49 us
    dot_general x1, matrix products, shards(): jnp.dot(data_block_image.reshape(plane, depth * COLS), per_cell, precisio...  2.64 us

profile of v6, /device:TPU:1, one launch (start us, length us, event | category | flops | bytes accessed | tf_op | source)
XLA Modules:
  0.0 128.8 jit_solution(14496763094140132494)
XLA Ops:
  0.7 0.7 compare_select_fusion.4
  1.5 0.7 compare_select_fusion.3
  2.4 1.4 %gather_fusion.1 = s32[32]{0:T(128)S(1)} fusion(s32[32]{0:T(128)} %param.5, s32[1024]{0:T(1024)S(1)} %pad_clamp_fusion.1), kind=kCustom, calls=%fused_computation.1 | custom fusion | bytes 384 | tf_op jit(solution)/shard_map/jit(_take)/gather | solution.py:393
  3.8 1.4 %copy.30.prior_ref = f32[64,32]{1,0:T(8,128)} copy(f32[64,32]{0,1:T(8,128)} %param.7) | data formatting | bytes 16384 | tf_op args[3]
  5.2 0.8 broadcast_in_dim.83.ids_ref
  5.9 1.2 select_convert_fusion.pairing_ref
  7.2 6.6 %shard_map.75 = bf16[32,4,4096]{2,1,0:T(4,128)(2,1)} custom-call(bf16[32,4,32768]{2,1,0:T(4,128)(2,1)} %fine_ref.1, bf16[2048,256]{1,0:T(8,128)(2,1)} %select_convert_fusion.pairing_ref), custom_call_target="tpu_custom_call" | custom-call | tf_op jit(solution)/shard_map/pallas_call | solution.py:97
  13.8 3.6 %gather_fusion = bf16[32,4,4096]{2,1,0:T(4,128)(2,1)} fusion(bf16[32,4,4096]{2,1,0:T(4,128)(2,1)} %shard_map.75, s32[1024]{0:T(1024)S(1)} %pad_clamp_fusion.1), kind=kCustom, calls=%fused_computation | custom fusion | bytes 2097280 | tf_op jit(solution)/shard_map/jit(_take)/gather | solution.py:394
  17.4 39.9 %shard_map.76 = (bf16[32,4,4096]{2,1,0:T(4,128)(2,1)}, s32[32,8,128]{2,1,0:T(8,128)}) custom-call(bf16[32,4,4096]{2,1,0:T(4,128)(2,1)} %gather_fusion, s32[32,8,128]{2,1,0:T(8,128)} %broadcast_in_dim.83.ids_ref), custom_call_target="tpu_custom_call" | custom-call | tf_op jit(solution)/shard_map/pallas_call | solution.py:276
  57.3 1.6 %slice_reduce_fusion = s32[32]{0:T(128)S(1)} fusion(s32[32,8,128]{2,1,0:T(8,128)} %get-tuple-element.7), kind=kLoop, calls=%fused_computation.42 | loop fusion | bytes 256 | tf_op jit(solution)/shard_map/slice | solution.py:397
  59.0 2.2 %gather_fusion.2 = bf16[16,4,4096]{2,1,0:T(4,128)(2,1)S(1)} fusion(bf16[32,4,4096]{2,1,0:T(4,128)(2,1)} %get-tuple-element.6, s32[1024]{0:T(1024)S(1)} %pad_clamp_fusion), kind=kCustom, calls=%fused_computation.2 | custom fusion | bytes 1048640 | tf_op jit(solution)/shard_map/jit(_take)/gather | solution.py:402
  61.3 0.9 fusion.51
  62.7 0.7 reshape.159
  64.2 0.7 copy-done.2
  64.9 8.2 %shard_map.77 = bf16[6,16,1024]{2,1,0:T(8,128)(2,1)} custom-call(bf16[6,16,1024]{2,1,0:T(8,128)(2,1)} %copy-done.2), custom_call_target="tpu_custom_call" | custom-call | tf_op jit(solution)/shard_map/pallas_call | solution.py:330
  73.1 1.0 convert_element_type.30
  74.1 0.7 copy.29
  74.8 0.7 copy.28
  75.8 1.5 %fusion.11 = f32[16,16,1024]{2,1,0:T(8,128)S(1)} fusion(f32[16,16,1024]{2,1,0:T(8,128)S(1)} %convert_element_type.29, f32[16,16,64]{2,1,0:T(8,128)S(1)} %select_n.168, f32[16,16,64]{2,1,0:T(8,128)S(1)} %select_n.165, f32[16,1,1024]{2,1,0:T(1,128)} %copy.29, f32[16,1,1024]{2,1,0:T(1,128)} %copy.28, f32[1,16,1024]{2,1,0:T(8,128)S(1)} %get-tuple-element.19, ...), kind=kLoop, calls=%fused_computation.14 | loop fusion | flops 3407872 | bytes 2490368 | tf_op jit(solution)/shard_map/sub | solution.py:371
  77.3 1.9 %reshape.160 = f32[4096,64]{1,0:T(8,128)} reshape(f32[16,16,1024]{2,1,0:T(8,128)S(1)} %fusion.11) | data formatting | bytes 2097152 | tf_op jit(solution)/shard_map/reshape | solution.py:408
  79.3 2.5 %fusion.52 = f32[64,64]{1,0:T(8,128)S(1)} fusion(bf16[64,4096]{1,0:T(8,128)(2,1)S(1)} %reshape.158, f32[4096,64]{1,0:T(8,128)} %reshape.160), kind=kOutput, calls=%fused_computation.108 | convolution fusion | flops 201326592 | bytes 1589248 | tf_op jit(solution)/shard_map/dot_general | solution.py:409
  81.8 0.7 pad_maximum_fusion.6.part_ref
  82.5 23.0 %shard_map.78 = f32[64,128]{1,0:T(8,128)} custom-call(f32[64,128]{1,0:T(8,128)} %pad_maximum_fusion.6.part_ref), custom_call_target="tpu_custom_call" | custom-call | tf_op jit(solution)/shard_map/pallas_call | solution.py:224
  105.5 1.4 %slice_multiply_fusion.gram_ref = f32[64,64]{1,0:T(8,128)} fusion(f32[64,128]{1,0:T(8,128)} %shard_map.78), kind=kLoop, calls=%fused_computation.40 | loop fusion | flops 4096 | bytes 32768 | tf_op jit(solution)/shard_map/div | solution.py:412
  106.8 8.0 %shard_map.79 = f32[64,32]{1,0:T(8,128)} custom-call(f32[64,64]{1,0:T(8,128)} %slice_multiply_fusion.gram_ref, f32[64,32]{1,0:T(8,128)} %copy.30.prior_ref), custom_call_target="tpu_custom_call" | custom-call | tf_op jit(solution)/shard_map/pallas_call | solution.py:139
  114.9 1.0 fusion.20
  115.9 1.6 %fusion.53 = f32[32,32]{1,0:T(8,128)} fusion(f32[64,32]{1,0:T(8,128)} %shard_map.79, f32[64,32]{0,1:T(8,128)S(1)} %fusion.20), kind=kOutput, calls=%fused_computation.109 | convolution fusion | flops 786432 | bytes 20480 | tf_op jit(solution)/shard_map/dot_general | solution.py:415
  117.5 0.8 copy.31
  118.3 2.4 %broadcast_multiply_fusion = f32[16,64,16,32]{1,0,3,2:T(8,128)} fusion(f32[64,32]{0,1:T(8,128)S(1)} %copy.31, f32[16,16]{0,1:T(8,128)S(1)} %fusion.44), kind=kLoop, calls=%fused_computation.7 | loop fusion | flops 524288 | bytes 2106368 | tf_op jit(solution)/shard_map/mul | solution.py:417
  120.7 3.5 %mul.52 = f32[1024,512]{0,1:T(8,128)S(1)} reshape(f32[16,64,16,32]{1,0,3,2:T(8,128)} %broadcast_multiply_fusion) | data formatting | bytes 4194304 | tf_op jit(solution)/shard_map/mul | solution.py:417
  124.2 2.6 %fusion.7 = bf16[16,16,512]{2,1,0:T(8,128)(2,1)} fusion(f32[16,16,1024]{2,1,0:T(8,128)S(1)} %fusion.11, f32[1024,512]{0,1:T(8,128)S(1)} %mul.52), kind=kOutput, calls=%fused_computation.11 | convolution fusion | flops 1610743808 | bytes 3407872 | tf_op jit(solution)/shard_map/dot_general | solution.py:423
  126.9 1.9 %fusion.4 = bf16[16,16,512]{2,1,0:T(8,128)(2,1)} fusion(bf16[16,16,1024]{2,1,0:T(8,128)(2,1)S(1)} %copy-done.1, f32[1024,512]{0,1:T(8,128)S(1)} %mul.52), kind=kOutput, calls=%fused_computation.10 | convolution fusion | flops 1610743808 | bytes 2883584 | tf_op jit(solution)/shard_map/dot_general | solution.py:420
  (35 shorter events, 2.2 us)
Async XLA Ops:
  63.5 12.4 %copy-start = (bf16[16,16,1024]{2,1,0:T(8,128)(2,1)}, bf16[16,16,1024]{2,1,0:T(8,128)(2,1)S(1)}, u32[]{:S(2)}) copy-start(bf16[16,16,1024]{2,1,0:T(8,128)(2,1)S(1)} %reshape.159) | copy-start | bytes 1572868
  64.2 0.7 copy-start.2
  79.3 2.5 %copy-start.3 = (f32[64,64]{1,0:T(8,128)S(1)}, f32[64,64]{1,0:T(8,128)}, u32[]{:S(2)}) copy-start(f32[64,64]{1,0:T(8,128)} %fusion.51) | copy-start | bytes 49156
  124.2 2.7 %copy-start.1 = (bf16[16,16,1024]{2,1,0:T(8,128)(2,1)S(1)}, bf16[16,16,1024]{2,1,0:T(8,128)(2,1)}, u32[]{:S(2)}) copy-start(bf16[16,16,1024]{2,1,0:T(8,128)(2,1)} %copy-done) | copy-start | bytes 1572868

commit v7 on v6

--- a/solution.py
+++ b/solution.py
@@ -121,7 +121,7 @@
     for j in range(size):
         pivot = jnp.sqrt(work[j : j + 1, j : j + 1])
         column = jnp.where(rows[:, j : j + 1] >= j, work[:, j : j + 1] / pivot, 0.0)
-        row = jnp.sum(jnp.where(rows == cols, column, 0.0), axis=0, keepdims=True)
+        row = jnp.where(cols[j : j + 1, :] >= j, work[j : j + 1, :] / pivot, 0.0)
         upper = jnp.where(rows == j, row, upper)
         work = work - column * row
     solved = prior_ref[...]
@@ -141,7 +141,7 @@
         out_shape=jax.ShapeDtypeStruct(prior_basis.shape, prior_basis.dtype),
         in_specs=[vmem, vmem],
         out_specs=vmem,
-    )(gram_matrix, prior_basis)
+    )((gram_matrix + gram_matrix.T) * 0.5, prior_basis)
 
 
 def tree_sum(values):
@@ -404,25 +404,18 @@
     partial_gram = jnp.dot(columns, columns.T, preferred_element_type=jnp.float32)
     data_wide = columns.astype(jnp.float32).T
     data_block = columns.T.reshape(EDGE, EDGE, EDGE * COLS)
-    data_block_image = diffusion(data_block)
-    data_image = data_block_image.reshape(CELLS, COLS)
+    data_image = diffusion(data_block).reshape(CELLS, COLS)
     partial_cross = jnp.dot(data_wide.T, data_image, precision=HIGHEST)
     totals = allreduce(jnp.concatenate([partial_gram, partial_cross], axis=1))
     gram_total, cross_total = totals[:, :COLS], totals[:, COLS:]
     gram_matrix = gram_total / total_cells
     coeffs = factor_basis(gram_matrix, prior_basis)
+    mode_basis = jnp.dot(data_wide, coeffs, precision=HIGHEST)
+    mode_image = jnp.dot(data_image, coeffs, precision=HIGHEST)
     inner = jnp.dot(cross_total / total_cells, coeffs, precision=HIGHEST)
     reduced = jnp.dot(coeffs.T, inner, precision=HIGHEST)
-    depth = data_block.shape[2] // COLS
-    per_cell = jnp.eye(depth, dtype=jnp.float32)[:, None, :, None] * coeffs[None, :, None, :]
-    per_cell = per_cell.reshape(depth * COLS, depth * MODES)
-    plane = data_block.shape[0] * data_block.shape[1]
-    mode_fields = jnp.dot(
-        data_block.reshape(plane, depth * COLS).astype(jnp.float32), per_cell, precision=HIGHEST
-    )
-    diffused = jnp.dot(data_block_image.reshape(plane, depth * COLS), per_cell, precision=HIGHEST)
-    mode_fields = mode_fields.reshape(EDGE, EDGE, EDGE * MODES).astype(jnp.bfloat16)
-    diffused = diffused.reshape(EDGE, EDGE, EDGE * MODES).astype(jnp.bfloat16)
+    mode_fields = mode_basis.reshape(EDGE, EDGE, EDGE * MODES).astype(jnp.bfloat16)
+    diffused = mode_image.reshape(EDGE, EDGE, EDGE * MODES).astype(jnp.bfloat16)
     return (gram_matrix, mode_fields, diffused, reduced)
 
 

time: 130 us -> 122 us (0.938)
  matrix products: 10.5 us -> 7.34 us
  other arithmetic: 10.2 us -> 7.18 us
    convert_element_type x0 -> x4, local copies, waits for them, and re-layouts: none -> 4.38 us  [the longest x2 2.19 us: shards(): diffused = mode_image.reshape(EDGE, EDGE, EDGE * MODES).astype(jnp.bfloat16)]
    mul x1 -> x0, local copies, waits for them, and re-layouts: 3.49 us -> none  [shards(): jnp.eye(depth, dtype=jnp.float32)[:, None, :, None]]
    mul x1, other arithmetic: 2.39 us -> 0.63 us  [factor_basis(): (gram_matrix + gram_matrix.T) * 0.5]
    dot_general x1, matrix products: 2.49 us -> 0.9 us  [shards(): partial_cross = jnp.dot(data_wide.T, data_image, precision=HIGHEST)]
    div x1, other arithmetic: 1.38 us -> 0.01 us  [shards(): gram_matrix = gram_total / total_cells]
where the time goes in v7:
time: 122 us
  Pallas kernels  85.7 us (70%)
  local copies, waits for them, and re-layouts  20.6 us (17%)
  matrix products  7.34 us (6%)
  other arithmetic  7.18 us (6%)
    pallas_call x1, Pallas kernels, exchange(): pl.pallas_call(functools.partial(exchange_kernel, plane, size_y), out_sha...  39.9 us
    pallas_call x1, Pallas kernels, allreduce(): pl.pallas_call(functools.partial(allreduce_kernel, groups), out_shape=jax...  23 us
    pallas_call x1, Pallas kernels, halo(): pl.pallas_call(functools.partial(halo_kernel, sizes), out_shape=jax.Shape...  8.22 us
    pallas_call x1, Pallas kernels, factor_basis(): pl.pallas_call(factor_kernel, out_shape=jax.ShapeDtypeStruct(prior_basis....  7.93 us
    pallas_call x1, Pallas kernels, average_cells(): pl.pallas_call(average_kernel, grid=(steps,), in_specs=[pl.BlockSpec((row...  6.64 us
    gather x1, local copies, waits for them, and re-layouts, shards(): payload = jnp.take(average_cells(patch_fields), source, axis=0, mode='clip')  3.59 us
    dot_general x1, matrix products, shards(): mode_image = jnp.dot(data_image, coeffs, precision=HIGHEST)  3.16 us

profile of v7, /device:TPU:1, one launch (start us, length us, event | category | flops | bytes accessed | tf_op | source)
XLA Modules:
  0.0 121.7 jit_solution(17742740808215545834)
XLA Ops:
  0.6 0.7 compare_select_fusion.4
  1.5 0.7 compare_select_fusion.3
  2.3 1.4 %gather_fusion.1 = s32[32]{0:T(128)S(1)} fusion(s32[32]{0:T(128)} %param.5, s32[1024]{0:T(1024)S(1)} %pad_clamp_fusion.1), kind=kCustom, calls=%fused_computation.1 | custom fusion | bytes 384 | tf_op jit(solution)/shard_map/jit(_take)/gather | solution.py:393
  3.7 0.8 broadcast_in_dim.81.ids_ref
  4.5 1.2 %select_convert_fusion.pairing_ref = bf16[2048,256]{1,0:T(8,128)(2,1)} fusion(s32[2048]{0:T(1024)S(1)} %fusion.29), kind=kLoop, calls=%fused_computation.5 | loop fusion | flops 1572864 | bytes 1056768 | tf_op jit(solution)/shard_map/convert_element_type | solution.py:70
  5.7 6.6 %shard_map.75 = bf16[32,4,4096]{2,1,0:T(4,128)(2,1)} custom-call(bf16[32,4,32768]{2,1,0:T(4,128)(2,1)} %fine_ref.1, bf16[2048,256]{1,0:T(8,128)(2,1)} %select_convert_fusion.pairing_ref), custom_call_target="tpu_custom_call" | custom-call | tf_op jit(solution)/shard_map/pallas_call | solution.py:97
  12.4 3.6 %gather_fusion = bf16[32,4,4096]{2,1,0:T(4,128)(2,1)} fusion(bf16[32,4,4096]{2,1,0:T(4,128)(2,1)} %shard_map.75, s32[1024]{0:T(1024)S(1)} %pad_clamp_fusion.1), kind=kCustom, calls=%fused_computation | custom fusion | bytes 2097280 | tf_op jit(solution)/shard_map/jit(_take)/gather | solution.py:394
  16.0 39.9 %shard_map.76 = (bf16[32,4,4096]{2,1,0:T(4,128)(2,1)}, s32[32,8,128]{2,1,0:T(8,128)}) custom-call(bf16[32,4,4096]{2,1,0:T(4,128)(2,1)} %gather_fusion, s32[32,8,128]{2,1,0:T(8,128)} %broadcast_in_dim.81.ids_ref), custom_call_target="tpu_custom_call" | custom-call | tf_op jit(solution)/shard_map/pallas_call | solution.py:276
  55.9 1.6 %slice_reduce_fusion = s32[32]{0:T(128)S(1)} fusion(s32[32,8,128]{2,1,0:T(8,128)} %get-tuple-element.7), kind=kLoop, calls=%fused_computation.38 | loop fusion | bytes 256 | tf_op jit(solution)/shard_map/slice | solution.py:397
  57.6 2.2 %gather_fusion.2 = bf16[16,4,4096]{2,1,0:T(4,128)(2,1)S(1)} fusion(bf16[32,4,4096]{2,1,0:T(4,128)(2,1)} %get-tuple-element.6, s32[1024]{0:T(1024)S(1)} %pad_clamp_fusion), kind=kCustom, calls=%fused_computation.2 | custom fusion | bytes 1048640 | tf_op jit(solution)/shard_map/jit(_take)/gather | solution.py:402
  59.9 0.5 copy.30
  60.7 0.7 reshape.132
  61.9 0.7 copy-done.1
  62.6 8.2 %shard_map.77 = bf16[6,16,1024]{2,1,0:T(8,128)(2,1)} custom-call(bf16[6,16,1024]{2,1,0:T(8,128)(2,1)} %copy-done.1), custom_call_target="tpu_custom_call" | custom-call | tf_op jit(solution)/shard_map/pallas_call | solution.py:330
  70.8 1.0 convert_element_type.28
  72.3 1.6 %fusion.1 = f32[16,16,1024]{2,1,0:T(8,128)} fusion(f32[16,16,1024]{2,1,0:T(8,128)S(1)} %convert_element_type.27, f32[16,16,64]{2,1,0:T(8,128)S(1)} %select_n.168, f32[16,16,64]{2,1,0:T(8,128)S(1)} %select_n.165, f32[16,1,1024]{2,1,0:T(1,128)S(1)} %copy.34, f32[16,1,1024]{2,1,0:T(1,128)S(1)} %copy.33, f32[1,16,1024]{2,1,0:T(8,128)S(1)} %get-tuple-element.31, ...), kind=kLoop, calls=%fused_computation.9 | loop fusion | flops 3407872 | bytes 2490368 | tf_op jit(solution)/shard_map/sub | solution.py:371
  73.9 1.9 %reshape.133 = f32[4096,64]{1,0:T(8,128)S(1)} reshape(f32[16,16,1024]{2,1,0:T(8,128)} %fusion.1) | data formatting | bytes 2097152 | tf_op jit(solution)/shard_map/reshape | solution.py:407
  75.8 0.9 fusion.42
  77.0 0.7 pad_maximum_fusion.6.part_ref
  77.7 23.0 %shard_map.78 = f32[64,128]{1,0:T(8,128)} custom-call(f32[64,128]{1,0:T(8,128)} %pad_maximum_fusion.6.part_ref), custom_call_target="tpu_custom_call" | custom-call | tf_op jit(solution)/shard_map/pallas_call | solution.py:224
  100.7 0.9 fusion.40
  101.8 0.6 fusion.10.gram_ref
  102.4 0.7 copy.37.prior_ref
  103.1 7.9 %shard_map.79 = f32[64,32]{1,0:T(8,128)} custom-call(f32[64,64]{1,0:T(8,128)} %fusion.10.gram_ref, f32[64,32]{1,0:T(8,128)} %copy.37.prior_ref), custom_call_target="tpu_custom_call" | custom-call | tf_op jit(solution)/shard_map/pallas_call | solution.py:139
  111.1 1.0 fusion.11
  112.1 1.6 %fusion.43 = f32[32,32]{1,0:T(8,128)} fusion(f32[64,32]{1,0:T(8,128)} %shard_map.79, f32[64,32]{0,1:T(8,128)S(1)} %fusion.11), kind=kOutput, calls=%fused_computation.104 | convolution fusion | flops 786432 | bytes 20480 | tf_op jit(solution)/shard_map/dot_general | solution.py:416
  113.7 3.2 %convolution_convert_fusion = bf16[4096,32]{0,1:T(8,128)(2,1)S(1)} fusion(f32[4096,64]{1,0:T(8,128)S(1)} %reshape.133, f32[64,32]{1,0:T(8,128)} %shard_map.79), kind=kOutput, calls=%fused_computation.3 | convolution fusion | flops 100794368 | bytes 1318912 | tf_op jit(solution)/shard_map/dot_general | solution.py:414
  116.9 0.5 copy.39
  117.4 1.7 %convert_element_type.32 = bf16[16,16,512]{2,1,0:T(8,128)(2,1)} reshape(bf16[4096,32]{1,0:T(8,128)(2,1)S(1)} %copy.39) | data formatting | bytes 524288 | tf_op jit(solution)/shard_map/convert_element_type | solution.py:418
  119.1 0.4 convolution_convert_fusion.1
  119.5 0.5 copy.38
  120.0 1.7 %convert_element_type.30 = bf16[16,16,512]{2,1,0:T(8,128)(2,1)} reshape(bf16[4096,32]{1,0:T(8,128)(2,1)S(1)} %copy.38) | data formatting | bytes 524288 | tf_op jit(solution)/shard_map/convert_element_type | solution.py:417
  (40 shorter events, 2.3 us)
Async XLA Ops:
  61.9 0.7 copy-start.1
  75.8 26.6 %copy-start.3 = (f32[64,32]{0,1:T(8,128)S(1)}, f32[64,32]{0,1:T(8,128)}, u32[]{:S(2)}) copy-start(f32[64,32]{0,1:T(8,128)} %param.7) | copy-start | bytes 24580
  101.8 17.3 %copy-start.2 = (f32[64,64]{1,0:T(8,128)}, f32[64,64]{1,0:T(8,128)S(1)}, u32[]{:S(2)}) copy-start(f32[64,64]{1,0:T(8,128)S(1)} %copy.41) | copy-start | bytes 49156
  113.7 5.4 %copy-start = (f32[64,32]{1,0:T(8,128)S(1)}, f32[64,32]{1,0:T(8,128)}, u32[]{:S(2)}) copy-start(f32[64,32]{1,0:T(8,128)} %shard_map.79) | copy-start | bytes 24580

commit v8 on v7

--- a/solution.py
+++ b/solution.py
@@ -73,7 +73,7 @@
 PAIRS_PER_STEP = 4
 
 
-def average_kernel(fine_ref, pairing_ref, out_ref):
+def average_kernel(source_ref, fine_ref, pairing_ref, out_ref, means_ref):
     slots = fine_ref.shape[0]
     rows = slots * FIELDS
     span = 2 * PATCH * PATCH
@@ -84,26 +84,65 @@
     means = jnp.dot(stacked, pairing_ref[...], preferred_element_type=jnp.float32)
     width = EDGE * EDGE
     for i in range(PAIRS_PER_STEP):
-        out_ref[:, :, i * width : (i + 1) * width] = (
-            means[i * rows : (i + 1) * rows].reshape(slots, FIELDS, width).astype(out_ref.dtype)
+        means_ref[:, :, i * width : (i + 1) * width] = (
+            means[i * rows : (i + 1) * rows].reshape(slots, FIELDS, width).astype(means_ref.dtype)
         )
-
-
-def average_cells(fine_data):
+    for slot in range(slots):
+        out_ref[slot] = means_ref[source_ref[slot]]
+
+
+def average_cells(fine_data, source):
     row_count = fine_data.shape[0]
     span = 2 * PATCH * PATCH * PAIRS_PER_STEP
     width = EDGE * EDGE * PAIRS_PER_STEP
     steps = EDGE // PAIRS_PER_STEP
-    return pl.pallas_call(
-        average_kernel,
+    grid_spec = pltpu.PrefetchScalarGridSpec(
+        num_scalar_prefetch=1,
         grid=(steps,),
         in_specs=[
-            pl.BlockSpec((row_count, FIELDS, span), lambda g: (0, 0, g)),
-            pl.BlockSpec((2 * PATCH * PATCH, EDGE * EDGE), lambda g: (0, 0)),
+            pl.BlockSpec((row_count, FIELDS, span), lambda g, order: (0, 0, g)),
+            pl.BlockSpec((2 * PATCH * PATCH, EDGE * EDGE), lambda g, order: (0, 0)),
         ],
-        out_specs=pl.BlockSpec((row_count, FIELDS, width), lambda g: (0, 0, g)),
+        out_specs=pl.BlockSpec((row_count, FIELDS, width), lambda g, order: (0, 0, g)),
+        scratch_shapes=[pltpu.VMEM((row_count, FIELDS, width), jnp.bfloat16)],
+    )
+    return pl.pallas_call(
+        average_kernel,
+        grid_spec=grid_spec,
         out_shape=jax.ShapeDtypeStruct((row_count, FIELDS, CELLS), jnp.bfloat16),
-    )(fine_data, pairing_matrix())
+    )(source, fine_data, pairing_matrix())
+
+
+def modes_kernel(data_ref, image_ref, coeffs_ref, fields_ref, diffused_ref):
+    coeffs = coeffs_ref[...]
+    high = coeffs.astype(jnp.bfloat16)
+    low = (coeffs - high.astype(jnp.float32)).astype(jnp.bfloat16)
+    cols, modes = coeffs.shape
+    for z in range(data_ref.shape[1] // cols):
+        data = data_ref[:, z * cols : (z + 1) * cols]
+        fields = jnp.dot(data, high, preferred_element_type=jnp.float32)
+        fields = fields + jnp.dot(data, low, preferred_element_type=jnp.float32)
+        fields_ref[:, z * modes : (z + 1) * modes] = fields.astype(fields_ref.dtype)
+        image = image_ref[:, z * cols : (z + 1) * cols]
+        image_high = image.astype(jnp.bfloat16)
+        image_low = (image - image_high.astype(jnp.float32)).astype(jnp.bfloat16)
+        diffused = jnp.dot(image_high, high, preferred_element_type=jnp.float32)
+        diffused = diffused + jnp.dot(image_high, low, preferred_element_type=jnp.float32)
+        diffused = diffused + jnp.dot(image_low, high, preferred_element_type=jnp.float32)
+        diffused_ref[:, z * modes : (z + 1) * modes] = diffused.astype(diffused_ref.dtype)
+
+
+def project_modes(data, image, coeffs):
+    rows, width = data.shape
+    out_width = width // coeffs.shape[0] * coeffs.shape[1]
+    vmem = pl.BlockSpec(memory_space=pltpu.VMEM)
+    shape = jax.ShapeDtypeStruct((rows, out_width), jnp.bfloat16)
+    return pl.pallas_call(
+        modes_kernel,
+        out_shape=(shape, shape),
+        in_specs=[vmem, vmem, vmem],
+        out_specs=(vmem, vmem),
+    )(data, image, coeffs)
 
 
 def seven_point(center, around_xy, around_z, stride):
@@ -391,7 +430,7 @@
     filled = jnp.any(slot_hits, axis=0)
     source = jnp.sum(jnp.where(slot_hits, slot_ids[:, None], 0), axis=0)
     sent_snapshot = jnp.where(filled, jnp.take(slot_snapshot, source, mode="clip"), -1)
-    payload = jnp.take(average_cells(patch_fields), source, axis=0, mode="clip")
+    payload = average_cells(patch_fields, source)
     sent_ids = jnp.broadcast_to(sent_snapshot[:, None, None], (slot_count, 8, 128))
     received, received_ids = exchange(payload, sent_ids)
     received_snapshot = received_ids[:, 0, 0]
@@ -404,18 +443,21 @@
     partial_gram = jnp.dot(columns, columns.T, preferred_element_type=jnp.float32)
     data_wide = columns.astype(jnp.float32).T
     data_block = columns.T.reshape(EDGE, EDGE, EDGE * COLS)
-    data_image = diffusion(data_block).reshape(CELLS, COLS)
+    data_block_image = diffusion(data_block)
+    data_image = data_block_image.reshape(CELLS, COLS)
     partial_cross = jnp.dot(data_wide.T, data_image, precision=HIGHEST)
     totals = allreduce(jnp.concatenate([partial_gram, partial_cross], axis=1))
     gram_total, cross_total = totals[:, :COLS], totals[:, COLS:]
     gram_matrix = gram_total / total_cells
     coeffs = factor_basis(gram_matrix, prior_basis)
-    mode_basis = jnp.dot(data_wide, coeffs, precision=HIGHEST)
-    mode_image = jnp.dot(data_image, coeffs, precision=HIGHEST)
     inner = jnp.dot(cross_total / total_cells, coeffs, precision=HIGHEST)
     reduced = jnp.dot(coeffs.T, inner, precision=HIGHEST)
-    mode_fields = mode_basis.reshape(EDGE, EDGE, EDGE * MODES).astype(jnp.bfloat16)
-    diffused = mode_image.reshape(EDGE, EDGE, EDGE * MODES).astype(jnp.bfloat16)
+    plane = data_block.shape[0] * data_block.shape[1]
+    mode_fields, diffused = project_modes(
+        data_block.reshape(plane, -1), data_block_image.reshape(plane, -1), coeffs
+    )
+    mode_fields = mode_fields.reshape(EDGE, EDGE, EDGE * MODES)
+    diffused = diffused.reshape(EDGE, EDGE, EDGE * MODES)
     return (gram_matrix, mode_fields, diffused, reduced)
 
 

time: 122 us -> 118 us (0.967)
  local copies, waits for them, and re-layouts: 20.6 us -> 14.9 us
  Pallas kernels: 85.7 us -> 90.1 us
  matrix products: 7.34 us -> 5.33 us
    pallas_call x1 -> x2, Pallas kernels: 6.64 us -> 11 us  [the longest x1 7.36 us: average_cells(): pl.pallas_call(average_kernel, grid_spec=grid_spec, out_shape=jax.ShapeDt...]
    convert_element_type x4 -> x0, local copies, waits for them, and re-layouts: 4.38 us -> none  [the longest x2 2.19 us: shards(): diffused = mode_image.reshape(EDGE, EDGE, EDGE * MODES).astype(jnp.bfloat16)]
    gather x1 -> x0, local copies, waits for them, and re-layouts: 3.59 us -> none  [shards(): payload = jnp.take(average_cells(patch_fields), source, axis=0, mode='clip')]
    dot_general x2 -> x0, matrix products: 3.58 us -> none  [the longest x1 3.16 us: shards(): mode_image = jnp.dot(data_image, coeffs, precision=HIGHEST)]
    dot_general x1, matrix products: 0.9 us -> 2.48 us  [shards(): partial_cross = jnp.dot(data_wide.T, data_image, precision=HIGHEST)]
    another operation x0 -> x1, local copies, waits for them, and re-layouts: none -> 1.51 us  [shards(): data_block.reshape(plane, -1)]
where the time goes in v8:
time: 118 us; the launch traced here: 117 us
  Pallas kernels  90.1 us (76%)
  local copies, waits for them, and re-layouts  14.9 us (13%)
  other arithmetic  6.26 us (5%)
  matrix products  5.33 us (5%)
    pallas_call x1, Pallas kernels, exchange(): pl.pallas_call(functools.partial(exchange_kernel, plane, size_y), out_sha...  39.9 us
    pallas_call x1, Pallas kernels, allreduce(): pl.pallas_call(functools.partial(allreduce_kernel, groups), out_shape=jax...  23 us
    pallas_call x1, Pallas kernels, halo(): pl.pallas_call(functools.partial(halo_kernel, sizes), out_shape=jax.Shape...  8.22 us
    pallas_call x1, Pallas kernels, factor_basis(): pl.pallas_call(factor_kernel, out_shape=jax.ShapeDtypeStruct(prior_basis....  7.93 us
    pallas_call x1, Pallas kernels, average_cells(): pl.pallas_call(average_kernel, grid_spec=grid_spec, out_shape=jax.ShapeDt...  7.36 us
    pallas_call x1, Pallas kernels, project_modes(): pl.pallas_call(modes_kernel, out_shape=(shape, shape), in_specs=[vmem, vm...  3.68 us
    dot_general x1, matrix products, shards(): partial_cross = jnp.dot(data_wide.T, data_image, precision=HIGHEST)  2.48 us
    unnamed x17, local copies, waits for them, and re-layouts  2.38 us

profile of v8, /device:TPU:1, one launch (start us, length us, event | category | flops | bytes accessed | tf_op | source)
XLA Modules:
  0.0 117.5 jit_solution(1778957577813750843)
XLA Ops:
  0.7 0.7 compare_select_fusion.4
  1.3 0.2 convert_reduce_fusion
  1.5 0.7 compare_select_fusion.3
  2.4 1.4 %gather_fusion = s32[32]{0:T(128)S(1)} fusion(s32[32]{0:T(128)} %param.5, s32[1024]{0:T(1024)S(1)} %pad_clamp_fusion.1), kind=kCustom, calls=%fused_computation | custom fusion | bytes 384 | tf_op jit(solution)/shard_map/jit(_take)/gather | solution.py:432
  3.8 1.4 %copy.36.prior_ref = f32[64,32]{1,0:T(8,128)} copy(f32[64,32]{0,1:T(8,128)} %param.7) | data formatting | bytes 16384 | tf_op args[3]
  5.2 0.8 broadcast_in_dim.79.ids_ref
  5.9 1.2 %select_convert_fusion.pairing_ref = bf16[2048,256]{1,0:T(8,128)(2,1)} fusion(s32[2048]{0:T(1024)S(1)} %fusion.29), kind=kLoop, calls=%fused_computation.2 | loop fusion | flops 1572864 | bytes 1056768 | tf_op jit(solution)/shard_map/convert_element_type | solution.py:70
  7.2 7.4 %shard_map.75.payload_ref = bf16[32,4,4096]{2,1,0:T(4,128)(2,1)} custom-call(s32[32]{0:T(128)} %copy-done.3, bf16[32,4,32768]{2,1,0:T(4,128)(2,1)} %fine_ref.1, bf16[2048,256]{1,0:T(8,128)(2,1)} %select_convert_fusion.pairing_ref), custom_call_target="tpu_custom_call" | custom-call | tf_op jit(solution)/shard_map/pallas_call | solution.py:109
  14.5 39.9 %shard_map.76 = (bf16[32,4,4096]{2,1,0:T(4,128)(2,1)}, s32[32,8,128]{2,1,0:T(8,128)}) custom-call(bf16[32,4,4096]{2,1,0:T(4,128)(2,1)} %shard_map.75.payload_ref, s32[32,8,128]{2,1,0:T(8,128)} %broadcast_in_dim.79.ids_ref), custom_call_target="tpu_custom_call" | custom-call | tf_op jit(solution)/shard_map/pallas_call | solution.py:315
  54.4 1.6 %slice_reduce_fusion = s32[32]{0:T(128)S(1)} fusion(s32[32,8,128]{2,1,0:T(8,128)} %get-tuple-element.9), kind=kLoop, calls=%fused_computation.35 | loop fusion | bytes 256 | tf_op jit(solution)/shard_map/slice | solution.py:436
  56.0 0.1 select_reduce_fusion.1
  56.1 2.2 %gather_fusion.1 = bf16[16,4,4096]{2,1,0:T(4,128)(2,1)S(1)} fusion(bf16[32,4,4096]{2,1,0:T(4,128)(2,1)} %get-tuple-element.8, s32[1024]{0:T(1024)S(1)} %pad_clamp_fusion), kind=kCustom, calls=%fused_computation.1 | custom fusion | bytes 1048640 | tf_op jit(solution)/shard_map/jit(_take)/gather | solution.py:441
  58.4 0.1 reshape.136
  58.5 0.3 fusion.41
  58.8 0.5 copy.29
  59.3 0.1 slice.79
  59.5 0.7 reshape.137
  60.2 1.5 %reshape_reshape.3.data_ref = bf16[256,1024]{1,0:T(8,128)(2,1)} reshape(bf16[4096,64]{1,0:T(8,128)(2,1)S(1)} %bitcast.29) | data formatting | bytes 1048576 | tf_op jit(solution)/shard_map/reshape;reshape | solution.py:457
  62.3 0.7 copy-done.1
  62.9 8.2 %shard_map.77 = bf16[6,16,1024]{2,1,0:T(8,128)(2,1)} custom-call(bf16[6,16,1024]{2,1,0:T(8,128)(2,1)} %copy-done.1), custom_call_target="tpu_custom_call" | custom-call | tf_op jit(solution)/shard_map/pallas_call | solution.py:369
  71.2 1.0 convert_element_type.16
  72.6 0.7 fusion.1
  73.3 1.9 %reshape.138 = f32[4096,64]{1,0:T(8,128)} reshape(f32[16,16,1024]{2,1,0:T(8,128)S(1)} %fusion.1) | data formatting | bytes 2097152 | tf_op jit(solution)/shard_map/reshape | solution.py:447
  75.3 2.5 %fusion.42 = f32[64,64]{1,0:T(8,128)S(1)} fusion(bf16[64,4096]{1,0:T(8,128)(2,1)S(1)} %reshape.136, f32[4096,64]{1,0:T(8,128)} %reshape.138), kind=kOutput, calls=%fused_computation.100 | convolution fusion | flops 201326592 | bytes 1589248 | tf_op jit(solution)/shard_map/dot_general | solution.py:448
  77.7 0.7 pad_maximum_fusion.6.part_ref
  78.4 23.0 %shard_map.78 = f32[64,128]{1,0:T(8,128)} custom-call(f32[64,128]{1,0:T(8,128)} %pad_maximum_fusion.6.part_ref), custom_call_target="tpu_custom_call" | custom-call | tf_op jit(solution)/shard_map/pallas_call | solution.py:263
  101.5 0.9 fusion.40
  102.6 0.6 fusion.10.gram_ref
  103.3 7.9 %shard_map.79.coeffs_ref = f32[64,32]{1,0:T(8,128)} custom-call(f32[64,64]{1,0:T(8,128)} %fusion.10.gram_ref, f32[64,32]{1,0:T(8,128)} %copy.36.prior_ref), custom_call_target="tpu_custom_call" | custom-call | tf_op jit(solution)/shard_map/pallas_call | solution.py:178
  111.2 3.7 %shard_map.80 = (bf16[256,512]{1,0:T(8,128)(2,1)}, bf16[256,512]{1,0:T(8,128)(2,1)}) custom-call(bf16[256,1024]{1,0:T(8,128)(2,1)} %reshape_reshape.3.data_ref, f32[256,1024]{1,0:T(8,128)} %bitcast.30, f32[64,32]{1,0:T(8,128)} %shard_map.79.coeffs_ref), custom_call_target="tpu_custom_call" | custom-call | tf_op jit(solution)/shard_map/pallas_call | solution.py:140
  114.9 1.0 fusion.11
  115.9 1.6 %fusion.43 = f32[32,32]{1,0:T(8,128)} fusion(f32[64,32]{1,0:T(8,128)} %shard_map.79.coeffs_ref, f32[64,32]{0,1:T(8,128)S(1)} %fusion.11), kind=kOutput, calls=%fused_computation.101 | convolution fusion | flops 786432 | bytes 20480 | tf_op jit(solution)/shard_map/dot_general | solution.py:454
  (35 shorter events, 1.5 us)
Async XLA Ops:
  2.3 4.9 %copy-start.3 = (s32[32]{0:T(128)}, s32[32]{0:T(128)S(1)}, u32[]{:S(2)}) copy-start(s32[32]{0:T(128)S(1)} %select_reduce_fusion.source_ref) | copy-start | bytes 388
  62.3 0.7 copy-start.1
  73.3 4.4 %copy-start = (f32[16,16,1024]{2,1,0:T(8,128)}, f32[16,16,1024]{2,1,0:T(8,128)S(1)}, u32[]{:S(2)}) copy-start(f32[16,16,1024]{2,1,0:T(8,128)S(1)} %fusion.1) | copy-start | bytes 3145732
  102.6 14.8 %copy-start.2 = (f32[64,64]{1,0:T(8,128)}, f32[64,64]{1,0:T(8,128)S(1)}, u32[]{:S(2)}) copy-start(f32[64,64]{1,0:T(8,128)S(1)} %copy.38) | copy-start | bytes 49156

commit v9 on v8

--- a/solution.py
+++ b/solution.py
@@ -151,7 +151,21 @@
     return total - 6.0 * center
 
 
-def factor_kernel(gram_ref, prior_ref, out_ref):
+def split(value):
+    high = value.astype(jnp.bfloat16)
+    return high, (value - high.astype(jnp.float32)).astype(jnp.bfloat16)
+
+
+def exact_dot(left, right, contract=1):
+    numbers = (((contract,), (0,)), ((), ()))
+    left_high, left_low = split(left)
+    right_high, right_low = split(right)
+    total = lax.dot_general(left_high, right_high, numbers, preferred_element_type=jnp.float32)
+    total = total + lax.dot_general(left_high, right_low, numbers, preferred_element_type=jnp.float32)
+    return total + lax.dot_general(left_low, right_high, numbers, preferred_element_type=jnp.float32)
+
+
+def factor_kernel(gram_ref, prior_ref, cross_ref, out_ref, reduced_ref):
     size = gram_ref.shape[0]
     rows = lax.broadcasted_iota(jnp.int32, (size, size), 0)
     cols = lax.broadcasted_iota(jnp.int32, (size, size), 1)
@@ -171,16 +185,44 @@
         result = jnp.where(picks == i, value, result)
         solved = solved - upper[:, i : i + 1] * value
     out_ref[...] = result
-
-
-def factor_basis(gram_matrix, prior_basis):
+    inner = exact_dot(cross_ref[...], result)
+    reduced_ref[...] = exact_dot(result, inner, contract=0)
+
+
+def factor_basis(gram_matrix, prior_basis, cross):
     vmem = pl.BlockSpec(memory_space=pltpu.VMEM)
+    modes = prior_basis.shape[1]
     return pl.pallas_call(
         factor_kernel,
-        out_shape=jax.ShapeDtypeStruct(prior_basis.shape, prior_basis.dtype),
+        out_shape=(
+            jax.ShapeDtypeStruct(prior_basis.shape, prior_basis.dtype),
+            jax.ShapeDtypeStruct((modes, modes), prior_basis.dtype),
+        ),
+        in_specs=[vmem, vmem, vmem],
+        out_specs=(vmem, vmem),
+    )((gram_matrix + gram_matrix.T) * 0.5, prior_basis, cross)
+
+
+def cross_kernel(data_ref, image_ref, out_ref):
+    cols = out_ref.shape[0]
+    total = jnp.zeros(out_ref.shape, jnp.float32)
+    for z in range(data_ref.shape[1] // cols):
+        data = data_ref[:, z * cols : (z + 1) * cols]
+        high, low = split(image_ref[:, z * cols : (z + 1) * cols])
+        numbers = (((0,), (0,)), ((), ()))
+        total = total + lax.dot_general(data, high, numbers, preferred_element_type=jnp.float32)
+        total = total + lax.dot_general(data, low, numbers, preferred_element_type=jnp.float32)
+    out_ref[...] = total
+
+
+def cross_products(data, image):
+    vmem = pl.BlockSpec(memory_space=pltpu.VMEM)
+    return pl.pallas_call(
+        cross_kernel,
+        out_shape=jax.ShapeDtypeStruct((COLS, COLS), jnp.float32),
         in_specs=[vmem, vmem],
         out_specs=vmem,
-    )((gram_matrix + gram_matrix.T) * 0.5, prior_basis)
+    )(data, image)
 
 
 def tree_sum(values):
@@ -441,18 +483,14 @@
     arrived = jnp.take(received, chosen, axis=0, mode="clip")
     columns = arrived.reshape(COLS, CELLS)
     partial_gram = jnp.dot(columns, columns.T, preferred_element_type=jnp.float32)
-    data_wide = columns.astype(jnp.float32).T
     data_block = columns.T.reshape(EDGE, EDGE, EDGE * COLS)
     data_block_image = diffusion(data_block)
-    data_image = data_block_image.reshape(CELLS, COLS)
-    partial_cross = jnp.dot(data_wide.T, data_image, precision=HIGHEST)
+    plane = data_block.shape[0] * data_block.shape[1]
+    partial_cross = cross_products(data_block.reshape(plane, -1), data_block_image.reshape(plane, -1))
     totals = allreduce(jnp.concatenate([partial_gram, partial_cross], axis=1))
     gram_total, cross_total = totals[:, :COLS], totals[:, COLS:]
     gram_matrix = gram_total / total_cells
-    coeffs = factor_basis(gram_matrix, prior_basis)
-    inner = jnp.dot(cross_total / total_cells, coeffs, precision=HIGHEST)
-    reduced = jnp.dot(coeffs.T, inner, precision=HIGHEST)
-    plane = data_block.shape[0] * data_block.shape[1]
+    coeffs, reduced = factor_basis(gram_matrix, prior_basis, cross_total / total_cells)
     mode_fields, diffused = project_modes(
         data_block.reshape(plane, -1), data_block_image.reshape(plane, -1), coeffs
     )

time: 118 us -> 117 us (level)
  matrix products: 5.33 us -> 0.28 us
  Pallas kernels: 90.1 us -> 93.8 us
  other arithmetic: 6.26 us -> 9.45 us
  local copies, waits for them, and re-layouts: 14.9 us -> 11.9 us
    dot_general x3 -> x0, matrix products: 5.05 us -> none  [the longest x1 2.48 us: shards(): partial_cross = jnp.dot(data_wide.T, data_image, precision=HIGHEST)]
    pallas_call x1 -> x2, Pallas kernels: 7.93 us -> 11.7 us  [the longest x1 8.28 us: factor_basis(): pl.pallas_call(factor_kernel, out_shape=(jax.ShapeDtypeStruct(prior_basis...]
    reshape x1 -> x0, local copies, waits for them, and re-layouts: 1.91 us -> none  [shards(): data_image = data_block_image.reshape(CELLS, COLS)]
    div x1, other arithmetic: 0.01 us -> 1.53 us  [shards(): cross_total / total_cells]
    unnamed x17 -> x12, local copies, waits for them, and re-layouts: 2.38 us -> 2.13 us
where the time goes in v9:
time: 117 us; the launch traced here: 116 us
  Pallas kernels  93.8 us (80%)
  local copies, waits for them, and re-layouts  11.9 us (10%)
  other arithmetic  9.45 us (8%)
    pallas_call x1, Pallas kernels, exchange(): pl.pallas_call(functools.partial(exchange_kernel, plane, size_y), out_sha...  39.9 us
    pallas_call x1, Pallas kernels, allreduce(): pl.pallas_call(functools.partial(allreduce_kernel, groups), out_shape=jax...  23 us
    pallas_call x1, Pallas kernels, factor_basis(): pl.pallas_call(factor_kernel, out_shape=(jax.ShapeDtypeStruct(prior_basis...  8.28 us
    pallas_call x1, Pallas kernels, halo(): pl.pallas_call(functools.partial(halo_kernel, sizes), out_shape=jax.Shape...  8.22 us
    pallas_call x1, Pallas kernels, average_cells(): pl.pallas_call(average_kernel, grid_spec=grid_spec, out_shape=jax.ShapeDt...  7.35 us
    pallas_call x1, Pallas kernels, project_modes(): pl.pallas_call(modes_kernel, out_shape=(shape, shape), in_specs=[vmem, vm...  3.68 us
    pallas_call x1, Pallas kernels, cross_products(): pl.pallas_call(cross_kernel, out_shape=jax.ShapeDtypeStruct((COLS, COLS),...  3.42 us

profile of v9, /device:TPU:1, one launch (start us, length us, event | category | flops | bytes accessed | tf_op | source)
XLA Modules:
  0.0 116.4 jit_solution(3543829639169866044)
XLA Ops:
  0.7 0.7 compare_select_fusion.4
  1.3 0.2 convert_reduce_fusion
  1.5 0.7 compare_select_fusion.3
  2.4 1.4 %gather_fusion = s32[32]{0:T(128)S(1)} fusion(s32[32]{0:T(128)} %param.5, s32[1024]{0:T(1024)S(1)} %pad_clamp_fusion.1), kind=kCustom, calls=%fused_computation | custom fusion | bytes 384 | tf_op jit(solution)/shard_map/jit(_take)/gather | solution.py:474
  3.8 1.4 %copy.29.prior_ref = f32[64,32]{1,0:T(8,128)} copy(f32[64,32]{0,1:T(8,128)} %param.7) | data formatting | bytes 16384 | tf_op args[3]
  5.2 0.8 broadcast_in_dim.79.ids_ref
  5.9 1.2 %select_convert_fusion.pairing_ref = bf16[2048,256]{1,0:T(8,128)(2,1)} fusion(s32[2048]{0:T(1024)S(1)} %fusion.26), kind=kLoop, calls=%fused_computation.2 | loop fusion | flops 1572864 | bytes 1056768 | tf_op jit(solution)/shard_map/convert_element_type | solution.py:70
  7.2 7.4 %shard_map.75.payload_ref = bf16[32,4,4096]{2,1,0:T(4,128)(2,1)} custom-call(s32[32]{0:T(128)} %copy-done.2, bf16[32,4,32768]{2,1,0:T(4,128)(2,1)} %fine_ref.1, bf16[2048,256]{1,0:T(8,128)(2,1)} %select_convert_fusion.pairing_ref), custom_call_target="tpu_custom_call" | custom-call | tf_op jit(solution)/shard_map/pallas_call | solution.py:109
  14.5 39.9 %shard_map.76 = (bf16[32,4,4096]{2,1,0:T(4,128)(2,1)}, s32[32,8,128]{2,1,0:T(8,128)}) custom-call(bf16[32,4,4096]{2,1,0:T(4,128)(2,1)} %shard_map.75.payload_ref, s32[32,8,128]{2,1,0:T(8,128)} %broadcast_in_dim.79.ids_ref), custom_call_target="tpu_custom_call" | custom-call | tf_op jit(solution)/shard_map/pallas_call | solution.py:357
  54.4 1.6 %slice_reduce_fusion = s32[32]{0:T(128)S(1)} fusion(s32[32,8,128]{2,1,0:T(8,128)} %get-tuple-element.11), kind=kLoop, calls=%fused_computation.33 | loop fusion | bytes 256 | tf_op jit(solution)/shard_map/slice | solution.py:478
  56.0 0.1 select_reduce_fusion.1
  56.1 2.2 %gather_fusion.1 = bf16[16,4,4096]{2,1,0:T(4,128)(2,1)S(1)} fusion(bf16[32,4,4096]{2,1,0:T(4,128)(2,1)} %get-tuple-element.10, s32[1024]{0:T(1024)S(1)} %pad_clamp_fusion), kind=kCustom, calls=%fused_computation.1 | custom fusion | bytes 1048640 | tf_op jit(solution)/shard_map/jit(_take)/gather | solution.py:483
  58.3 0.1 reshape.134
  58.5 0.3 fusion.36
  58.8 0.5 copy.23
  59.3 0.1 slice.79
  59.4 0.1 slice.77
  59.5 0.7 reshape.135
  60.2 1.5 %reshape_reshape.4.data_ref = bf16[256,1024]{1,0:T(8,128)(2,1)} reshape(bf16[4096,64]{1,0:T(8,128)(2,1)S(1)} %bitcast.24) | data formatting | bytes 1048576 | tf_op jit(solution)/shard_map/reshape;reshape | solution.py:489
  61.9 0.1 stack_reshape.7
  62.0 0.1 stack_reshape.6
  62.3 0.7 copy-done.1
  62.9 8.2 %shard_map.77 = bf16[6,16,1024]{2,1,0:T(8,128)(2,1)} custom-call(bf16[6,16,1024]{2,1,0:T(8,128)(2,1)} %copy-done.1), custom_call_target="tpu_custom_call" | custom-call | tf_op jit(solution)/shard_map/pallas_call | solution.py:411
  71.2 1.0 convert_element_type.15
  72.6 1.6 %fusion.1 = f32[16,16,1024]{2,1,0:T(8,128)} fusion(f32[16,16,1024]{2,1,0:T(8,128)S(1)} %convert_element_type.14, f32[16,16,64]{2,1,0:T(8,128)S(1)} %select_n.168, f32[16,16,64]{2,1,0:T(8,128)S(1)} %select_n.165, f32[16,1,1024]{2,1,0:T(1,128)S(1)} %copy.27, f32[16,1,1024]{2,1,0:T(1,128)S(1)} %copy.26, f32[1,16,1024]{2,1,0:T(8,128)S(1)} %get-tuple-element.27, ...), kind=kLoop, calls=%fused_computation.6 | loop fusion | flops 3407872 | bytes 2490368 | tf_op jit(solution)/shard_map/sub | solution.py:452
  74.3 3.4 %shard_map.78 = f32[64,64]{1,0:T(8,128)} custom-call(bf16[256,1024]{1,0:T(8,128)(2,1)} %reshape_reshape.4.data_ref, f32[256,1024]{1,0:T(8,128)} %bitcast.25), custom_call_target="tpu_custom_call" | custom-call | tf_op jit(solution)/shard_map/pallas_call | solution.py:220
  77.7 1.5 %pad_maximum_fusion.6.part_ref = f32[64,128]{1,0:T(8,128)} fusion(f32[64,64]{1,0:T(8,128)} %shard_map.78, f32[64,64]{1,0:T(8,128)S(1)} %fusion.36), kind=kLoop, calls=%fused_computation.24 | loop fusion | flops 8192 | bytes 65536 | tf_op jit(solution)/shard_map/concatenate | solution.py:490
  79.1 23.0 %shard_map.79 = f32[64,128]{1,0:T(8,128)} custom-call(f32[64,128]{1,0:T(8,128)} %pad_maximum_fusion.6.part_ref), custom_call_target="tpu_custom_call" | custom-call | tf_op jit(solution)/shard_map/pallas_call | solution.py:305
  102.2 1.5 %slice_multiply_fusion = (f32[64,64]{1,0:T(8,128)}, f32[64,64]{1,0:T(8,128)S(1)}) fusion(f32[64,128]{1,0:T(8,128)} %shard_map.79), kind=kLoop, calls=%fused_computation.31 | loop fusion | flops 8192 | bytes 65536 | tf_op jit(solution)/shard_map/div | solution.py:493
  103.8 0.6 fusion.10.gram_ref
  104.4 8.3 %shard_map.80 = (f32[64,32]{1,0:T(8,128)}, f32[32,32]{1,0:T(8,128)}) custom-call(f32[64,64]{1,0:T(8,128)} %fusion.10.gram_ref, f32[64,32]{1,0:T(8,128)} %copy.29.prior_ref, f32[64,64]{1,0:T(8,128)} %get-tuple-element.28.cross_ref), custom_call_target="tpu_custom_call" | custom-call | tf_op jit(solution)/shard_map/pallas_call | solution.py:195
  112.7 3.7 %shard_map.81 = (bf16[256,512]{1,0:T(8,128)(2,1)}, bf16[256,512]{1,0:T(8,128)(2,1)}) custom-call(bf16[256,1024]{1,0:T(8,128)(2,1)} %reshape_reshape.4.data_ref, f32[256,1024]{1,0:T(8,128)} %bitcast.26, f32[64,32]{1,0:T(8,128)} %get-tuple-element.12.coeffs_ref), custom_call_target="tpu_custom_call" | custom-call | tf_op jit(solution)/shard_map/pallas_call | solution.py:140
  (27 shorter events, 1.0 us)
Async XLA Ops:
  2.3 4.9 %copy-start.2 = (s32[32]{0:T(128)}, s32[32]{0:T(128)S(1)}, u32[]{:S(2)}) copy-start(s32[32]{0:T(128)S(1)} %select_reduce_fusion.source_ref) | copy-start | bytes 388
  62.3 0.7 copy-start.1
  103.7 12.7 %copy-start = (f32[64,64]{1,0:T(8,128)}, f32[64,64]{1,0:T(8,128)S(1)}, u32[]{:S(2)}) copy-start(f32[64,64]{1,0:T(8,128)S(1)} %get-tuple-element.29) | copy-start | bytes 49156

commit v10 on v9

--- a/solution.py
+++ b/solution.py
@@ -234,7 +234,7 @@
 REDUCE_GROUPS = (("gx", "gz_1"), ("gy",), ("gz_0",))
 
 
-def allreduce_kernel(groups, part_ref, out_ref, acc, *rest):
+def allreduce_kernel(groups, scale, gram_ref, cross_ref, gram_out, cross_out, acc, *rest):
     bufs, (send_sems, recv_sems) = rest[: len(groups)], rest[len(groups) :]
     me = {axis: lax.axis_index(axis) for group in groups for axis, _ in group}
 
@@ -268,7 +268,9 @@
                 barrier, inc=1, device_id=peer(group, step), device_id_type=pl.DeviceIdType.MESH
             )
     pl.semaphore_wait(barrier, sum(counts) - len(counts))
-    acc[...] = part_ref[...]
+    cols = gram_ref.shape[1]
+    acc[:, :cols] = gram_ref[...]
+    acc[:, cols:] = cross_ref[...]
     slot = 0
     for group, count, buf in zip(groups, counts, bufs):
         copies = []
@@ -293,25 +295,31 @@
             held = jnp.maximum(lax.rem(mine - source + count, count) - 1, 0)
             values.append(jnp.where(mine == source, own, buf[held]))
         acc[...] = tree_sum(values)
-    out_ref[...] = acc[...]
-
-
-def allreduce(part):
+    total = acc[...]
+    gram_out[...] = total[:, :cols] * scale
+    cross_out[...] = total[:, cols:] * scale
+
+
+def allreduce(gram, cross, scale):
+    part = jax.ShapeDtypeStruct((gram.shape[0], gram.shape[1] + cross.shape[1]), gram.dtype)
     groups = tuple(
         tuple((axis, lax.axis_size(axis)) for axis in group) for group in REDUCE_GROUPS
     )
     counts = [functools.reduce(lambda a, b: a * b, [size for _, size in group]) for group in groups]
     copies = sum(count - 1 for count in counts)
     return pl.pallas_call(
-        functools.partial(allreduce_kernel, groups),
-        out_shape=jax.ShapeDtypeStruct(part.shape, part.dtype),
-        in_specs=[pl.BlockSpec(memory_space=pltpu.VMEM)],
-        out_specs=pl.BlockSpec(memory_space=pltpu.VMEM),
+        functools.partial(allreduce_kernel, groups, scale),
+        out_shape=(
+            jax.ShapeDtypeStruct(gram.shape, gram.dtype),
+            jax.ShapeDtypeStruct(cross.shape, cross.dtype),
+        ),
+        in_specs=[pl.BlockSpec(memory_space=pltpu.VMEM)] * 2,
+        out_specs=(pl.BlockSpec(memory_space=pltpu.VMEM),) * 2,
         scratch_shapes=[pltpu.VMEM(part.shape, part.dtype)]
         + [pltpu.VMEM((max(count - 1, 1),) + part.shape, part.dtype) for count in counts]
         + [pltpu.SemaphoreType.DMA((copies,)), pltpu.SemaphoreType.DMA((copies,))],
         compiler_params=pltpu.CompilerParams(collective_id=0, has_side_effects=True),
-    )(part)
+    )(gram, cross)
 
 
 def exchange_kernel(plane, size_y, payload_ref, ids_ref, out_ref, out_ids_ref, send_sems, recv_sems, local_sems):
@@ -487,10 +495,8 @@
     data_block_image = diffusion(data_block)
     plane = data_block.shape[0] * data_block.shape[1]
     partial_cross = cross_products(data_block.reshape(plane, -1), data_block_image.reshape(plane, -1))
-    totals = allreduce(jnp.concatenate([partial_gram, partial_cross], axis=1))
-    gram_total, cross_total = totals[:, :COLS], totals[:, COLS:]
-    gram_matrix = gram_total / total_cells
-    coeffs, reduced = factor_basis(gram_matrix, prior_basis, cross_total / total_cells)
+    gram_matrix, cross_matrix = allreduce(partial_gram, partial_cross, 1.0 / total_cells)
+    coeffs, reduced = factor_basis(gram_matrix, prior_basis, cross_matrix)
     mode_fields, diffused = project_modes(
         data_block.reshape(plane, -1), data_block_image.reshape(plane, -1), coeffs
     )

time: 117 us -> 118 us (level)
  other arithmetic: 9.45 us -> 7.23 us
  local copies, waits for them, and re-layouts: 11.9 us -> 14.1 us
    div x1 -> x0, other arithmetic: 1.53 us -> none  [shards(): cross_total / total_cells]
    concatenate x1 -> x0, other arithmetic: 1.45 us -> none  [shards(): totals = allreduce(jnp.concatenate([partial_gram, partial_cross], axis=1))]
    unnamed x12 -> x11, local copies, waits for them, and re-layouts: 2.13 us -> 3.51 us
where the time goes in v10:
time: 118 us; the launch traced here: 117 us
  Pallas kernels  94 us (80%)
  local copies, waits for them, and re-layouts  14.1 us (12%)
  other arithmetic  7.23 us (6%)
    pallas_call x1, Pallas kernels, exchange(): pl.pallas_call(functools.partial(exchange_kernel, plane, size_y), out_sha...  39.9 us
    pallas_call x1, Pallas kernels, allreduce(): pl.pallas_call(functools.partial(allreduce_kernel, groups, scale), out_sh...  23.2 us
    pallas_call x1, Pallas kernels, factor_basis(): pl.pallas_call(factor_kernel, out_shape=(jax.ShapeDtypeStruct(prior_basis...  8.28 us
    pallas_call x1, Pallas kernels, halo(): pl.pallas_call(functools.partial(halo_kernel, sizes), out_shape=jax.Shape...  8.22 us
    pallas_call x1, Pallas kernels, average_cells(): pl.pallas_call(average_kernel, grid_spec=grid_spec, out_shape=jax.ShapeDt...  7.35 us
    pallas_call x1, Pallas kernels, project_modes(): pl.pallas_call(modes_kernel, out_shape=(shape, shape), in_specs=[vmem, vm...  3.68 us
    unnamed x11, local copies, waits for them, and re-layouts  3.51 us
    pallas_call x1, Pallas kernels, cross_products(): pl.pallas_call(cross_kernel, out_shape=jax.ShapeDtypeStruct((COLS, COLS),...  3.42 us

profile of v10, /device:TPU:1, one launch (start us, length us, event | category | flops | bytes accessed | tf_op | source)
XLA Modules:
  0.0 117.0 jit_solution(3767074771744336129)
XLA Ops:
  0.7 0.7 compare_select_fusion.4
  1.3 0.2 convert_reduce_fusion
  1.5 0.7 compare_select_fusion.3
  2.4 1.4 %gather_fusion = s32[32]{0:T(128)S(1)} fusion(s32[32]{0:T(128)} %param.5, s32[1024]{0:T(1024)S(1)} %pad_clamp_fusion.1), kind=kCustom, calls=%fused_computation | custom fusion | bytes 384 | tf_op jit(solution)/shard_map/jit(_take)/gather | solution.py:482
  3.8 1.4 %copy.29.prior_ref = f32[64,32]{1,0:T(8,128)} copy(f32[64,32]{0,1:T(8,128)} %param.7) | data formatting | bytes 16384 | tf_op args[3]
  5.2 0.8 broadcast_in_dim.79.ids_ref
  5.9 1.2 %select_convert_fusion.pairing_ref = bf16[2048,256]{1,0:T(8,128)(2,1)} fusion(s32[2048]{0:T(1024)S(1)} %fusion.26), kind=kLoop, calls=%fused_computation.2 | loop fusion | flops 1572864 | bytes 1056768 | tf_op jit(solution)/shard_map/convert_element_type | solution.py:70
  7.2 7.4 %shard_map.75.payload_ref = bf16[32,4,4096]{2,1,0:T(4,128)(2,1)} custom-call(s32[32]{0:T(128)} %copy-done.1, bf16[32,4,32768]{2,1,0:T(4,128)(2,1)} %fine_ref.1, bf16[2048,256]{1,0:T(8,128)(2,1)} %select_convert_fusion.pairing_ref), custom_call_target="tpu_custom_call" | custom-call | tf_op jit(solution)/shard_map/pallas_call | solution.py:109
  14.5 39.9 %shard_map.76 = (bf16[32,4,4096]{2,1,0:T(4,128)(2,1)}, s32[32,8,128]{2,1,0:T(8,128)}) custom-call(bf16[32,4,4096]{2,1,0:T(4,128)(2,1)} %shard_map.75.payload_ref, s32[32,8,128]{2,1,0:T(8,128)} %broadcast_in_dim.79.ids_ref), custom_call_target="tpu_custom_call" | custom-call | tf_op jit(solution)/shard_map/pallas_call | solution.py:365
  54.4 1.6 %slice_reduce_fusion = s32[32]{0:T(128)S(1)} fusion(s32[32,8,128]{2,1,0:T(8,128)} %get-tuple-element.13), kind=kLoop, calls=%fused_computation.30 | loop fusion | bytes 256 | tf_op jit(solution)/shard_map/slice | solution.py:486
  56.0 0.1 select_reduce_fusion.1
  56.1 2.2 %gather_fusion.1 = bf16[16,4,4096]{2,1,0:T(4,128)(2,1)S(1)} fusion(bf16[32,4,4096]{2,1,0:T(4,128)(2,1)} %get-tuple-element.12, s32[1024]{0:T(1024)S(1)} %pad_clamp_fusion), kind=kCustom, calls=%fused_computation.1 | custom fusion | bytes 1048640 | tf_op jit(solution)/shard_map/jit(_take)/gather | solution.py:491
  58.3 0.1 reshape.134
  58.5 0.9 fusion.36.gram_ref
  59.4 0.5 copy.23
  59.9 0.1 slice.73
  60.0 0.1 slice.71
  60.1 0.7 reshape.135
  60.8 1.5 %reshape_reshape.4.data_ref = bf16[256,1024]{1,0:T(8,128)(2,1)} reshape(bf16[4096,64]{1,0:T(8,128)(2,1)S(1)} %bitcast.24) | data formatting | bytes 1048576 | tf_op jit(solution)/shard_map/reshape;reshape | solution.py:497
  62.5 0.1 stack_reshape.7
  62.6 0.1 stack_reshape.6
  62.9 0.7 copy-done
  63.6 8.2 %shard_map.77 = bf16[6,16,1024]{2,1,0:T(8,128)(2,1)} custom-call(bf16[6,16,1024]{2,1,0:T(8,128)(2,1)} %copy-done), custom_call_target="tpu_custom_call" | custom-call | tf_op jit(solution)/shard_map/pallas_call | solution.py:419
  71.8 1.0 convert_element_type.15
  73.2 1.6 %fusion.1 = f32[16,16,1024]{2,1,0:T(8,128)} fusion(f32[16,16,1024]{2,1,0:T(8,128)S(1)} %convert_element_type.14, f32[16,16,64]{2,1,0:T(8,128)S(1)} %select_n.168, f32[16,16,64]{2,1,0:T(8,128)S(1)} %select_n.165, f32[16,1,1024]{2,1,0:T(1,128)S(1)} %copy.27, f32[16,1,1024]{2,1,0:T(1,128)S(1)} %copy.26, f32[1,16,1024]{2,1,0:T(8,128)S(1)} %get-tuple-element.31, ...), kind=kLoop, calls=%fused_computation.6 | loop fusion | flops 3407872 | bytes 2490368 | tf_op jit(solution)/shard_map/sub | solution.py:460
  74.9 3.4 %shard_map.78.cross_ref = f32[64,64]{1,0:T(8,128)} custom-call(bf16[256,1024]{1,0:T(8,128)(2,1)} %reshape_reshape.4.data_ref, f32[256,1024]{1,0:T(8,128)} %bitcast.25), custom_call_target="tpu_custom_call" | custom-call | tf_op jit(solution)/shard_map/pallas_call | solution.py:220
  78.3 23.2 %shard_map.79 = (f32[64,64]{1,0:T(8,128)}, f32[64,64]{1,0:T(8,128)}) custom-call(f32[64,64]{1,0:T(8,128)} %fusion.36.gram_ref, f32[64,64]{1,0:T(8,128)} %shard_map.78.cross_ref), custom_call_target="tpu_custom_call" | custom-call | tf_op jit(solution)/shard_map/pallas_call | solution.py:310
  101.5 0.8 copy.28
  102.3 1.4 %fusion.10.gram_ref = f32[64,64]{1,0:T(8,128)} fusion(f32[64,64]{1,0:T(8,128)} %get-tuple-element.36, f32[64,64]{0,1:T(8,128)S(1)} %copy.28), kind=kLoop, calls=%fused_computation.29 | loop fusion | flops 8192 | bytes 49152 | tf_op jit(solution)/shard_map/mul | solution.py:203
  103.7 8.3 %shard_map.80 = (f32[64,32]{1,0:T(8,128)}, f32[32,32]{1,0:T(8,128)}) custom-call(f32[64,64]{1,0:T(8,128)} %fusion.10.gram_ref, f32[64,32]{1,0:T(8,128)} %copy.29.prior_ref, f32[64,64]{1,0:T(8,128)} %get-tuple-element.15.cross_ref), custom_call_target="tpu_custom_call" | custom-call | tf_op jit(solution)/shard_map/pallas_call | solution.py:195
  112.0 3.7 %shard_map.81 = (bf16[256,512]{1,0:T(8,128)(2,1)}, bf16[256,512]{1,0:T(8,128)(2,1)}) custom-call(bf16[256,1024]{1,0:T(8,128)(2,1)} %reshape_reshape.4.data_ref, f32[256,1024]{1,0:T(8,128)} %bitcast.26, f32[64,32]{1,0:T(8,128)} %get-tuple-element.16.coeffs_ref), custom_call_target="tpu_custom_call" | custom-call | tf_op jit(solution)/shard_map/pallas_call | solution.py:140
  115.7 1.4 %copy.44 = f32[64,64]{1,0:T(8,128)} copy(f32[64,64]{1,0:T(8,128)} %get-tuple-element.36) | data formatting | bytes 32768
  (24 shorter events, 0.9 us)
Async XLA Ops:
  2.3 4.9 %copy-start.1 = (s32[32]{0:T(128)}, s32[32]{0:T(128)S(1)}, u32[]{:S(2)}) copy-start(s32[32]{0:T(128)S(1)} %select_reduce_fusion.source_ref) | copy-start | bytes 388
  62.9 0.7 copy-start

commit v11 on v9

--- a/solution.py
+++ b/solution.py
@@ -477,11 +477,11 @@
     received, received_ids = exchange(payload, sent_ids)
     received_snapshot = received_ids[:, 0, 0]
     snapshots = jnp.arange(SNAPS, dtype=jnp.int32)
-    chosen = jnp.sum(
-        jnp.where(received_snapshot[None, :] == snapshots[:, None], slot_ids[None, :], 0), axis=1
-    )
-    arrived = jnp.take(received, chosen, axis=0, mode="clip")
-    columns = arrived.reshape(COLS, CELLS)
+    picks = (received_snapshot[None, :] == snapshots[:, None]).astype(received.dtype)
+    arrived = jnp.dot(
+        picks, received.reshape(slot_count, FIELDS * CELLS), preferred_element_type=jnp.float32
+    )
+    columns = arrived.astype(received.dtype).reshape(COLS, CELLS)
     partial_gram = jnp.dot(columns, columns.T, preferred_element_type=jnp.float32)
     data_block = columns.T.reshape(EDGE, EDGE, EDGE * COLS)
     data_block_image = diffusion(data_block)

time: 117 us -> 117 us (level)
    gather x1 -> x0, local copies, waits for them, and re-layouts: 2.22 us -> none  [shards(): arrived = jnp.take(received, chosen, axis=0, mode='clip')]
    unnamed x12 -> x13, local copies, waits for them, and re-layouts: 2.13 us -> 3.95 us
where the time goes in v11:
time: 117 us; the launch traced here: 116 us
  Pallas kernels  93.8 us (80%)
  local copies, waits for them, and re-layouts  11.8 us (10%)
  other arithmetic  9.33 us (8%)
    pallas_call x1, Pallas kernels, exchange(): pl.pallas_call(functools.partial(exchange_kernel, plane, size_y), out_sha...  39.9 us
    pallas_call x1, Pallas kernels, allreduce(): pl.pallas_call(functools.partial(allreduce_kernel, groups), out_shape=jax...  23 us
    pallas_call x1, Pallas kernels, factor_basis(): pl.pallas_call(factor_kernel, out_shape=(jax.ShapeDtypeStruct(prior_basis...  8.28 us
    pallas_call x1, Pallas kernels, halo(): pl.pallas_call(functools.partial(halo_kernel, sizes), out_shape=jax.Shape...  8.21 us
    pallas_call x1, Pallas kernels, average_cells(): pl.pallas_call(average_kernel, grid_spec=grid_spec, out_shape=jax.ShapeDt...  7.37 us
    unnamed x13, local copies, waits for them, and re-layouts  3.95 us
    pallas_call x1, Pallas kernels, project_modes(): pl.pallas_call(modes_kernel, out_shape=(shape, shape), in_specs=[vmem, vm...  3.68 us
    pallas_call x1, Pallas kernels, cross_products(): pl.pallas_call(cross_kernel, out_shape=jax.ShapeDtypeStruct((COLS, COLS),...  3.41 us

profile of v11, /device:TPU:1, one launch (start us, length us, event | category | flops | bytes accessed | tf_op | source)
XLA Modules:
  0.0 116.4 jit_solution(2461975357807718929)
XLA Ops:
  0.7 0.7 compare_select_fusion.4
  1.3 0.2 convert_reduce_fusion
  1.5 0.7 compare_select_fusion.3
  2.4 1.4 %gather_fusion = s32[32]{0:T(128)S(1)} fusion(s32[32]{0:T(128)} %param.5, s32[1024]{0:T(1024)S(1)} %pad_clamp_fusion), kind=kCustom, calls=%fused_computation | custom fusion | bytes 384 | tf_op jit(solution)/shard_map/jit(_take)/gather | solution.py:474
  3.8 1.4 %copy.29.prior_ref = f32[64,32]{1,0:T(8,128)} copy(f32[64,32]{0,1:T(8,128)} %param.7) | data formatting | bytes 16384 | tf_op args[3]
  5.2 0.8 broadcast_in_dim.62.ids_ref
  5.9 1.2 %select_convert_fusion.pairing_ref = bf16[2048,256]{1,0:T(8,128)(2,1)} fusion(s32[2048]{0:T(1024)S(1)} %fusion.26), kind=kLoop, calls=%fused_computation.2 | loop fusion | flops 1572864 | bytes 1056768 | tf_op jit(solution)/shard_map/convert_element_type | solution.py:70
  7.2 7.4 %shard_map.75.payload_ref = bf16[32,4,4096]{2,1,0:T(4,128)(2,1)} custom-call(s32[32]{0:T(128)} %copy-done.2, bf16[32,4,32768]{2,1,0:T(4,128)(2,1)} %fine_ref.1, bf16[2048,256]{1,0:T(8,128)(2,1)} %select_convert_fusion.pairing_ref), custom_call_target="tpu_custom_call" | custom-call | tf_op jit(solution)/shard_map/pallas_call | solution.py:109
  14.5 39.9 %shard_map.76 = (bf16[32,4,4096]{2,1,0:T(4,128)(2,1)}, s32[32,8,128]{2,1,0:T(8,128)}) custom-call(bf16[32,4,4096]{2,1,0:T(4,128)(2,1)} %shard_map.75.payload_ref, s32[32,8,128]{2,1,0:T(8,128)} %broadcast_in_dim.62.ids_ref), custom_call_target="tpu_custom_call" | custom-call | tf_op jit(solution)/shard_map/pallas_call | solution.py:357
  54.4 1.6 %slice_reduce_fusion = s32[32]{0:T(128)S(1)} fusion(s32[32,8,128]{2,1,0:T(8,128)} %get-tuple-element.10), kind=kLoop, calls=%fused_computation.33 | loop fusion | bytes 256 | tf_op jit(solution)/shard_map/slice | solution.py:478
  56.0 1.8 %copy.32 = bf16[4,8,4,4096]{3,1,2,0:T(8,128)(2,1)S(1)} copy(bf16[4,8,4,4096]{3,2,1,0:T(4,128)(2,1)} %bitcast.31) | data formatting | bytes 2097152
  57.8 0.3 convolution_convert_fusion
  58.1 0.4 reshape.138
  58.5 0.3 fusion.37
  58.8 0.5 copy.23
  59.3 0.1 slice.79
  59.4 0.1 slice.77
  59.6 0.7 reshape.139
  60.3 1.5 %reshape_reshape.4.data_ref = bf16[256,1024]{1,0:T(8,128)(2,1)} reshape(bf16[4096,64]{1,0:T(8,128)(2,1)S(1)} %bitcast.27) | data formatting | bytes 1048576 | tf_op jit(solution)/shard_map/reshape;reshape | solution.py:489
  61.9 0.1 stack_reshape.7
  62.0 0.1 stack_reshape.6
  62.3 0.7 copy-done.1
  63.0 8.2 %shard_map.77 = bf16[6,16,1024]{2,1,0:T(8,128)(2,1)} custom-call(bf16[6,16,1024]{2,1,0:T(8,128)(2,1)} %copy-done.1), custom_call_target="tpu_custom_call" | custom-call | tf_op jit(solution)/shard_map/pallas_call | solution.py:411
  71.2 1.0 convert_element_type.20
  72.7 1.6 %fusion.1 = f32[16,16,1024]{2,1,0:T(8,128)} fusion(f32[16,16,1024]{2,1,0:T(8,128)S(1)} %convert_element_type.19, f32[16,16,64]{2,1,0:T(8,128)S(1)} %select_n.163, f32[16,16,64]{2,1,0:T(8,128)S(1)} %select_n.160, f32[16,1,1024]{2,1,0:T(1,128)S(1)} %copy.27, f32[16,1,1024]{2,1,0:T(1,128)S(1)} %copy.26, f32[1,16,1024]{2,1,0:T(8,128)S(1)} %get-tuple-element.27, ...), kind=kLoop, calls=%fused_computation.6 | loop fusion | flops 3407872 | bytes 2490368 | tf_op jit(solution)/shard_map/sub | solution.py:452
  74.3 3.4 %shard_map.78 = f32[64,64]{1,0:T(8,128)} custom-call(bf16[256,1024]{1,0:T(8,128)(2,1)} %reshape_reshape.4.data_ref, f32[256,1024]{1,0:T(8,128)} %bitcast.28), custom_call_target="tpu_custom_call" | custom-call | tf_op jit(solution)/shard_map/pallas_call | solution.py:220
  77.7 1.5 %pad_maximum_fusion.6.part_ref = f32[64,128]{1,0:T(8,128)} fusion(f32[64,64]{1,0:T(8,128)} %shard_map.78, f32[64,64]{1,0:T(8,128)S(1)} %fusion.37), kind=kLoop, calls=%fused_computation.24 | loop fusion | flops 8192 | bytes 65536 | tf_op jit(solution)/shard_map/concatenate | solution.py:490
  79.2 23.0 %shard_map.79 = f32[64,128]{1,0:T(8,128)} custom-call(f32[64,128]{1,0:T(8,128)} %pad_maximum_fusion.6.part_ref), custom_call_target="tpu_custom_call" | custom-call | tf_op jit(solution)/shard_map/pallas_call | solution.py:305
  102.2 1.5 %slice_multiply_fusion = (f32[64,64]{1,0:T(8,128)}, f32[64,64]{1,0:T(8,128)S(1)}) fusion(f32[64,128]{1,0:T(8,128)} %shard_map.79), kind=kLoop, calls=%fused_computation.31 | loop fusion | flops 8192 | bytes 65536 | tf_op jit(solution)/shard_map/div | solution.py:493
  103.8 0.6 fusion.10.gram_ref
  104.4 8.3 %shard_map.80 = (f32[64,32]{1,0:T(8,128)}, f32[32,32]{1,0:T(8,128)}) custom-call(f32[64,64]{1,0:T(8,128)} %fusion.10.gram_ref, f32[64,32]{1,0:T(8,128)} %copy.29.prior_ref, f32[64,64]{1,0:T(8,128)} %get-tuple-element.28.cross_ref), custom_call_target="tpu_custom_call" | custom-call | tf_op jit(solution)/shard_map/pallas_call | solution.py:195
  112.7 3.7 %shard_map.81 = (bf16[256,512]{1,0:T(8,128)(2,1)}, bf16[256,512]{1,0:T(8,128)(2,1)}) custom-call(bf16[256,1024]{1,0:T(8,128)(2,1)} %reshape_reshape.4.data_ref, f32[256,1024]{1,0:T(8,128)} %bitcast.29, f32[64,32]{1,0:T(8,128)} %get-tuple-element.12.coeffs_ref), custom_call_target="tpu_custom_call" | custom-call | tf_op jit(solution)/shard_map/pallas_call | solution.py:140
  (26 shorter events, 1.0 us)
Async XLA Ops:
  2.3 4.9 %copy-start.2 = (s32[32]{0:T(128)}, s32[32]{0:T(128)S(1)}, u32[]{:S(2)}) copy-start(s32[32]{0:T(128)S(1)} %select_reduce_fusion.source_ref) | copy-start | bytes 388
  62.3 0.7 copy-start.1
  103.7 12.7 %copy-start = (f32[64,64]{1,0:T(8,128)}, f32[64,64]{1,0:T(8,128)S(1)}, u32[]{:S(2)}) copy-start(f32[64,64]{1,0:T(8,128)S(1)} %get-tuple-element.29) | copy-start | bytes 49156

commit v12 on v9

--- a/solution.py
+++ b/solution.py
@@ -114,22 +114,22 @@
 
 
 def modes_kernel(data_ref, image_ref, coeffs_ref, fields_ref, diffused_ref):
-    coeffs = coeffs_ref[...]
-    high = coeffs.astype(jnp.bfloat16)
-    low = (coeffs - high.astype(jnp.float32)).astype(jnp.bfloat16)
-    cols, modes = coeffs.shape
-    for z in range(data_ref.shape[1] // cols):
-        data = data_ref[:, z * cols : (z + 1) * cols]
-        fields = jnp.dot(data, high, preferred_element_type=jnp.float32)
-        fields = fields + jnp.dot(data, low, preferred_element_type=jnp.float32)
-        fields_ref[:, z * modes : (z + 1) * modes] = fields.astype(fields_ref.dtype)
-        image = image_ref[:, z * cols : (z + 1) * cols]
-        image_high = image.astype(jnp.bfloat16)
-        image_low = (image - image_high.astype(jnp.float32)).astype(jnp.bfloat16)
-        diffused = jnp.dot(image_high, high, preferred_element_type=jnp.float32)
-        diffused = diffused + jnp.dot(image_high, low, preferred_element_type=jnp.float32)
-        diffused = diffused + jnp.dot(image_low, high, preferred_element_type=jnp.float32)
-        diffused_ref[:, z * modes : (z + 1) * modes] = diffused.astype(diffused_ref.dtype)
+    high, low = split(coeffs_ref[...])
+    cols, modes = high.shape
+    rows = data_ref.shape[0]
+    depth = data_ref.shape[1] // cols
+    data = jnp.concatenate([data_ref[:, z * cols : (z + 1) * cols] for z in range(depth)], axis=0)
+    fields = jnp.dot(data, high, preferred_element_type=jnp.float32)
+    fields = fields + jnp.dot(data, low, preferred_element_type=jnp.float32)
+    image = jnp.concatenate([image_ref[:, z * cols : (z + 1) * cols] for z in range(depth)], axis=0)
+    image_high, image_low = split(image)
+    diffused = jnp.dot(image_high, high, preferred_element_type=jnp.float32)
+    diffused = diffused + jnp.dot(image_high, low, preferred_element_type=jnp.float32)
+    diffused = diffused + jnp.dot(image_low, high, preferred_element_type=jnp.float32)
+    for z in range(depth):
+        part = slice(z * rows, (z + 1) * rows)
+        fields_ref[:, z * modes : (z + 1) * modes] = fields[part].astype(fields_ref.dtype)
+        diffused_ref[:, z * modes : (z + 1) * modes] = diffused[part].astype(diffused_ref.dtype)
 
 
 def project_modes(data, image, coeffs):

time: 117 us -> 117 us (level)
  no operation moved by 1% of the time
where the time goes in v12:
time: 117 us
  Pallas kernels  94 us (80%)
  local copies, waits for them, and re-layouts  11.9 us (10%)
  other arithmetic  9.45 us (8%)
    pallas_call x1, Pallas kernels, exchange(): pl.pallas_call(functools.partial(exchange_kernel, plane, size_y), out_sha...  39.9 us
    pallas_call x1, Pallas kernels, allreduce(): pl.pallas_call(functools.partial(allreduce_kernel, groups), out_shape=jax...  23 us
    pallas_call x1, Pallas kernels, factor_basis(): pl.pallas_call(factor_kernel, out_shape=(jax.ShapeDtypeStruct(prior_basis...  8.28 us
    pallas_call x1, Pallas kernels, halo(): pl.pallas_call(functools.partial(halo_kernel, sizes), out_shape=jax.Shape...  8.22 us
    pallas_call x1, Pallas kernels, average_cells(): pl.pallas_call(average_kernel, grid_spec=grid_spec, out_shape=jax.ShapeDt...  7.35 us
    pallas_call x1, Pallas kernels, project_modes(): pl.pallas_call(modes_kernel, out_shape=(shape, shape), in_specs=[vmem, vm...  3.88 us
    pallas_call x1, Pallas kernels, cross_products(): pl.pallas_call(cross_kernel, out_shape=jax.ShapeDtypeStruct((COLS, COLS),...  3.42 us

profile of v12, /device:TPU:1, one launch (start us, length us, event | category | flops | bytes accessed | tf_op | source)
XLA Modules:
  0.0 116.5 jit_solution(9651423489990574736)
XLA Ops:
  0.7 0.7 compare_select_fusion.4
  1.3 0.2 convert_reduce_fusion
  1.5 0.7 compare_select_fusion.3
  2.4 1.4 %gather_fusion = s32[32]{0:T(128)S(1)} fusion(s32[32]{0:T(128)} %param.5, s32[1024]{0:T(1024)S(1)} %pad_clamp_fusion.1), kind=kCustom, calls=%fused_computation | custom fusion | bytes 384 | tf_op jit(solution)/shard_map/jit(_take)/gather | solution.py:474
  3.8 1.4 %copy.29.prior_ref = f32[64,32]{1,0:T(8,128)} copy(f32[64,32]{0,1:T(8,128)} %param.7) | data formatting | bytes 16384 | tf_op args[3]
  5.2 0.8 broadcast_in_dim.79.ids_ref
  5.9 1.2 %select_convert_fusion.pairing_ref = bf16[2048,256]{1,0:T(8,128)(2,1)} fusion(s32[2048]{0:T(1024)S(1)} %fusion.26), kind=kLoop, calls=%fused_computation.2 | loop fusion | flops 1572864 | bytes 1056768 | tf_op jit(solution)/shard_map/convert_element_type | solution.py:70
  7.2 7.4 %shard_map.75.payload_ref = bf16[32,4,4096]{2,1,0:T(4,128)(2,1)} custom-call(s32[32]{0:T(128)} %copy-done.2, bf16[32,4,32768]{2,1,0:T(4,128)(2,1)} %fine_ref.1, bf16[2048,256]{1,0:T(8,128)(2,1)} %select_convert_fusion.pairing_ref), custom_call_target="tpu_custom_call" | custom-call | tf_op jit(solution)/shard_map/pallas_call | solution.py:109
  14.5 39.9 %shard_map.76 = (bf16[32,4,4096]{2,1,0:T(4,128)(2,1)}, s32[32,8,128]{2,1,0:T(8,128)}) custom-call(bf16[32,4,4096]{2,1,0:T(4,128)(2,1)} %shard_map.75.payload_ref, s32[32,8,128]{2,1,0:T(8,128)} %broadcast_in_dim.79.ids_ref), custom_call_target="tpu_custom_call" | custom-call | tf_op jit(solution)/shard_map/pallas_call | solution.py:357
  54.4 1.6 %slice_reduce_fusion = s32[32]{0:T(128)S(1)} fusion(s32[32,8,128]{2,1,0:T(8,128)} %get-tuple-element.11), kind=kLoop, calls=%fused_computation.33 | loop fusion | bytes 256 | tf_op jit(solution)/shard_map/slice | solution.py:478
  56.0 0.1 select_reduce_fusion.1
  56.1 2.2 %gather_fusion.1 = bf16[16,4,4096]{2,1,0:T(4,128)(2,1)S(1)} fusion(bf16[32,4,4096]{2,1,0:T(4,128)(2,1)} %get-tuple-element.10, s32[1024]{0:T(1024)S(1)} %pad_clamp_fusion), kind=kCustom, calls=%fused_computation.1 | custom fusion | bytes 1048640 | tf_op jit(solution)/shard_map/jit(_take)/gather | solution.py:483
  58.3 0.1 reshape.134
  58.5 0.3 fusion.36
  58.8 0.5 copy.23
  59.3 0.1 slice.79
  59.4 0.1 slice.77
  59.5 0.7 reshape.135
  60.2 1.5 %reshape_reshape.4.data_ref = bf16[256,1024]{1,0:T(8,128)(2,1)} reshape(bf16[4096,64]{1,0:T(8,128)(2,1)S(1)} %bitcast.24) | data formatting | bytes 1048576 | tf_op jit(solution)/shard_map/reshape;reshape | solution.py:489
  61.9 0.1 stack_reshape.7
  62.0 0.1 stack_reshape.6
  62.3 0.7 copy-done.1
  62.9 8.2 %shard_map.77 = bf16[6,16,1024]{2,1,0:T(8,128)(2,1)} custom-call(bf16[6,16,1024]{2,1,0:T(8,128)(2,1)} %copy-done.1), custom_call_target="tpu_custom_call" | custom-call | tf_op jit(solution)/shard_map/pallas_call | solution.py:411
  71.2 1.0 convert_element_type.15
  72.6 1.6 %fusion.1 = f32[16,16,1024]{2,1,0:T(8,128)} fusion(f32[16,16,1024]{2,1,0:T(8,128)S(1)} %convert_element_type.14, f32[16,16,64]{2,1,0:T(8,128)S(1)} %select_n.168, f32[16,16,64]{2,1,0:T(8,128)S(1)} %select_n.165, f32[16,1,1024]{2,1,0:T(1,128)S(1)} %copy.27, f32[16,1,1024]{2,1,0:T(1,128)S(1)} %copy.26, f32[1,16,1024]{2,1,0:T(8,128)S(1)} %get-tuple-element.27, ...), kind=kLoop, calls=%fused_computation.6 | loop fusion | flops 3407872 | bytes 2490368 | tf_op jit(solution)/shard_map/sub | solution.py:452
  74.3 3.4 %shard_map.78 = f32[64,64]{1,0:T(8,128)} custom-call(bf16[256,1024]{1,0:T(8,128)(2,1)} %reshape_reshape.4.data_ref, f32[256,1024]{1,0:T(8,128)} %bitcast.25), custom_call_target="tpu_custom_call" | custom-call | tf_op jit(solution)/shard_map/pallas_call | solution.py:220
  77.7 1.5 %pad_maximum_fusion.6.part_ref = f32[64,128]{1,0:T(8,128)} fusion(f32[64,64]{1,0:T(8,128)} %shard_map.78, f32[64,64]{1,0:T(8,128)S(1)} %fusion.36), kind=kLoop, calls=%fused_computation.24 | loop fusion | flops 8192 | bytes 65536 | tf_op jit(solution)/shard_map/concatenate | solution.py:490
  79.1 23.0 %shard_map.79 = f32[64,128]{1,0:T(8,128)} custom-call(f32[64,128]{1,0:T(8,128)} %pad_maximum_fusion.6.part_ref), custom_call_target="tpu_custom_call" | custom-call | tf_op jit(solution)/shard_map/pallas_call | solution.py:305
  102.1 1.5 %slice_multiply_fusion = (f32[64,64]{1,0:T(8,128)}, f32[64,64]{1,0:T(8,128)S(1)}) fusion(f32[64,128]{1,0:T(8,128)} %shard_map.79), kind=kLoop, calls=%fused_computation.31 | loop fusion | flops 8192 | bytes 65536 | tf_op jit(solution)/shard_map/div | solution.py:493
  103.7 0.6 fusion.10.gram_ref
  104.4 8.3 %shard_map.80 = (f32[64,32]{1,0:T(8,128)}, f32[32,32]{1,0:T(8,128)}) custom-call(f32[64,64]{1,0:T(8,128)} %fusion.10.gram_ref, f32[64,32]{1,0:T(8,128)} %copy.29.prior_ref, f32[64,64]{1,0:T(8,128)} %get-tuple-element.28.cross_ref), custom_call_target="tpu_custom_call" | custom-call | tf_op jit(solution)/shard_map/pallas_call | solution.py:195
  112.7 3.9 %shard_map.81 = (bf16[256,512]{1,0:T(8,128)(2,1)}, bf16[256,512]{1,0:T(8,128)(2,1)}) custom-call(bf16[256,1024]{1,0:T(8,128)(2,1)} %reshape_reshape.4.data_ref, f32[256,1024]{1,0:T(8,128)} %bitcast.26, f32[64,32]{1,0:T(8,128)} %get-tuple-element.12.coeffs_ref), custom_call_target="tpu_custom_call" | custom-call | tf_op jit(solution)/shard_map/pallas_call | solution.py:140
  (27 shorter events, 1.0 us)
Async XLA Ops:
  2.3 4.9 %copy-start.2 = (s32[32]{0:T(128)}, s32[32]{0:T(128)S(1)}, u32[]{:S(2)}) copy-start(s32[32]{0:T(128)S(1)} %select_reduce_fusion.source_ref) | copy-start | bytes 388
  62.3 0.7 copy-start.1
  103.7 12.9 %copy-start = (f32[64,64]{1,0:T(8,128)}, f32[64,64]{1,0:T(8,128)S(1)}, u32[]{:S(2)}) copy-start(f32[64,64]{1,0:T(8,128)S(1)} %get-tuple-element.29) | copy-start | bytes 49156
